TPU v7x, 32 devices: a whole 2x2x4 slice. The times are simulated.
32 devices in a mesh: seq: 8 (over z, x), head: 4 (over y, core).
Axes of the slice: x: 2, y: 2, z: 4, core: 2. Of those that a mesh axis runs over, the one named last changes fastest.
Arguments:
- queries: bfloat16 [2048, 4096], P('seq', 'head'), may hold values from -6 to 6
- key_rows: bfloat16 [2048, 4096], P('seq', 'head'), may hold values from -18 to 18
- values: bfloat16 [2048, 4096], P('seq', 'head'), may hold values from -6 to 6
- write_gate: float32 [2048, 32], P('seq', 'head'), may hold values from 0.05 to 1
- ridge_diag: float32 [32, 128], P('head'), may hold values from 0.1 to 4
- norm_gain: float32 [4096], replicated, may hold values from 0.5 to 1.5
- gate_logits: bfloat16 [2048, 4096], P(('seq', 'head')), may hold values from -8 to 8
Outputs:
- layer_out: bfloat16 [2048, 4096], P(('seq', 'head'))
All inputs are finite; a program needn't handle non-finite values.
Results may differ from a plain program's by a relative error of at most 0.018.
Values may be sent and summed in bfloat16 or wider, within the bound.
No kernel may reach another device: no remote copies, remote signals or barrier semaphores. Data moves between devices by JAX's collectives and lax.ppermute only.
A program may use at most 128 MiB of HBM per device.

v0:
```python
import functools

import jax
import jax.numpy as jnp
from jax import lax
from jax.experimental import pallas as pl
from jax.experimental.pallas import tpu as pltpu
from jax.sharding import PartitionSpec as P


ITERS = 8
EPS = 1e-06

F32 = jnp.float32
BF16 = jnp.bfloat16
VMEM = pl.BlockSpec(memory_space=pltpu.VMEM)
SMEM = pl.BlockSpec(memory_space=pltpu.SMEM)


def call(body, shapes, specs, scratch=(), mib=16, flops=0):
    single = not isinstance(shapes, list)
    return pl.pallas_call(
        body,
        out_shape=shapes,
        in_specs=specs,
        out_specs=VMEM if single else [VMEM] * len(shapes),
        scratch_shapes=list(scratch),
        compiler_params=pltpu.CompilerParams(vmem_limit_bytes=mib << 20),
        cost_estimate=pl.CostEstimate(flops=flops, bytes_accessed=1 << 20, transcendentals=0),
    )


def dot(a, b, dims=((1,), (0,))):
    return lax.dot_general(a, b, (dims, ((), ())), preferred_element_type=F32)


def square_sum(block, axis):
    return jnp.sum(block * block, axis=axis, keepdims=True)


def key_state_kernel(width, k_ref, gate_ref, kk_ref):
    heads = gate_ref.shape[0]
    half = width // 2
    row = lax.broadcasted_iota(jnp.int32, (half, width), 0)
    col = lax.broadcasted_iota(jnp.int32, (half, width), 1)
    gates = gate_ref[...].T
    diags = []
    for h in range(heads):
        key = k_ref[:, h * width : (h + 1) * width]
        key_f = key.astype(F32)
        wide = key_f * (gates[:, h : h + 1] / (square_sum(key_f, 1) + EPS))
        diags.append(jnp.sum(wide * key_f, axis=0, keepdims=True))
        kk = dot(wide.astype(BF16), key, ((0,), (0,)))
        other = pltpu.roll(kk[half:], half, 1)
        packed = jnp.where(row > col, other, jnp.where(row == col, 0.0, kk[:half]))
        kk_ref[h * half : (h + 1) * half] = packed.astype(BF16)
    store_diag(kk_ref, heads * half, jnp.concatenate(diags, axis=0))


def store_diag(ref, at, diag):
    heads = diag.shape[0]
    high = diag.astype(BF16)
    ref[at : at + 2 * heads] = jnp.concatenate(
        [high, (diag - high.astype(F32)).astype(BF16)], axis=0
    )


def load_diag(ref, at):
    both = ref[at:].astype(F32)
    heads = both.shape[0] // 2
    return both[:heads] + both[heads:]


def key_join_kernel(at, mine_ref, other_ref, total_ref):
    total_ref[:at] = (mine_ref[:at].astype(F32) + other_ref[:at].astype(F32)).astype(BF16)
    store_diag(total_ref, at, load_diag(mine_ref, at) + load_diag(other_ref, at))


def value_join_kernel(mine_ref, other_ref, total_ref):
    total_ref[...] = (mine_ref[...].astype(F32) + other_ref[...].astype(F32)).astype(BF16)


def value_state_kernel(width, k_ref, v_ref, gate_ref, val_ref, vk_ref):
    gates = gate_ref[...].T
    for h in range(gate_ref.shape[0]):
        cols = slice(h * width, (h + 1) * width)
        key = k_ref[:, cols]
        scale = lax.rsqrt(square_sum(key.astype(F32), 1) + EPS)
        val = (v_ref[:, cols].astype(F32) * (gates[:, h : h + 1] * scale)).astype(BF16)
        val_ref[:, cols] = val
        vk_ref[h] = dot(val, key, ((0,), (0,))).astype(BF16)


def prepare_kernel(width, q_ref, k_ref, gate_ref, kt_ref, qt_ref, wt_ref):
    heads, toks = gate_ref.shape
    half = toks // 2
    gates = gate_ref[...].T
    keep = lax.broadcasted_iota(jnp.int32, (half, half), 0) <= lax.broadcasted_iota(
        jnp.int32, (half, half), 1
    )
    for h in range(heads):
        cols = slice(h * width, (h + 1) * width)
        key = k_ref[:, cols]
        kt_ref[h] = key.T
        weight = gates[:, h : h + 1] / (square_sum(key.astype(F32), 1) + EPS)
        wt_ref[h, 0] = jnp.where(keep, weight[:half], 0.0)
        wt_ref[h, 1] = jnp.broadcast_to(weight[:half], (half, half))
        wt_ref[h, 2] = jnp.where(keep, weight[half:], 0.0)
        query = q_ref[:, cols].T.astype(F32)
        qt_ref[h] = query * lax.rsqrt(square_sum(query, 0) + EPS)


def gate_kernel(gain_ref, logit_ref, out_ref):
    out_ref[...] = gain_ref[...] * jax.nn.sigmoid(logit_ref[...].astype(F32))


def prefix(place_ref, refs, load):
    total = 0.0
    for k, ref in enumerate(refs):
        total = total + load(ref) * ((place_ref[0] >> k) & 1).astype(F32)
    return total


def cg_kernel(width, rounds, place_ref, k_ref, kt_ref, qt_ref, wt_ref, ridge_ref, *refs):
    totals = refs[:rounds]
    x_ref, lhs, ridges, rs, ps, xs = refs[rounds:]
    heads, _, toks = qt_ref.shape
    half = toks // 2
    part = width // 2
    inner = lax.broadcasted_iota(jnp.int32, (part, part), 0) < lax.broadcasted_iota(
        jnp.int32, (part, part), 1
    )
    ridge_t = (ridge_ref[...] + prefix(place_ref, totals, lambda ref: load_diag(ref, heads * part))).T
    norms = []
    for h in range(heads):
        rows = slice(h * part, (h + 1) * part)
        upper = prefix(place_ref, totals, lambda ref: ref[rows].astype(F32))
        turned = upper.T
        tri = upper[:, :part]
        tri_t = turned[:part]
        lhs[h, :toks] = k_ref[:, h * width : (h + 1) * width]
        lhs[h, toks : toks + part] = jnp.concatenate(
            [jnp.where(inner, tri, tri_t), upper[:, part:]], axis=1
        ).astype(BF16)
        lhs[h, toks + part :] = jnp.concatenate(
            [turned[part:], jnp.where(inner, tri_t, tri)], axis=1
        ).astype(BF16)
        ridges[h] = jnp.broadcast_to(ridge_t[:, h : h + 1], (width, width))
        query = qt_ref[h]
        xs[h] = jnp.zeros_like(query)
        rs[h] = query
        ps[h] = query
        norms.append(square_sum(query, 0))

    def project(h):
        direction = ps[h]
        out = dot(lhs[h], direction.astype(BF16))
        ridge = jnp.concatenate([ridges[h]] * (toks // width), axis=1)
        return direction, out, out[toks:] + ridge * direction

    def step(_, norms):
        after = []
        for h in range(heads):
            direction, out, image = project(h)
            top = jnp.concatenate(
                [
                    (wt_ref[h, 0] * out[:half, :half]).astype(BF16),
                    (wt_ref[h, 1] * out[:half, half:]).astype(BF16),
                ],
                axis=1,
            )
            low = jnp.concatenate(
                [
                    jnp.zeros((half, half), BF16),
                    (wt_ref[h, 2] * out[half:toks, half:]).astype(BF16),
                ],
                axis=1,
            )
            image = image + dot(kt_ref[h], jnp.concatenate([top, low], axis=0))
            alpha = norms[h] / jnp.sum(direction * image, axis=0, keepdims=True)
            xs[h] = xs[h] + alpha * direction
            residual = rs[h] - alpha * image
            rs[h] = residual
            following = square_sum(residual, 0)
            ps[h] = residual + (following / norms[h]) * direction
            after.append(following)
        return tuple(after)

    norms = lax.fori_loop(0, ITERS - 1, step, tuple(norms))
    for h in range(heads):
        direction, out, image = project(h)
        curve = jnp.sum(direction * image, axis=0, keepdims=True)
        score = out[:half]
        left = jnp.sum(score[:, :half] * score[:, :half] * wt_ref[h, 0], axis=0, keepdims=True)
        right = jnp.sum(score[:, half:] * score[:, half:] * wt_ref[h, 1], axis=0, keepdims=True)
        score = out[half:toks, half:]
        right = right + jnp.sum(score * score * wt_ref[h, 2], axis=0, keepdims=True)
        alpha = norms[h] / (curve + jnp.concatenate([left, right], axis=1))
        x_ref[:, h * width : (h + 1) * width] = (xs[h] + alpha * direction).astype(BF16).T


def read_kernel(width, spots, rounds, place_ref, me_ref, x_ref, k_ref, val_ref, *refs):
    totals, outs, tmp = refs[:rounds], refs[rounds : rounds + spots], refs[rounds + spots]
    toks = k_ref.shape[0]
    rows = toks // spots
    me = me_ref[0]
    keep = lax.broadcasted_iota(jnp.int32, (toks, toks), 0) >= lax.broadcasted_iota(
        jnp.int32, (toks, toks), 1
    )
    for h in range(k_ref.shape[1] // width):
        cols = slice(h * width, (h + 1) * width)
        x = x_ref[:, cols]
        state = prefix(place_ref, totals, lambda ref: ref[h].astype(F32)).astype(BF16)
        score = jnp.where(keep, dot(x, k_ref[:, cols], ((1,), (1,))), 0.0).astype(BF16)
        out = dot(x, state, ((1,), (1,))) + dot(score, val_ref[:, cols])
        tmp[:, cols] = out.astype(BF16)
    for k in range(spots):
        outs[k][...] = tmp[pl.ds(pl.multiple_of((me ^ k) * rows, rows), rows), :]


def norm_kernel(spots, me_ref, *refs):
    pieces, gate_ref, out_ref = refs[:spots], refs[spots], refs[spots + 1]
    me = me_ref[0]
    wide = pieces[0].shape[1]
    total = 0.0
    for k in range(spots):
        total = total + square_sum(pieces[k][...].astype(F32), 1)
    factor = lax.rsqrt(total / (wide * spots) + EPS)
    for k in range(spots):
        cols = pl.ds(pl.multiple_of((me ^ k) * wide, wide), wide)
        out_ref[:, cols] = (pieces[k][...].astype(F32) * factor * gate_ref[:, cols]).astype(BF16)


def swap(x, axis, size, step):
    return lax.ppermute(x, axis, [(i, i ^ step) for i in range(size)])


def shape(*dims, dtype=BF16):
    return jax.ShapeDtypeStruct(dims, dtype)


def shards(mesh, queries, key_rows, values, write_gate, ridge_diag, norm_gain, gate_logits):
    toks, cols = queries.shape
    heads = write_gate.shape[1]
    width = cols // heads
    spots = mesh.shape["head"]
    size = mesh.shape["seq"]
    rounds = size.bit_length() - 1
    rows = toks // spots
    me = lax.axis_index("head").astype(jnp.int32).reshape(1)
    place = lax.axis_index("seq").astype(jnp.int32).reshape(1)
    gates = write_gate.T
    packed = heads * width // 2 + 2 * heads
    work = 2 * toks * width * width * heads

    kk = call(
        functools.partial(key_state_kernel, width), shape(packed, width), [VMEM] * 2, flops=work
    )(key_rows, gates)
    vals, vk = call(
        functools.partial(value_state_kernel, width),
        [shape(toks, cols), shape(heads, width, width)],
        [VMEM] * 3,
        flops=work,
    )(key_rows, values, gates)
    kt, qt, wt = call(
        functools.partial(prepare_kernel, width),
        [
            shape(heads, width, toks),
            shape(heads, width, toks, dtype=F32),
            shape(heads, 3, toks // 2, toks // 2, dtype=F32),
        ],
        [VMEM] * 3,
        mib=24,
        flops=work,
    )(queries, key_rows, gates)
    gated = call(gate_kernel, shape(*gate_logits.shape, dtype=F32), [VMEM] * 2, flops=work)(
        norm_gain[None, :], gate_logits
    )

    key_in, value_in = [], []
    for k in range(rounds):
        key_in.append(swap(kk, "seq", size, 1 << k))
        if k + 1 < rounds:
            kk = call(
                functools.partial(key_join_kernel, packed - 2 * heads),
                shape(packed, width),
                [VMEM] * 2,
                mib=4,
            )(kk, key_in[-1])
    for k in range(rounds):
        value_in.append(swap(vk, "seq", size, 1 << k))
        if k + 1 < rounds:
            vk = call(value_join_kernel, shape(heads, width, width), [VMEM] * 2, mib=4)(
                vk, value_in[-1]
            )

    x = call(
        functools.partial(cg_kernel, width, rounds),
        shape(toks, cols),
        [SMEM] + [VMEM] * (5 + rounds),
        [
            pltpu.VMEM((heads, toks + width, width), BF16),
            pltpu.VMEM((heads, width, width), F32),
        ]
        + [pltpu.VMEM((heads, width, toks), F32)] * 3,
        mib=32,
        flops=20 * work,
    )(place, key_rows, kt, qt, wt, ridge_diag, *key_in)

    pieces = call(
        functools.partial(read_kernel, width, spots, rounds),
        [shape(rows, cols)] * spots,
        [SMEM] * 2 + [VMEM] * (3 + rounds),
        [pltpu.VMEM((toks, cols), BF16)],
        flops=work,
    )(place, me, x, key_rows, vals, *value_in)
    arrived = [pieces[0]] + [swap(pieces[k], "head", spots, k) for k in range(1, spots)]
    return call(
        functools.partial(norm_kernel, spots),
        shape(rows, spots * cols),
        [SMEM] + [VMEM] * (spots + 1),
        flops=work,
    )(me, *arrived, gated)


def solution(mesh):
    return jax.shard_map(
        functools.partial(shards, mesh),
        mesh=mesh,
        in_specs=(
            P("seq", "head"),
            P("seq", "head"),
            P("seq", "head"),
            P("seq", "head"),
            P("head", None),
            P(),
            P(("seq", "head"), None),
        ),
        out_specs=P(("seq", "head"), None),
        check_vma=False,
    )
```

profile of v0, /device:TPU:0, one launch (start us, length us, event | category | flops | bytes accessed | tf_op | source)
XLA Modules:
  0.0 62.4 jit_solution(13461344000303371617)
XLA Ops:
  0.0 0.0 copy-start
  0.0 1.0 %copy-done = bf16[256,1024]{1,0:T(8,128)(2,1)S(1)} copy-done((bf16[256,1024]{1,0:T(8,128)(2,1)S(1)}, bf16[256,1024]{1,0:T(8,128)(2,1)}, u32[]{:S(2)}) %copy-start) | copy-done | bytes 524312
  1.0 0.0 copy-start.3
  1.0 1.0 %copy-done.3 = bf16[256,1024]{1,0:T(8,128)(2,1)S(1)} copy-done((bf16[256,1024]{1,0:T(8,128)(2,1)S(1)}, bf16[256,1024]{1,0:T(8,128)(2,1)}, u32[]{:S(2)}) %copy-start.3) | copy-done | bytes 524312
  2.1 0.0 copy-start.5
  2.1 0.7 %copy-done.5 = f32[256,8]{0,1:T(8,128)S(1)} copy-done((f32[256,8]{0,1:T(8,128)S(1)}, f32[256,8]{0,1:T(8,128)}, u32[]{:S(2)}) %copy-start.5) | copy-done | bytes 8216
  2.8 2.0 %shard_map.78 = (bf16[256,1024]{1,0:T(8,128)(2,1)S(1)}, bf16[8,128,128]{2,1,0:T(8,128)(2,1)S(1)}) custom-call(bf16[256,1024]{1,0:T(8,128)(2,1)S(1)} %copy-done, bf16[256,1024]{1,0:T(8,128)(2,1)S(1)} %copy-done.3, f32[8,256]{1,0:T(8,128)S(1)} %bitcast.4), custom_call_target="tpu_custom_call" | custom-call | flops 67108864 | bytes 1048576 | tf_op jit(solution)/shard_map/pallas_call | solution.py:259
  4.8 0.0 copy-start.1
  4.8 0.0 copy-start.4
  4.8 0.0 copy-start.6
  4.8 3.0 %collective-permute-start.3 = (bf16[8,128,128]{2,1,0:T(8,128)(2,1)S(1)}, bf16[8,128,128]{2,1,0:T(8,128)(2,1)S(1)}, u32[]{:S(2)}, u32[]{:S(2)}) collective-permute-start(bf16[8,128,128]{2,1,0:T(8,128)(2,1)S(1)} %get-tuple-element.18.mine_ref), channel_id=1, source_target_pairs={{0,4},{4,0},{8,12},{12,8},{16,20},{20,16},{24,28},{28,24},{1,5},{5... | collective-permute-start | bytes 786440 | tf_op jit(solution)/shard_map/ppermute | solution.py:235
  7.9 3.1 %shard_map.74.mine_ref = bf16[528,128]{1,0:T(8,128)(2,1)S(1)} custom-call(bf16[256,1024]{1,0:T(8,128)(2,1)S(1)} %copy-done, f32[8,256]{1,0:T(8,128)S(1)} %bitcast.5), custom_call_target="tpu_custom_call" | custom-call | flops 67108864 | bytes 1048576 | tf_op jit(solution)/shard_map/pallas_call | solution.py:256
  10.9 0.0 copy-start.8
  11.0 0.1 collective-permute-start
  11.0 4.0 %collective-permute-done.3.other_ref.refs_0_ = bf16[8,128,128]{2,1,0:T(8,128)(2,1)S(1)} collective-permute-done((bf16[8,128,128]{2,1,0:T(8,128)(2,1)S(1)}, bf16[8,128,128]{2,1,0:T(8,128)(2,1)S(1)}, u32[]{:S(2)}, u32[]{:S(2)}) %collective-permute-start.3) | collective-permute-done | bytes 262176 | tf_op jit(solution)/shard_map/ppermute | solution.py:235
  15.0 0.1 shard_map.79.mine_ref
  15.1 2.2 %collective-permute-start.4 = (bf16[8,128,128]{2,1,0:T(8,128)(2,1)S(1)}, bf16[8,128,128]{2,1,0:T(8,128)(2,1)S(1)}, u32[]{:S(2)}, u32[]{:S(2)}) collective-permute-start(bf16[8,128,128]{2,1,0:T(8,128)(2,1)S(1)} %shard_map.79.mine_ref), channel_id=1, source_target_pairs={{0,8},{4,12},{8,0},{12,4},{16,24},{20,28},{24,16},{28,20},{1,9},{5... | collective-permute-start | bytes 786440 | tf_op jit(solution)/shard_map/ppermute | solution.py:235
  17.2 0.0 collective-permute-done.other_ref.refs_0_
  17.3 1.7 %collective-permute-start.1 = (bf16[528,128]{1,0:T(8,128)(2,1)S(1)}, bf16[528,128]{1,0:T(8,128)(2,1)S(1)}, u32[]{:S(2)}, u32[]{:S(2)}) collective-permute-start(bf16[528,128]{1,0:T(8,128)(2,1)S(1)} %shard_map.75.mine_ref), channel_id=1, source_target_pairs={{0,8},{4,12},{8,0},{12,4},{16,24},{20,28},{24,16},{28,20},{1,9},{5... | collective-permute-start | bytes 405512 | tf_op jit(solution)/shard_map/ppermute | solution.py:235
  19.0 5.4 %collective-permute-done.4.other_ref.refs_1_ = bf16[8,128,128]{2,1,0:T(8,128)(2,1)S(1)} collective-permute-done((bf16[8,128,128]{2,1,0:T(8,128)(2,1)S(1)}, bf16[8,128,128]{2,1,0:T(8,128)(2,1)S(1)}, u32[]{:S(2)}, u32[]{:S(2)}) %collective-permute-start.4) | collective-permute-done | bytes 262176 | tf_op jit(solution)/shard_map/ppermute | solution.py:235
  24.4 0.1 shard_map.80
  24.4 3.1 %collective-permute-start.5 = (bf16[8,128,128]{2,1,0:T(8,128)(2,1)S(1)}, bf16[8,128,128]{2,1,0:T(8,128)(2,1)S(1)}, u32[]{:S(2)}, u32[]{:S(2)}) collective-permute-start(bf16[8,128,128]{2,1,0:T(8,128)(2,1)S(1)} %shard_map.80), channel_id=1, source_target_pairs={{0,16},{4,20},{8,24},{12,28},{16,0},{20,4},{24,8},{28,12},{1,17},{... | collective-permute-start | bytes 786440 | tf_op jit(solution)/shard_map/ppermute | solution.py:235
  27.6 0.0 collective-permute-done.1.other_ref.refs_1_
  27.6 2.8 %collective-permute-start.2 = (bf16[528,128]{1,0:T(8,128)(2,1)S(1)}, bf16[528,128]{1,0:T(8,128)(2,1)S(1)}, u32[]{:S(2)}, u32[]{:S(2)}) collective-permute-start(bf16[528,128]{1,0:T(8,128)(2,1)S(1)} %shard_map.76), channel_id=1, source_target_pairs={{0,16},{4,20},{8,24},{12,28},{16,0},{20,4},{24,8},{28,12},{1,17},{... | collective-permute-start | bytes 405512 | tf_op jit(solution)/shard_map/ppermute | solution.py:235
  30.4 0.0 copy-done.1
  30.4 0.0 copy-done.4
  30.5 0.0 copy-done.6
  30.5 1.7 %shard_map.73 = (bf16[8,128,256]{2,1,0:T(8,128)(2,1)S(1)}, f32[8,128,256]{2,1,0:T(8,128)S(1)}, f32[8,3,128,128]{3,2,1,0:T(8,128)S(1)}) custom-call(bf16[256,1024]{1,0:T(8,128)(2,1)S(1)} %copy-done.4, bf16[256,1024]{1,0:T(8,128)(2,1)S(1)} %copy-done.1, f32[8,256]{1,0:T(8,128)S(1)} %bitcast.6), custom_call_target="tpu_custom_call" | custom-call | flops 67108864 | bytes 1048576 | tf_op jit(solution)/shard_map/pallas_call | solution.py:265
  32.2 7.7 %collective-permute-done.2.refs_2_ = bf16[528,128]{1,0:T(8,128)(2,1)S(1)} collective-permute-done((bf16[528,128]{1,0:T(8,128)(2,1)S(1)}, bf16[528,128]{1,0:T(8,128)(2,1)S(1)}, u32[]{:S(2)}, u32[]{:S(2)}) %collective-permute-start.2) | collective-permute-done | bytes 135200 | tf_op jit(solution)/shard_map/ppermute | solution.py:235
  39.9 0.0 copy-done.8
  39.9 11.5 %shard_map.77.x_ref = bf16[256,1024]{1,0:T(8,128)(2,1)S(1)} custom-call(s32[1]{0:T(128)} %bitcast.1.place_ref, bf16[256,1024]{1,0:T(8,128)(2,1)S(1)} %copy-done.1, bf16[8,128,256]{2,1,0:T(8,128)(2,1)S(1)} %get-tuple-element.14.kt_ref, f32[8,128,256]{2,1,0:T(8,128)S(1)} %get-tuple-element.15.qt_ref, f32[8,3,128,128]{3,2,1,0:T(8,128)S(1)} %get-tuple-element.16.wt_ref, ...), custom_call_target="tpu_custom_call" | custom-call | flops 1342177280 | bytes 1048576 | tf_op jit(solution)/shard_map/pallas_call | solution.py:297
  51.4 0.0 copy-start.2
  51.4 0.0 copy-start.7
  51.4 0.0 collective-permute-done.5.refs_2_
  51.4 1.6 %shard_map.81 = (bf16[64,1024]{1,0:T(8,128)(2,1)S(1)}, bf16[64,1024]{1,0:T(8,128)(2,1)S(1)}, bf16[64,1024]{1,0:T(8,128)(2,1)S(1)}, bf16[64,1024]{1,0:T(8,128)(2,1)S(1)}) custom-call(s32[1]{0:T(128)} %bitcast.1.place_ref, s32[1]{0:T(128)} %bitcast.me_ref, bf16[256,1024]{1,0:T(8,128)(2,1)S(1)} %shard_map.77.x_ref, bf16[256,1024]{1,0:T(8,128)(2,1)S(1)} %copy-done.1, ...), custom_call_target="tpu_custom_call" | custom-call | flops 67108864 | bytes 1048576 | tf_op jit(solution)/shard_map/pallas_call | solution.py:310
  53.0 0.1 collective-permute-start.6
  53.1 1.2 %collective-permute-start.7 = (bf16[64,1024]{1,0:T(8,128)(2,1)S(1)}, bf16[64,1024]{1,0:T(8,128)(2,1)S(1)}, u32[]{:S(2)}, u32[]{:S(2)}) collective-permute-start(bf16[64,1024]{1,0:T(8,128)(2,1)S(1)} %get-tuple-element.21), channel_id=1, source_target_pairs={{0,2},{1,3},{2,0},{3,1},{4,6},{5,7},{6,4},{7,5},{8,10},{9,11},{10,... | collective-permute-start | bytes 393224 | tf_op jit(solution)/shard_map/ppermute | solution.py:235
  54.3 0.7 %collective-permute-start.8 = (bf16[64,1024]{1,0:T(8,128)(2,1)S(1)}, bf16[64,1024]{1,0:T(8,128)(2,1)S(1)}, u32[]{:S(2)}, u32[]{:S(2)}) collective-permute-start(bf16[64,1024]{1,0:T(8,128)(2,1)S(1)} %get-tuple-element.22), channel_id=1, source_target_pairs={{0,3},{1,2},{2,1},{3,0},{4,7},{5,6},{6,5},{7,4},{8,11},{9,10},{10,... | collective-permute-start | bytes 393224 | tf_op jit(solution)/shard_map/ppermute | solution.py:235
  54.9 0.0 copy-done.2
  55.0 0.0 copy-done.7
  55.0 0.1 shard_map.82.refs_4_
  55.1 0.0 collective-permute-done.6.refs_1_
  55.1 4.4 %collective-permute-done.7.refs_2_ = bf16[64,1024]{1,0:T(8,128)(2,1)S(1)} collective-permute-done((bf16[64,1024]{1,0:T(8,128)(2,1)S(1)}, bf16[64,1024]{1,0:T(8,128)(2,1)S(1)}, u32[]{:S(2)}, u32[]{:S(2)}) %collective-permute-start.7) | collective-permute-done | bytes 131104 | tf_op jit(solution)/shard_map/ppermute | solution.py:235
  59.5 1.7 %collective-permute-done.8.refs_3_ = bf16[64,1024]{1,0:T(8,128)(2,1)S(1)} collective-permute-done((bf16[64,1024]{1,0:T(8,128)(2,1)S(1)}, bf16[64,1024]{1,0:T(8,128)(2,1)S(1)}, u32[]{:S(2)}, u32[]{:S(2)}) %collective-permute-start.8) | collective-permute-done | bytes 131104 | tf_op jit(solution)/shard_map/ppermute | solution.py:235
  61.3 1.1 %shard_map.83 = bf16[64,4096]{1,0:T(8,128)(2,1)} custom-call(s32[1]{0:T(128)} %bitcast.me_ref, bf16[64,1024]{1,0:T(8,128)(2,1)S(1)} %get-tuple-element.19.refs_0_, bf16[64,1024]{1,0:T(8,128)(2,1)S(1)} %collective-permute-done.6.refs_1_, bf16[64,1024]{1,0:T(8,128)(2,1)S(1)} %collective-permute-done.7.refs_2_, ...), custom_call_target="tpu_custom_call" | custom-call | flops 67108864 | bytes 1048576 | tf_op jit(solution)/shard_map/pallas_call | solution.py:318
  (2 shorter events, 0.1 us)
Async XLA Ops:
  0.0 1.0 %copy-start = (bf16[256,1024]{1,0:T(8,128)(2,1)S(1)}, bf16[256,1024]{1,0:T(8,128)(2,1)}, u32[]{:S(2)}) copy-start(bf16[256,1024]{1,0:T(8,128)(2,1)} %k_ref.9) | copy-start | bytes 1572868
  1.0 1.0 %copy-start.3 = (bf16[256,1024]{1,0:T(8,128)(2,1)S(1)}, bf16[256,1024]{1,0:T(8,128)(2,1)}, u32[]{:S(2)}) copy-start(bf16[256,1024]{1,0:T(8,128)(2,1)} %v_ref.1) | copy-start | bytes 1572868
  2.1 0.7 %copy-start.5 = (f32[256,8]{0,1:T(8,128)S(1)}, f32[256,8]{0,1:T(8,128)}, u32[]{:S(2)}) copy-start(f32[256,8]{0,1:T(8,128)} %param.10) | copy-start | bytes 24580
  4.8 25.7 %copy-start.1 = (bf16[256,1024]{1,0:T(8,128)(2,1)S(1)}, bf16[256,1024]{1,0:T(8,128)(2,1)}, u32[]{:S(2)}) copy-start(bf16[256,1024]{1,0:T(8,128)(2,1)} %k_ref.9) | copy-start | bytes 1572868
  4.8 25.7 %copy-start.4 = (bf16[256,1024]{1,0:T(8,128)(2,1)S(1)}, bf16[256,1024]{1,0:T(8,128)(2,1)}, u32[]{:S(2)}) copy-start(bf16[256,1024]{1,0:T(8,128)(2,1)} %q_ref.1) | copy-start | bytes 1572868
  4.8 25.6 %copy-start.6 = (f32[256,8]{0,1:T(8,128)S(1)}, f32[256,8]{0,1:T(8,128)}, u32[]{:S(2)}) copy-start(f32[256,8]{0,1:T(8,128)} %param.10) | copy-start | bytes 24580
  4.8 10.2 %collective-permute-start.3 = (bf16[8,128,128]{2,1,0:T(8,128)(2,1)S(1)}, bf16[8,128,128]{2,1,0:T(8,128)(2,1)S(1)}, u32[]{:S(2)}, u32[]{:S(2)}) collective-permute-start(bf16[8,128,128]{2,1,0:T(8,128)(2,1)S(1)} %get-tuple-element.18.mine_ref), channel_id=1, source_target_pairs={{0,4},{4,0},{8,12},{12,8},{16,20},{20,16},{24,28},{28,24},{1,5},{5... | collective-permute-start | bytes 786440 | tf_op jit(solution)/shard_map/ppermute | solution.py:235
  10.9 28.9 %copy-start.8 = (f32[8,128]{1,0:T(8,128)S(1)}, f32[8,128]{1,0:T(8,128)}, u32[]{:S(2)}) copy-start(f32[8,128]{1,0:T(8,128)} %ridge_ref.1) | copy-start | bytes 12292
  11.0 6.3 %collective-permute-start = (bf16[528,128]{1,0:T(8,128)(2,1)S(1)}, bf16[528,128]{1,0:T(8,128)(2,1)S(1)}, u32[]{:S(2)}, u32[]{:S(2)}) collective-permute-start(bf16[528,128]{1,0:T(8,128)(2,1)S(1)} %shard_map.74.mine_ref), channel_id=1, source_target_pairs={{0,4},{4,0},{8,12},{12,8},{16,20},{20,16},{24,28},{28,24},{1,5},{5... | collective-permute-start | bytes 405512 | tf_op jit(solution)/shard_map/ppermute | solution.py:235
  15.1 9.3 %collective-permute-start.4 = (bf16[8,128,128]{2,1,0:T(8,128)(2,1)S(1)}, bf16[8,128,128]{2,1,0:T(8,128)(2,1)S(1)}, u32[]{:S(2)}, u32[]{:S(2)}) collective-permute-start(bf16[8,128,128]{2,1,0:T(8,128)(2,1)S(1)} %shard_map.79.mine_ref), channel_id=1, source_target_pairs={{0,8},{4,12},{8,0},{12,4},{16,24},{20,28},{24,16},{28,20},{1,9},{5... | collective-permute-start | bytes 786440 | tf_op jit(solution)/shard_map/ppermute | solution.py:235
  17.3 10.3 %collective-permute-start.1 = (bf16[528,128]{1,0:T(8,128)(2,1)S(1)}, bf16[528,128]{1,0:T(8,128)(2,1)S(1)}, u32[]{:S(2)}, u32[]{:S(2)}) collective-permute-start(bf16[528,128]{1,0:T(8,128)(2,1)S(1)} %shard_map.75.mine_ref), channel_id=1, source_target_pairs={{0,8},{4,12},{8,0},{12,4},{16,24},{20,28},{24,16},{28,20},{1,9},{5... | collective-permute-start | bytes 405512 | tf_op jit(solution)/shard_map/ppermute | solution.py:235
  24.4 27.0 %collective-permute-start.5 = (bf16[8,128,128]{2,1,0:T(8,128)(2,1)S(1)}, bf16[8,128,128]{2,1,0:T(8,128)(2,1)S(1)}, u32[]{:S(2)}, u32[]{:S(2)}) collective-permute-start(bf16[8,128,128]{2,1,0:T(8,128)(2,1)S(1)} %shard_map.80), channel_id=1, source_target_pairs={{0,16},{4,20},{8,24},{12,28},{16,0},{20,4},{24,8},{28,12},{1,17},{... | collective-permute-start | bytes 786440 | tf_op jit(solution)/shard_map/ppermute | solution.py:235
  27.6 12.3 %collective-permute-start.2 = (bf16[528,128]{1,0:T(8,128)(2,1)S(1)}, bf16[528,128]{1,0:T(8,128)(2,1)S(1)}, u32[]{:S(2)}, u32[]{:S(2)}) collective-permute-start(bf16[528,128]{1,0:T(8,128)(2,1)S(1)} %shard_map.76), channel_id=1, source_target_pairs={{0,16},{4,20},{8,24},{12,28},{16,0},{20,4},{24,8},{28,12},{1,17},{... | collective-permute-start | bytes 405512 | tf_op jit(solution)/shard_map/ppermute | solution.py:235
  51.4 3.6 %copy-start.2 = (bf16[64,4096]{1,0:T(8,128)(2,1)S(1)}, bf16[64,4096]{1,0:T(8,128)(2,1)}, u32[]{:S(2)}) copy-start(bf16[64,4096]{1,0:T(8,128)(2,1)} %logit_ref.1) | copy-start | bytes 1572868
  51.4 3.6 %copy-start.7 = (f32[4096]{0:T(1024)S(1)}, f32[4096]{0:T(1024)}, u32[]{:S(2)}) copy-start(f32[4096]{0:T(1024)} %param.12) | copy-start | bytes 49156
  53.0 2.1 %collective-permute-start.6 = (bf16[64,1024]{1,0:T(8,128)(2,1)S(1)}, bf16[64,1024]{1,0:T(8,128)(2,1)S(1)}, u32[]{:S(2)}, u32[]{:S(2)}) collective-permute-start(bf16[64,1024]{1,0:T(8,128)(2,1)S(1)} %get-tuple-element.20), channel_id=1, source_target_pairs={{0,1},{1,0},{2,3},{3,2},{4,5},{5,4},{6,7},{7,6},{8,9},{9,8},{10,11... | collective-permute-start | bytes 393224 | tf_op jit(solution)/shard_map/ppermute | solution.py:235
  53.1 6.4 %collective-permute-start.7 = (bf16[64,1024]{1,0:T(8,128)(2,1)S(1)}, bf16[64,1024]{1,0:T(8,128)(2,1)S(1)}, u32[]{:S(2)}, u32[]{:S(2)}) collective-permute-start(bf16[64,1024]{1,0:T(8,128)(2,1)S(1)} %get-tuple-element.21), channel_id=1, source_target_pairs={{0,2},{1,3},{2,0},{3,1},{4,6},{5,7},{6,4},{7,5},{8,10},{9,11},{10,... | collective-permute-start | bytes 393224 | tf_op jit(solution)/shard_map/ppermute | solution.py:235
  54.3 7.0 %collective-permute-start.8 = (bf16[64,1024]{1,0:T(8,128)(2,1)S(1)}, bf16[64,1024]{1,0:T(8,128)(2,1)S(1)}, u32[]{:S(2)}, u32[]{:S(2)}) collective-permute-start(bf16[64,1024]{1,0:T(8,128)(2,1)S(1)} %get-tuple-element.22), channel_id=1, source_target_pairs={{0,3},{1,2},{2,1},{3,0},{4,7},{5,6},{6,5},{7,4},{8,11},{9,10},{10,... | collective-permute-start | bytes 393224 | tf_op jit(solution)/shard_map/ppermute | solution.py:235
where the time goes:
time: 62.6 us; the launch traced here: 62.4 us
  waiting for transfers between devices  23.2 us (37%)
  Pallas kernels  21.4 us (34%)
  starting transfers between devices  14.9 us (24%)
  local copies, waits for them, and re-layouts  2.82 us (5%)
    ppermute x9, waiting for transfers between devices, swap(): return lax.ppermute(x, axis, [(i, i ^ step) for i in range(size)])  23.2 us
    ppermute x9, starting transfers between devices, swap(): return lax.ppermute(x, axis, [(i, i ^ step) for i in range(size)])  14.9 us
    pallas_call x1, Pallas kernels, shards(): call(functools.partial(cg_kernel, width, rounds), shape(toks, cols), [SME...  11.5 us
    pallas_call x1, Pallas kernels, shards(): call(functools.partial(key_state_kernel, width), shape(packed, width), [V...  3.09 us
    unnamed x18, local copies, waits for them, and re-layouts  2.82 us
    pallas_call x1, Pallas kernels, shards(): call(functools.partial(value_state_kernel, width), [shape(toks, cols), sh...  2 us
    pallas_call x1, Pallas kernels, shards(): call(functools.partial(prepare_kernel, width), [shape(heads, width, toks)...  1.71 us
    pallas_call x1, Pallas kernels, shards(): call(functools.partial(read_kernel, width, spots, rounds), [shape(rows, c...  1.6 us
  transfers between devices with their start and end apart: 9, of which 5 were waited for; matrix products, arithmetic and copies ran while one was open for 0% of the time, Pallas kernels for 27%

commit v1 on v0

--- a/solution.py
+++ b/solution.py
@@ -14,10 +14,9 @@
 F32 = jnp.float32
 BF16 = jnp.bfloat16
 VMEM = pl.BlockSpec(memory_space=pltpu.VMEM)
-SMEM = pl.BlockSpec(memory_space=pltpu.SMEM)
-
-
-def call(body, shapes, specs, scratch=(), mib=16, flops=0):
+
+
+def call(body, shapes, specs, scratch=(), mib=4, flops=0):
     single = not isinstance(shapes, list)
     return pl.pallas_call(
         body,
@@ -114,14 +113,15 @@
     out_ref[...] = gain_ref[...] * jax.nn.sigmoid(logit_ref[...].astype(F32))
 
 
-def prefix(place_ref, refs, load):
+def prefix(refs, load):
+    place = lax.axis_index("seq")
     total = 0.0
     for k, ref in enumerate(refs):
-        total = total + load(ref) * ((place_ref[0] >> k) & 1).astype(F32)
+        total = total + load(ref) * ((place >> k) & 1).astype(F32)
     return total
 
 
-def cg_kernel(width, rounds, place_ref, k_ref, kt_ref, qt_ref, wt_ref, ridge_ref, *refs):
+def cg_kernel(width, rounds, k_ref, kt_ref, qt_ref, wt_ref, ridge_ref, *refs):
     totals = refs[:rounds]
     x_ref, lhs, ridges, rs, ps, xs = refs[rounds:]
     heads, _, toks = qt_ref.shape
@@ -130,11 +130,11 @@
     inner = lax.broadcasted_iota(jnp.int32, (part, part), 0) < lax.broadcasted_iota(
         jnp.int32, (part, part), 1
     )
-    ridge_t = (ridge_ref[...] + prefix(place_ref, totals, lambda ref: load_diag(ref, heads * part))).T
+    ridge_t = (ridge_ref[...] + prefix(totals, lambda ref: load_diag(ref, heads * part))).T
     norms = []
     for h in range(heads):
         rows = slice(h * part, (h + 1) * part)
-        upper = prefix(place_ref, totals, lambda ref: ref[rows].astype(F32))
+        upper = prefix(totals, lambda ref: ref[rows].astype(F32))
         turned = upper.T
         tri = upper[:, :part]
         tri_t = turned[:part]
@@ -199,18 +199,18 @@
         x_ref[:, h * width : (h + 1) * width] = (xs[h] + alpha * direction).astype(BF16).T
 
 
-def read_kernel(width, spots, rounds, place_ref, me_ref, x_ref, k_ref, val_ref, *refs):
+def read_kernel(width, spots, rounds, x_ref, k_ref, val_ref, *refs):
     totals, outs, tmp = refs[:rounds], refs[rounds : rounds + spots], refs[rounds + spots]
     toks = k_ref.shape[0]
     rows = toks // spots
-    me = me_ref[0]
+    me = lax.axis_index("head")
     keep = lax.broadcasted_iota(jnp.int32, (toks, toks), 0) >= lax.broadcasted_iota(
         jnp.int32, (toks, toks), 1
     )
     for h in range(k_ref.shape[1] // width):
         cols = slice(h * width, (h + 1) * width)
         x = x_ref[:, cols]
-        state = prefix(place_ref, totals, lambda ref: ref[h].astype(F32)).astype(BF16)
+        state = prefix(totals, lambda ref: ref[h].astype(F32)).astype(BF16)
         score = jnp.where(keep, dot(x, k_ref[:, cols], ((1,), (1,))), 0.0).astype(BF16)
         out = dot(x, state, ((1,), (1,))) + dot(score, val_ref[:, cols])
         tmp[:, cols] = out.astype(BF16)
@@ -218,9 +218,9 @@
         outs[k][...] = tmp[pl.ds(pl.multiple_of((me ^ k) * rows, rows), rows), :]
 
 
-def norm_kernel(spots, me_ref, *refs):
+def norm_kernel(spots, *refs):
     pieces, gate_ref, out_ref = refs[:spots], refs[spots], refs[spots + 1]
-    me = me_ref[0]
+    me = lax.axis_index("head")
     wide = pieces[0].shape[1]
     total = 0.0
     for k in range(spots):
@@ -247,8 +247,6 @@
     size = mesh.shape["seq"]
     rounds = size.bit_length() - 1
     rows = toks // spots
-    me = lax.axis_index("head").astype(jnp.int32).reshape(1)
-    place = lax.axis_index("seq").astype(jnp.int32).reshape(1)
     gates = write_gate.T
     packed = heads * width // 2 + 2 * heads
     work = 2 * toks * width * width * heads
@@ -270,7 +268,7 @@
             shape(heads, 3, toks // 2, toks // 2, dtype=F32),
         ],
         [VMEM] * 3,
-        mib=24,
+        mib=4,
         flops=work,
     )(queries, key_rows, gates)
     gated = call(gate_kernel, shape(*gate_logits.shape, dtype=F32), [VMEM] * 2, flops=work)(
@@ -297,30 +295,30 @@
     x = call(
         functools.partial(cg_kernel, width, rounds),
         shape(toks, cols),
-        [SMEM] + [VMEM] * (5 + rounds),
+        [VMEM] * (5 + rounds),
         [
             pltpu.VMEM((heads, toks + width, width), BF16),
             pltpu.VMEM((heads, width, width), F32),
         ]
         + [pltpu.VMEM((heads, width, toks), F32)] * 3,
-        mib=32,
+        mib=8,
         flops=20 * work,
-    )(place, key_rows, kt, qt, wt, ridge_diag, *key_in)
+    )(key_rows, kt, qt, wt, ridge_diag, *key_in)
 
     pieces = call(
         functools.partial(read_kernel, width, spots, rounds),
         [shape(rows, cols)] * spots,
-        [SMEM] * 2 + [VMEM] * (3 + rounds),
+        [VMEM] * (3 + rounds),
         [pltpu.VMEM((toks, cols), BF16)],
         flops=work,
-    )(place, me, x, key_rows, vals, *value_in)
+    )(x, key_rows, vals, *value_in)
     arrived = [pieces[0]] + [swap(pieces[k], "head", spots, k) for k in range(1, spots)]
     return call(
         functools.partial(norm_kernel, spots),
         shape(rows, spots * cols),
-        [SMEM] + [VMEM] * (spots + 1),
+        [VMEM] * (spots + 1),
         flops=work,
-    )(me, *arrived, gated)
+    )(*arrived, gated)
 
 
 def solution(mesh):

time: 62.6 us -> 62.6 us (level)
    unnamed x18 -> x16, local copies, waits for them, and re-layouts: 2.82 us -> 2.81 us
where the time goes in v1:
time: 62.6 us; the launch traced here: 62.4 us
  waiting for transfers between devices  23.2 us (37%)
  Pallas kernels  21.4 us (34%)
  starting transfers between devices  14.9 us (24%)
  local copies, waits for them, and re-layouts  2.81 us (4%)
    ppermute x9, waiting for transfers between devices, swap(): return lax.ppermute(x, axis, [(i, i ^ step) for i in range(size)])  23.2 us
    ppermute x9, starting transfers between devices, swap(): return lax.ppermute(x, axis, [(i, i ^ step) for i in range(size)])  14.9 us
    pallas_call x1, Pallas kernels, shards(): call(functools.partial(cg_kernel, width, rounds), shape(toks, cols), [VME...  11.6 us
    pallas_call x1, Pallas kernels, shards(): call(functools.partial(key_state_kernel, width), shape(packed, width), [V...  3.09 us
    unnamed x16, local copies, waits for them, and re-layouts  2.81 us
    pallas_call x1, Pallas kernels, shards(): call(functools.partial(value_state_kernel, width), [shape(toks, cols), sh...  2 us
    pallas_call x1, Pallas kernels, shards(): call(functools.partial(prepare_kernel, width), [shape(heads, width, toks)...  1.72 us
    pallas_call x1, Pallas kernels, shards(): call(functools.partial(read_kernel, width, spots, rounds), [shape(rows, c...  1.6 us
  transfers between devices with their start and end apart: 9, of which 5 were waited for; matrix products, arithmetic and copies ran while one was open for 0% of the time, Pallas kernels for 27%

profile of v1, /device:TPU:0, one launch (start us, length us, event | category | flops | bytes accessed | tf_op | source)
XLA Modules:
  0.0 62.4 jit_solution(5148132532313842614)
XLA Ops:
  0.0 0.0 copy-start
  0.0 1.0 %copy-done = bf16[256,1024]{1,0:T(8,128)(2,1)S(1)} copy-done((bf16[256,1024]{1,0:T(8,128)(2,1)S(1)}, bf16[256,1024]{1,0:T(8,128)(2,1)}, u32[]{:S(2)}) %copy-start) | copy-done | bytes 524312
  1.0 0.0 copy-start.3
  1.0 1.0 %copy-done.3 = bf16[256,1024]{1,0:T(8,128)(2,1)S(1)} copy-done((bf16[256,1024]{1,0:T(8,128)(2,1)S(1)}, bf16[256,1024]{1,0:T(8,128)(2,1)}, u32[]{:S(2)}) %copy-start.3) | copy-done | bytes 524312
  2.1 0.0 copy-start.5
  2.1 0.7 %copy-done.5 = f32[256,8]{0,1:T(8,128)S(1)} copy-done((f32[256,8]{0,1:T(8,128)S(1)}, f32[256,8]{0,1:T(8,128)}, u32[]{:S(2)}) %copy-start.5) | copy-done | bytes 8216
  2.8 2.0 %shard_map.78 = (bf16[256,1024]{1,0:T(8,128)(2,1)S(1)}, bf16[8,128,128]{2,1,0:T(8,128)(2,1)S(1)}) custom-call(bf16[256,1024]{1,0:T(8,128)(2,1)S(1)} %copy-done, bf16[256,1024]{1,0:T(8,128)(2,1)S(1)} %copy-done.3, f32[8,256]{1,0:T(8,128)S(1)} %bitcast.2), custom_call_target="tpu_custom_call" | custom-call | flops 67108864 | bytes 1048576 | tf_op jit(solution)/shard_map/pallas_call | solution.py:257
  4.8 0.0 copy-start.1
  4.8 0.0 copy-start.4
  4.8 3.0 %collective-permute-start.3 = (bf16[8,128,128]{2,1,0:T(8,128)(2,1)S(1)}, bf16[8,128,128]{2,1,0:T(8,128)(2,1)S(1)}, u32[]{:S(2)}, u32[]{:S(2)}) collective-permute-start(bf16[8,128,128]{2,1,0:T(8,128)(2,1)S(1)} %get-tuple-element.18.mine_ref), channel_id=1, source_target_pairs={{0,4},{4,0},{8,12},{12,8},{16,20},{20,16},{24,28},{28,24},{1,5},{5... | collective-permute-start | bytes 786440 | tf_op jit(solution)/shard_map/ppermute | solution.py:235
  7.8 3.1 %shard_map.74.mine_ref = bf16[528,128]{1,0:T(8,128)(2,1)S(1)} custom-call(bf16[256,1024]{1,0:T(8,128)(2,1)S(1)} %copy-done, f32[8,256]{1,0:T(8,128)S(1)} %bitcast.3), custom_call_target="tpu_custom_call" | custom-call | flops 67108864 | bytes 1048576 | tf_op jit(solution)/shard_map/pallas_call | solution.py:254
  10.9 0.0 copy-start.7
  10.9 0.1 collective-permute-start
  11.0 4.0 %collective-permute-done.3.other_ref.refs_0_ = bf16[8,128,128]{2,1,0:T(8,128)(2,1)S(1)} collective-permute-done((bf16[8,128,128]{2,1,0:T(8,128)(2,1)S(1)}, bf16[8,128,128]{2,1,0:T(8,128)(2,1)S(1)}, u32[]{:S(2)}, u32[]{:S(2)}) %collective-permute-start.3) | collective-permute-done | bytes 262176 | tf_op jit(solution)/shard_map/ppermute | solution.py:235
  15.0 0.1 shard_map.79.mine_ref
  15.1 2.2 %collective-permute-start.4 = (bf16[8,128,128]{2,1,0:T(8,128)(2,1)S(1)}, bf16[8,128,128]{2,1,0:T(8,128)(2,1)S(1)}, u32[]{:S(2)}, u32[]{:S(2)}) collective-permute-start(bf16[8,128,128]{2,1,0:T(8,128)(2,1)S(1)} %shard_map.79.mine_ref), channel_id=1, source_target_pairs={{0,8},{4,12},{8,0},{12,4},{16,24},{20,28},{24,16},{28,20},{1,9},{5... | collective-permute-start | bytes 786440 | tf_op jit(solution)/shard_map/ppermute | solution.py:235
  17.2 0.0 collective-permute-done.other_ref.refs_0_
  17.3 1.7 %collective-permute-start.1 = (bf16[528,128]{1,0:T(8,128)(2,1)S(1)}, bf16[528,128]{1,0:T(8,128)(2,1)S(1)}, u32[]{:S(2)}, u32[]{:S(2)}) collective-permute-start(bf16[528,128]{1,0:T(8,128)(2,1)S(1)} %shard_map.75.mine_ref), channel_id=1, source_target_pairs={{0,8},{4,12},{8,0},{12,4},{16,24},{20,28},{24,16},{28,20},{1,9},{5... | collective-permute-start | bytes 405512 | tf_op jit(solution)/shard_map/ppermute | solution.py:235
  19.0 5.4 %collective-permute-done.4.other_ref.refs_1_ = bf16[8,128,128]{2,1,0:T(8,128)(2,1)S(1)} collective-permute-done((bf16[8,128,128]{2,1,0:T(8,128)(2,1)S(1)}, bf16[8,128,128]{2,1,0:T(8,128)(2,1)S(1)}, u32[]{:S(2)}, u32[]{:S(2)}) %collective-permute-start.4) | collective-permute-done | bytes 262176 | tf_op jit(solution)/shard_map/ppermute | solution.py:235
  24.4 0.1 shard_map.80
  24.4 3.1 %collective-permute-start.5 = (bf16[8,128,128]{2,1,0:T(8,128)(2,1)S(1)}, bf16[8,128,128]{2,1,0:T(8,128)(2,1)S(1)}, u32[]{:S(2)}, u32[]{:S(2)}) collective-permute-start(bf16[8,128,128]{2,1,0:T(8,128)(2,1)S(1)} %shard_map.80), channel_id=1, source_target_pairs={{0,16},{4,20},{8,24},{12,28},{16,0},{20,4},{24,8},{28,12},{1,17},{... | collective-permute-start | bytes 786440 | tf_op jit(solution)/shard_map/ppermute | solution.py:235
  27.6 0.0 collective-permute-done.1.other_ref.refs_1_
  27.6 2.8 %collective-permute-start.2 = (bf16[528,128]{1,0:T(8,128)(2,1)S(1)}, bf16[528,128]{1,0:T(8,128)(2,1)S(1)}, u32[]{:S(2)}, u32[]{:S(2)}) collective-permute-start(bf16[528,128]{1,0:T(8,128)(2,1)S(1)} %shard_map.76), channel_id=1, source_target_pairs={{0,16},{4,20},{8,24},{12,28},{16,0},{20,4},{24,8},{28,12},{1,17},{... | collective-permute-start | bytes 405512 | tf_op jit(solution)/shard_map/ppermute | solution.py:235
  30.4 0.0 copy-done.1
  30.4 0.0 copy-done.4
  30.4 1.7 %shard_map.73 = (bf16[8,128,256]{2,1,0:T(8,128)(2,1)S(1)}, f32[8,128,256]{2,1,0:T(8,128)S(1)}, f32[8,3,128,128]{3,2,1,0:T(8,128)S(1)}) custom-call(bf16[256,1024]{1,0:T(8,128)(2,1)S(1)} %copy-done.4, bf16[256,1024]{1,0:T(8,128)(2,1)S(1)} %copy-done.1, f32[8,256]{1,0:T(8,128)S(1)} %bitcast.4), custom_call_target="tpu_custom_call" | custom-call | flops 67108864 | bytes 1048576 | tf_op jit(solution)/shard_map/pallas_call | solution.py:263
  32.2 7.7 %collective-permute-done.2.refs_2_ = bf16[528,128]{1,0:T(8,128)(2,1)S(1)} collective-permute-done((bf16[528,128]{1,0:T(8,128)(2,1)S(1)}, bf16[528,128]{1,0:T(8,128)(2,1)S(1)}, u32[]{:S(2)}, u32[]{:S(2)}) %collective-permute-start.2) | collective-permute-done | bytes 135200 | tf_op jit(solution)/shard_map/ppermute | solution.py:235
  39.9 0.0 copy-done.7
  39.9 11.6 %shard_map.77.x_ref = bf16[256,1024]{1,0:T(8,128)(2,1)S(1)} custom-call(bf16[256,1024]{1,0:T(8,128)(2,1)S(1)} %copy-done.1, bf16[8,128,256]{2,1,0:T(8,128)(2,1)S(1)} %get-tuple-element.14.kt_ref, f32[8,128,256]{2,1,0:T(8,128)S(1)} %get-tuple-element.15.qt_ref, f32[8,3,128,128]{3,2,1,0:T(8,128)S(1)} %get-tuple-element.16.wt_ref, f32[8,128]{1,0:T(8,128)S(1)} %copy-done.7, ...), custom_call_target="tpu_custom_call" | custom-call | flops 1342177280 | bytes 1048576 | tf_op jit(solution)/shard_map/pallas_call | solution.py:295
  51.4 0.0 copy-start.2
  51.4 0.0 copy-start.6
  51.5 0.0 collective-permute-done.5.refs_2_
  51.5 1.6 %shard_map.81 = (bf16[64,1024]{1,0:T(8,128)(2,1)S(1)}, bf16[64,1024]{1,0:T(8,128)(2,1)S(1)}, bf16[64,1024]{1,0:T(8,128)(2,1)S(1)}, bf16[64,1024]{1,0:T(8,128)(2,1)S(1)}) custom-call(bf16[256,1024]{1,0:T(8,128)(2,1)S(1)} %shard_map.77.x_ref, bf16[256,1024]{1,0:T(8,128)(2,1)S(1)} %copy-done.1, bf16[256,1024]{1,0:T(8,128)(2,1)S(1)} %get-tuple-element.17.val_ref, ...), custom_call_target="tpu_custom_call" | custom-call | flops 67108864 | bytes 1048576 | tf_op jit(solution)/shard_map/pallas_call | solution.py:308
  53.1 0.1 collective-permute-start.6
  53.2 1.2 %collective-permute-start.7 = (bf16[64,1024]{1,0:T(8,128)(2,1)S(1)}, bf16[64,1024]{1,0:T(8,128)(2,1)S(1)}, u32[]{:S(2)}, u32[]{:S(2)}) collective-permute-start(bf16[64,1024]{1,0:T(8,128)(2,1)S(1)} %get-tuple-element.21), channel_id=1, source_target_pairs={{0,2},{1,3},{2,0},{3,1},{4,6},{5,7},{6,4},{7,5},{8,10},{9,11},{10,... | collective-permute-start | bytes 393224 | tf_op jit(solution)/shard_map/ppermute | solution.py:235
  54.3 0.7 %collective-permute-start.8 = (bf16[64,1024]{1,0:T(8,128)(2,1)S(1)}, bf16[64,1024]{1,0:T(8,128)(2,1)S(1)}, u32[]{:S(2)}, u32[]{:S(2)}) collective-permute-start(bf16[64,1024]{1,0:T(8,128)(2,1)S(1)} %get-tuple-element.22), channel_id=1, source_target_pairs={{0,3},{1,2},{2,1},{3,0},{4,7},{5,6},{6,5},{7,4},{8,11},{9,10},{10,... | collective-permute-start | bytes 393224 | tf_op jit(solution)/shard_map/ppermute | solution.py:235
  55.0 0.0 copy-done.2
  55.0 0.0 copy-done.6
  55.0 0.1 shard_map.82.refs_4_
  55.2 0.0 collective-permute-done.6.refs_1_
  55.2 4.4 %collective-permute-done.7.refs_2_ = bf16[64,1024]{1,0:T(8,128)(2,1)S(1)} collective-permute-done((bf16[64,1024]{1,0:T(8,128)(2,1)S(1)}, bf16[64,1024]{1,0:T(8,128)(2,1)S(1)}, u32[]{:S(2)}, u32[]{:S(2)}) %collective-permute-start.7) | collective-permute-done | bytes 131104 | tf_op jit(solution)/shard_map/ppermute | solution.py:235
  59.6 1.7 %collective-permute-done.8.refs_3_ = bf16[64,1024]{1,0:T(8,128)(2,1)S(1)} collective-permute-done((bf16[64,1024]{1,0:T(8,128)(2,1)S(1)}, bf16[64,1024]{1,0:T(8,128)(2,1)S(1)}, u32[]{:S(2)}, u32[]{:S(2)}) %collective-permute-start.8) | collective-permute-done | bytes 131104 | tf_op jit(solution)/shard_map/ppermute | solution.py:235
  61.3 1.1 %shard_map.83 = bf16[64,4096]{1,0:T(8,128)(2,1)} custom-call(bf16[64,1024]{1,0:T(8,128)(2,1)S(1)} %get-tuple-element.19.refs_0_, bf16[64,1024]{1,0:T(8,128)(2,1)S(1)} %collective-permute-done.6.refs_1_, bf16[64,1024]{1,0:T(8,128)(2,1)S(1)} %collective-permute-done.7.refs_2_, bf16[64,1024]{1,0:T(8,128)(2,1)S(1)} %collective-permute-done.8.refs_3_, ...), custom_call_target="tpu_custom_call" | custom-call | flops 67108864 | bytes 1048576 | tf_op jit(solution)/shard_map/pallas_call | solution.py:316
  (2 shorter events, 0.1 us)
Async XLA Ops:
  0.0 1.0 %copy-start = (bf16[256,1024]{1,0:T(8,128)(2,1)S(1)}, bf16[256,1024]{1,0:T(8,128)(2,1)}, u32[]{:S(2)}) copy-start(bf16[256,1024]{1,0:T(8,128)(2,1)} %k_ref.9) | copy-start | bytes 1572868
  1.0 1.0 %copy-start.3 = (bf16[256,1024]{1,0:T(8,128)(2,1)S(1)}, bf16[256,1024]{1,0:T(8,128)(2,1)}, u32[]{:S(2)}) copy-start(bf16[256,1024]{1,0:T(8,128)(2,1)} %v_ref.1) | copy-start | bytes 1572868
  2.1 0.7 %copy-start.5 = (f32[256,8]{0,1:T(8,128)S(1)}, f32[256,8]{0,1:T(8,128)}, u32[]{:S(2)}) copy-start(f32[256,8]{0,1:T(8,128)} %param.10) | copy-start | bytes 24580
  4.8 25.6 %copy-start.1 = (bf16[256,1024]{1,0:T(8,128)(2,1)S(1)}, bf16[256,1024]{1,0:T(8,128)(2,1)}, u32[]{:S(2)}) copy-start(bf16[256,1024]{1,0:T(8,128)(2,1)} %k_ref.9) | copy-start | bytes 1572868
  4.8 25.6 %copy-start.4 = (bf16[256,1024]{1,0:T(8,128)(2,1)S(1)}, bf16[256,1024]{1,0:T(8,128)(2,1)}, u32[]{:S(2)}) copy-start(bf16[256,1024]{1,0:T(8,128)(2,1)} %q_ref.1) | copy-start | bytes 1572868
  4.8 10.2 %collective-permute-start.3 = (bf16[8,128,128]{2,1,0:T(8,128)(2,1)S(1)}, bf16[8,128,128]{2,1,0:T(8,128)(2,1)S(1)}, u32[]{:S(2)}, u32[]{:S(2)}) collective-permute-start(bf16[8,128,128]{2,1,0:T(8,128)(2,1)S(1)} %get-tuple-element.18.mine_ref), channel_id=1, source_target_pairs={{0,4},{4,0},{8,12},{12,8},{16,20},{20,16},{24,28},{28,24},{1,5},{5... | collective-permute-start | bytes 786440 | tf_op jit(solution)/shard_map/ppermute | solution.py:235
  10.9 28.9 %copy-start.7 = (f32[8,128]{1,0:T(8,128)S(1)}, f32[8,128]{1,0:T(8,128)}, u32[]{:S(2)}) copy-start(f32[8,128]{1,0:T(8,128)} %ridge_ref.1) | copy-start | bytes 12292
  10.9 6.3 %collective-permute-start = (bf16[528,128]{1,0:T(8,128)(2,1)S(1)}, bf16[528,128]{1,0:T(8,128)(2,1)S(1)}, u32[]{:S(2)}, u32[]{:S(2)}) collective-permute-start(bf16[528,128]{1,0:T(8,128)(2,1)S(1)} %shard_map.74.mine_ref), channel_id=1, source_target_pairs={{0,4},{4,0},{8,12},{12,8},{16,20},{20,16},{24,28},{28,24},{1,5},{5... | collective-permute-start | bytes 405512 | tf_op jit(solution)/shard_map/ppermute | solution.py:235
  15.1 9.3 %collective-permute-start.4 = (bf16[8,128,128]{2,1,0:T(8,128)(2,1)S(1)}, bf16[8,128,128]{2,1,0:T(8,128)(2,1)S(1)}, u32[]{:S(2)}, u32[]{:S(2)}) collective-permute-start(bf16[8,128,128]{2,1,0:T(8,128)(2,1)S(1)} %shard_map.79.mine_ref), channel_id=1, source_target_pairs={{0,8},{4,12},{8,0},{12,4},{16,24},{20,28},{24,16},{28,20},{1,9},{5... | collective-permute-start | bytes 786440 | tf_op jit(solution)/shard_map/ppermute | solution.py:235
  17.3 10.3 %collective-permute-start.1 = (bf16[528,128]{1,0:T(8,128)(2,1)S(1)}, bf16[528,128]{1,0:T(8,128)(2,1)S(1)}, u32[]{:S(2)}, u32[]{:S(2)}) collective-permute-start(bf16[528,128]{1,0:T(8,128)(2,1)S(1)} %shard_map.75.mine_ref), channel_id=1, source_target_pairs={{0,8},{4,12},{8,0},{12,4},{16,24},{20,28},{24,16},{28,20},{1,9},{5... | collective-permute-start | bytes 405512 | tf_op jit(solution)/shard_map/ppermute | solution.py:235
  24.4 27.0 %collective-permute-start.5 = (bf16[8,128,128]{2,1,0:T(8,128)(2,1)S(1)}, bf16[8,128,128]{2,1,0:T(8,128)(2,1)S(1)}, u32[]{:S(2)}, u32[]{:S(2)}) collective-permute-start(bf16[8,128,128]{2,1,0:T(8,128)(2,1)S(1)} %shard_map.80), channel_id=1, source_target_pairs={{0,16},{4,20},{8,24},{12,28},{16,0},{20,4},{24,8},{28,12},{1,17},{... | collective-permute-start | bytes 786440 | tf_op jit(solution)/shard_map/ppermute | solution.py:235
  27.6 12.3 %collective-permute-start.2 = (bf16[528,128]{1,0:T(8,128)(2,1)S(1)}, bf16[528,128]{1,0:T(8,128)(2,1)S(1)}, u32[]{:S(2)}, u32[]{:S(2)}) collective-permute-start(bf16[528,128]{1,0:T(8,128)(2,1)S(1)} %shard_map.76), channel_id=1, source_target_pairs={{0,16},{4,20},{8,24},{12,28},{16,0},{20,4},{24,8},{28,12},{1,17},{... | collective-permute-start | bytes 405512 | tf_op jit(solution)/shard_map/ppermute | solution.py:235
  51.4 3.6 %copy-start.2 = (bf16[64,4096]{1,0:T(8,128)(2,1)S(1)}, bf16[64,4096]{1,0:T(8,128)(2,1)}, u32[]{:S(2)}) copy-start(bf16[64,4096]{1,0:T(8,128)(2,1)} %logit_ref.1) | copy-start | bytes 1572868
  51.4 3.6 %copy-start.6 = (f32[4096]{0:T(1024)S(1)}, f32[4096]{0:T(1024)}, u32[]{:S(2)}) copy-start(f32[4096]{0:T(1024)} %param.12) | copy-start | bytes 49156
  53.1 2.1 %collective-permute-start.6 = (bf16[64,1024]{1,0:T(8,128)(2,1)S(1)}, bf16[64,1024]{1,0:T(8,128)(2,1)S(1)}, u32[]{:S(2)}, u32[]{:S(2)}) collective-permute-start(bf16[64,1024]{1,0:T(8,128)(2,1)S(1)} %get-tuple-element.20), channel_id=1, source_target_pairs={{0,1},{1,0},{2,3},{3,2},{4,5},{5,4},{6,7},{7,6},{8,9},{9,8},{10,11... | collective-permute-start | bytes 393224 | tf_op jit(solution)/shard_map/ppermute | solution.py:235
  53.2 6.4 %collective-permute-start.7 = (bf16[64,1024]{1,0:T(8,128)(2,1)S(1)}, bf16[64,1024]{1,0:T(8,128)(2,1)S(1)}, u32[]{:S(2)}, u32[]{:S(2)}) collective-permute-start(bf16[64,1024]{1,0:T(8,128)(2,1)S(1)} %get-tuple-element.21), channel_id=1, source_target_pairs={{0,2},{1,3},{2,0},{3,1},{4,6},{5,7},{6,4},{7,5},{8,10},{9,11},{10,... | collective-permute-start | bytes 393224 | tf_op jit(solution)/shard_map/ppermute | solution.py:235
  54.3 7.0 %collective-permute-start.8 = (bf16[64,1024]{1,0:T(8,128)(2,1)S(1)}, bf16[64,1024]{1,0:T(8,128)(2,1)S(1)}, u32[]{:S(2)}, u32[]{:S(2)}) collective-permute-start(bf16[64,1024]{1,0:T(8,128)(2,1)S(1)} %get-tuple-element.22), channel_id=1, source_target_pairs={{0,3},{1,2},{2,1},{3,0},{4,7},{5,6},{6,5},{7,4},{8,11},{9,10},{10,... | collective-permute-start | bytes 393224 | tf_op jit(solution)/shard_map/ppermute | solution.py:235

commit v2 on v1

--- a/solution.py
+++ b/solution.py
@@ -9,6 +9,7 @@
 
 
 ITERS = 8
+FIRST = 4
 EPS = 1e-06
 
 F32 = jnp.float32
@@ -37,19 +38,29 @@
     return jnp.sum(block * block, axis=axis, keepdims=True)
 
 
-def key_state_kernel(width, k_ref, gate_ref, kk_ref):
+def key_state_kernel(width, k_hbm, gate_hbm, kk_ref, kt_ref, k_ref, gate_ref, sems):
     heads = gate_ref.shape[0]
     half = width // 2
+    loads = [pltpu.make_async_copy(gate_hbm, gate_ref, sems.at[heads])]
+    for h in range(heads):
+        cols = slice(h * width, (h + 1) * width)
+        loads.append(pltpu.make_async_copy(k_hbm.at[:, cols], k_ref.at[:, cols], sems.at[h]))
+    for load in loads:
+        load.start()
     row = lax.broadcasted_iota(jnp.int32, (half, width), 0)
     col = lax.broadcasted_iota(jnp.int32, (half, width), 1)
-    gates = gate_ref[...].T
+    loads[0].wait()
     diags = []
     for h in range(heads):
+        loads[1 + h].wait()
         key = k_ref[:, h * width : (h + 1) * width]
-        key_f = key.astype(F32)
-        wide = key_f * (gates[:, h : h + 1] / (square_sum(key_f, 1) + EPS))
-        diags.append(jnp.sum(wide * key_f, axis=0, keepdims=True))
-        kk = dot(wide.astype(BF16), key, ((0,), (0,)))
+        turned = key.T
+        kt_ref[h] = turned
+        turned = turned.astype(F32)
+        wide = turned * (gate_ref[h : h + 1] / (square_sum(turned, 0) + EPS))
+        kk = dot(wide.astype(BF16), key)
+        diag = jnp.where(row == col, kk[:half], jnp.where(row + half == col, kk[half:], 0.0))
+        diags.append(jnp.sum(diag, axis=0, keepdims=True))
         other = pltpu.roll(kk[half:], half, 1)
         packed = jnp.where(row > col, other, jnp.where(row == col, 0.0, kk[:half]))
         kk_ref[h * half : (h + 1) * half] = packed.astype(BF16)
@@ -75,8 +86,18 @@
     store_diag(total_ref, at, load_diag(mine_ref, at) + load_diag(other_ref, at))
 
 
+def value_fold_kernel(mine_ref, other_ref, total_ref):
+    count = total_ref.shape[0]
+    part = pl.ds((lax.axis_index("seq") & 1) * count, count)
+    total_ref[...] = (mine_ref[part].astype(F32) + other_ref[part].astype(F32)).astype(BF16)
+
+
 def value_join_kernel(mine_ref, other_ref, total_ref):
     total_ref[...] = (mine_ref[...].astype(F32) + other_ref[...].astype(F32)).astype(BF16)
+
+
+def value_prefix_kernel(*refs):
+    refs[-1][...] = prefix(refs[:-1], lambda ref: ref[...].astype(F32), 1).astype(BF16)
 
 
 def value_state_kernel(width, k_ref, v_ref, gate_ref, val_ref, vk_ref):
@@ -90,7 +111,7 @@
         vk_ref[h] = dot(val, key, ((0,), (0,))).astype(BF16)
 
 
-def prepare_kernel(width, q_ref, k_ref, gate_ref, kt_ref, qt_ref, wt_ref):
+def prepare_kernel(width, q_ref, k_ref, gate_ref, qt_ref, wt_ref):
     heads, toks = gate_ref.shape
     half = toks // 2
     gates = gate_ref[...].T
@@ -100,7 +121,6 @@
     for h in range(heads):
         cols = slice(h * width, (h + 1) * width)
         key = k_ref[:, cols]
-        kt_ref[h] = key.T
         weight = gates[:, h : h + 1] / (square_sum(key.astype(F32), 1) + EPS)
         wt_ref[h, 0] = jnp.where(keep, weight[:half], 0.0)
         wt_ref[h, 1] = jnp.broadcast_to(weight[:half], (half, half))
@@ -113,19 +133,57 @@
     out_ref[...] = gain_ref[...] * jax.nn.sigmoid(logit_ref[...].astype(F32))
 
 
-def prefix(refs, load):
+def prefix(refs, load, first=0):
     place = lax.axis_index("seq")
     total = 0.0
     for k, ref in enumerate(refs):
-        total = total + load(ref) * ((place >> k) & 1).astype(F32)
+        total = total + load(ref) * ((place >> (first + k)) & 1).astype(F32)
     return total
 
 
-def cg_kernel(width, rounds, k_ref, kt_ref, qt_ref, wt_ref, ridge_ref, *refs):
+def project(lhs, ridges, ps, h):
+    toks = ps.shape[2]
+    direction = ps[h]
+    out = dot(lhs[h], direction.astype(BF16))
+    ridge = jnp.concatenate([ridges[h]] * (toks // ridges.shape[2]), axis=1)
+    return direction, out, out[toks:] + ridge * direction
+
+
+def sweep(kt_ref, wt_ref, lhs, ridges, old, new, norms):
+    half = old[0].shape[2] // 2
+    after = []
+    for h in range(kt_ref.shape[0]):
+        direction, out, image = project(lhs, ridges, old[1], h)
+        top = jnp.concatenate(
+            [
+                (wt_ref[h, 0] * out[:half, :half]).astype(BF16),
+                (wt_ref[h, 1] * out[:half, half:]).astype(BF16),
+            ],
+            axis=1,
+        )
+        low = jnp.concatenate(
+            [
+                jnp.zeros((half, half), BF16),
+                (wt_ref[h, 2] * out[half : 2 * half, half:]).astype(BF16),
+            ],
+            axis=1,
+        )
+        image = image + dot(kt_ref[h], jnp.concatenate([top, low], axis=0))
+        alpha = norms[h] / jnp.sum(direction * image, axis=0, keepdims=True)
+        residual = old[0][h] - alpha * image
+        new[0][h] = residual
+        following = square_sum(residual, 0)
+        new[1][h] = residual + (following / norms[h]) * direction
+        step = alpha * direction
+        new[2][h] = step if old[2] is None else old[2][h] + step
+        after.append(following)
+    return tuple(after)
+
+
+def cg_first_kernel(width, rounds, sweeps, k_ref, kt_ref, qt_ref, wt_ref, ridge_ref, *refs):
     totals = refs[:rounds]
-    x_ref, lhs, ridges, rs, ps, xs = refs[rounds:]
+    lhs, ridges, norm_ref, *state = refs[rounds:]
     heads, _, toks = qt_ref.shape
-    half = toks // 2
     part = width // 2
     inner = lax.broadcasted_iota(jnp.int32, (part, part), 0) < lax.broadcasted_iota(
         jnp.int32, (part, part), 1
@@ -146,61 +204,38 @@
             [turned[part:], jnp.where(inner, tri_t, tri)], axis=1
         ).astype(BF16)
         ridges[h] = jnp.broadcast_to(ridge_t[:, h : h + 1], (width, width))
-        query = qt_ref[h]
-        xs[h] = jnp.zeros_like(query)
-        rs[h] = query
-        ps[h] = query
-        norms.append(square_sum(query, 0))
-
-    def project(h):
-        direction = ps[h]
-        out = dot(lhs[h], direction.astype(BF16))
-        ridge = jnp.concatenate([ridges[h]] * (toks // width), axis=1)
-        return direction, out, out[toks:] + ridge * direction
-
-    def step(_, norms):
-        after = []
-        for h in range(heads):
-            direction, out, image = project(h)
-            top = jnp.concatenate(
-                [
-                    (wt_ref[h, 0] * out[:half, :half]).astype(BF16),
-                    (wt_ref[h, 1] * out[:half, half:]).astype(BF16),
-                ],
-                axis=1,
-            )
-            low = jnp.concatenate(
-                [
-                    jnp.zeros((half, half), BF16),
-                    (wt_ref[h, 2] * out[half:toks, half:]).astype(BF16),
-                ],
-                axis=1,
-            )
-            image = image + dot(kt_ref[h], jnp.concatenate([top, low], axis=0))
-            alpha = norms[h] / jnp.sum(direction * image, axis=0, keepdims=True)
-            xs[h] = xs[h] + alpha * direction
-            residual = rs[h] - alpha * image
-            rs[h] = residual
-            following = square_sum(residual, 0)
-            ps[h] = residual + (following / norms[h]) * direction
-            after.append(following)
-        return tuple(after)
-
-    norms = lax.fori_loop(0, ITERS - 1, step, tuple(norms))
-    for h in range(heads):
-        direction, out, image = project(h)
+        norms.append(square_sum(qt_ref[h], 0))
+    fixed = (kt_ref, wt_ref, lhs, ridges)
+    norms = sweep(*fixed, (qt_ref, qt_ref, None), state, norms)
+    norms = lax.fori_loop(1, sweeps, lambda _, now: sweep(*fixed, state, state, now), norms)
+    norm_ref[...] = jnp.concatenate(norms, axis=0)
+
+
+def cg_last_kernel(width, sweeps, kt_ref, wt_ref, lhs, ridges, norm_ref, *refs):
+    given, x_ref, state = refs[:3], refs[3], refs[4:]
+    heads = kt_ref.shape[0]
+    half = wt_ref.shape[2]
+    fixed = (kt_ref, wt_ref, lhs, ridges)
+    norms = tuple(norm_ref[h : h + 1] for h in range(heads))
+    norms = sweep(*fixed, given, state, norms)
+    norms = lax.fori_loop(1, sweeps, lambda _, now: sweep(*fixed, state, state, now), norms)
+    for h in range(heads):
+        direction, out, image = project(lhs, ridges, state[1], h)
         curve = jnp.sum(direction * image, axis=0, keepdims=True)
         score = out[:half]
         left = jnp.sum(score[:, :half] * score[:, :half] * wt_ref[h, 0], axis=0, keepdims=True)
         right = jnp.sum(score[:, half:] * score[:, half:] * wt_ref[h, 1], axis=0, keepdims=True)
-        score = out[half:toks, half:]
+        score = out[half : 2 * half, half:]
         right = right + jnp.sum(score * score * wt_ref[h, 2], axis=0, keepdims=True)
         alpha = norms[h] / (curve + jnp.concatenate([left, right], axis=1))
-        x_ref[:, h * width : (h + 1) * width] = (xs[h] + alpha * direction).astype(BF16).T
-
-
-def read_kernel(width, spots, rounds, x_ref, k_ref, val_ref, *refs):
-    totals, outs, tmp = refs[:rounds], refs[rounds : rounds + spots], refs[rounds + spots]
+        x = state[2][h] + alpha * direction
+        x_ref[:, h * width : (h + 1) * width] = x.astype(BF16).T
+
+
+def read_kernel(width, spots, x_ref, k_ref, val_ref, near_ref, own_ref, far_ref, *refs):
+    outs, tmp = refs[:spots], refs[spots]
+    count = own_ref.shape[0]
+    later = lax.axis_index("seq") & 1
     toks = k_ref.shape[0]
     rows = toks // spots
     me = lax.axis_index("head")
@@ -210,7 +245,9 @@
     for h in range(k_ref.shape[1] // width):
         cols = slice(h * width, (h + 1) * width)
         x = x_ref[:, cols]
-        state = prefix(totals, lambda ref: ref[h].astype(F32)).astype(BF16)
+        state = jnp.where(later == h // count, own_ref[h % count], far_ref[h % count])
+        near = near_ref[h].astype(F32) * later.astype(F32)
+        state = (state.astype(F32) + near).astype(BF16)
         score = jnp.where(keep, dot(x, k_ref[:, cols], ((1,), (1,))), 0.0).astype(BF16)
         out = dot(x, state, ((1,), (1,))) + dot(score, val_ref[:, cols])
         tmp[:, cols] = out.astype(BF16)
@@ -251,8 +288,16 @@
     packed = heads * width // 2 + 2 * heads
     work = 2 * toks * width * width * heads
 
-    kk = call(
-        functools.partial(key_state_kernel, width), shape(packed, width), [VMEM] * 2, flops=work
+    kk, kt = call(
+        functools.partial(key_state_kernel, width),
+        [shape(packed, width), shape(heads, width, toks)],
+        [pl.BlockSpec(memory_space=pltpu.MemorySpace.HBM)] * 2,
+        [
+            pltpu.VMEM((toks, cols), BF16),
+            pltpu.VMEM((heads, toks), F32),
+            pltpu.SemaphoreType.DMA((heads + 1,)),
+        ],
+        flops=work,
     )(key_rows, gates)
     vals, vk = call(
         functools.partial(value_state_kernel, width),
@@ -260,10 +305,9 @@
         [VMEM] * 3,
         flops=work,
     )(key_rows, values, gates)
-    kt, qt, wt = call(
+    qt, wt = call(
         functools.partial(prepare_kernel, width),
         [
-            shape(heads, width, toks),
             shape(heads, width, toks, dtype=F32),
             shape(heads, 3, toks // 2, toks // 2, dtype=F32),
         ],
@@ -285,33 +329,43 @@
                 [VMEM] * 2,
                 mib=4,
             )(kk, key_in[-1])
-    for k in range(rounds):
+    near = swap(vk, "seq", size, 1)
+    vk = call(value_fold_kernel, shape(heads // 2, width, width), [VMEM] * 2)(vk, near)
+    for k in range(1, rounds):
         value_in.append(swap(vk, "seq", size, 1 << k))
         if k + 1 < rounds:
-            vk = call(value_join_kernel, shape(heads, width, width), [VMEM] * 2, mib=4)(
-                vk, value_in[-1]
-            )
-
+            vk = call(value_join_kernel, shape(*vk.shape), [VMEM] * 2)(vk, value_in[-1])
+    own = call(value_prefix_kernel, shape(*vk.shape), [VMEM] * (rounds - 1))(*value_in)
+    far = swap(own, "seq", size, 1)
+
+    lhs, ridges, norms, *state = call(
+        functools.partial(cg_first_kernel, width, rounds, FIRST),
+        [
+            shape(heads, toks + width, width),
+            shape(heads, width, width, dtype=F32),
+            shape(heads, toks, dtype=F32),
+        ]
+        + [shape(heads, width, toks, dtype=F32)] * 3,
+        [VMEM] * (5 + rounds),
+        mib=4,
+        flops=10 * work,
+    )(key_rows, kt, qt, wt, ridge_diag, *key_in)
     x = call(
-        functools.partial(cg_kernel, width, rounds),
+        functools.partial(cg_last_kernel, width, ITERS - 1 - FIRST),
         shape(toks, cols),
-        [VMEM] * (5 + rounds),
-        [
-            pltpu.VMEM((heads, toks + width, width), BF16),
-            pltpu.VMEM((heads, width, width), F32),
-        ]
-        + [pltpu.VMEM((heads, width, toks), F32)] * 3,
+        [VMEM] * 8,
+        [pltpu.VMEM((heads, width, toks), F32)] * 3,
         mib=8,
-        flops=20 * work,
-    )(key_rows, kt, qt, wt, ridge_diag, *key_in)
+        flops=10 * work,
+    )(kt, wt, lhs, ridges, norms, *state)
 
     pieces = call(
-        functools.partial(read_kernel, width, spots, rounds),
+        functools.partial(read_kernel, width, spots),
         [shape(rows, cols)] * spots,
-        [VMEM] * (3 + rounds),
+        [VMEM] * 6,
         [pltpu.VMEM((toks, cols), BF16)],
         flops=work,
-    )(x, key_rows, vals, *value_in)
+    )(x, key_rows, vals, near, own, far)
     arrived = [pieces[0]] + [swap(pieces[k], "head", spots, k) for k in range(1, spots)]
     return call(
         functools.partial(norm_kernel, spots),

time: 62.6 us -> 62.2 us (level)
  waiting for transfers between devices: 23.2 us -> 26.5 us
  starting transfers between devices: 14.9 us -> 11.8 us
    ppermute x9 -> x10, waiting for transfers between devices: 23.2 us -> 26.5 us  [swap(): return lax.ppermute(x, axis, [(i, i ^ step) for i in range(size)])]
    ppermute x9 -> x10, starting transfers between devices: 14.9 us -> 11.8 us  [swap(): return lax.ppermute(x, axis, [(i, i ^ step) for i in range(size)])]
    pallas_call x6 -> x8, Pallas kernels: 18.1 us -> 17.5 us  [the longest x1 6.19 us: shards(): call(functools.partial(cg_first_kernel, width, rounds, FIRST), [shape(hea...]
  transfers between devices with their start and end apart: 9 -> 10, of which waited for: 5 -> 5; matrix products, arithmetic and copies ran while one was open for 0% -> 0% of each run, Pallas kernels for 27% -> 26%
where the time goes in v2:
time: 62.2 us; the launch traced here: 62 us
  waiting for transfers between devices  26.5 us (43%)
  Pallas kernels  20.8 us (33%)
  starting transfers between devices  11.8 us (19%)
  local copies, waits for them, and re-layouts  2.81 us (5%)
    ppermute x10, waiting for transfers between devices, swap(): return lax.ppermute(x, axis, [(i, i ^ step) for i in range(size)])  26.5 us
    ppermute x10, starting transfers between devices, swap(): return lax.ppermute(x, axis, [(i, i ^ step) for i in range(size)])  11.8 us
    pallas_call x1, Pallas kernels, shards(): call(functools.partial(cg_first_kernel, width, rounds, FIRST), [shape(hea...  6.19 us
    pallas_call x1, Pallas kernels, shards(): call(functools.partial(cg_last_kernel, width, ITERS - 1 - FIRST), shape(t...  5.39 us
    unnamed x16, local copies, waits for them, and re-layouts  2.81 us
    pallas_call x1, Pallas kernels, shards(): call(functools.partial(key_state_kernel, width), [shape(packed, width), s...  2.76 us
    pallas_call x1, Pallas kernels, shards(): call(functools.partial(value_state_kernel, width), [shape(toks, cols), sh...  2 us
    pallas_call x1, Pallas kernels, shards(): call(functools.partial(read_kernel, width, spots), [shape(rows, cols)] *...  1.6 us
  transfers between devices with their start and end apart: 10, of which 5 were waited for; matrix products, arithmetic and copies ran while one was open for 0% of the time, Pallas kernels for 26%

profile of v2, /device:TPU:0, one launch (start us, length us, event | category | flops | bytes accessed | tf_op | source)
XLA Modules:
  0.0 62.0 jit_solution(13450880587955150268)
XLA Ops:
  0.0 0.0 copy-start
  0.0 1.0 %copy-done = bf16[256,1024]{1,0:T(8,128)(2,1)S(1)} copy-done((bf16[256,1024]{1,0:T(8,128)(2,1)S(1)}, bf16[256,1024]{1,0:T(8,128)(2,1)}, u32[]{:S(2)}) %copy-start) | copy-done | bytes 524312
  1.0 0.0 copy-start.3
  1.0 1.0 %copy-done.3 = bf16[256,1024]{1,0:T(8,128)(2,1)S(1)} copy-done((bf16[256,1024]{1,0:T(8,128)(2,1)S(1)}, bf16[256,1024]{1,0:T(8,128)(2,1)}, u32[]{:S(2)}) %copy-start.3) | copy-done | bytes 524312
  2.1 0.0 copy-start.5
  2.1 0.7 %copy-done.5 = f32[256,8]{0,1:T(8,128)S(1)} copy-done((f32[256,8]{0,1:T(8,128)S(1)}, f32[256,8]{0,1:T(8,128)}, u32[]{:S(2)}) %copy-start.5) | copy-done | bytes 8216
  2.8 2.0 %shard_map.79 = (bf16[256,1024]{1,0:T(8,128)(2,1)S(1)}, bf16[8,128,128]{2,1,0:T(8,128)(2,1)S(1)}) custom-call(bf16[256,1024]{1,0:T(8,128)(2,1)S(1)} %copy-done, bf16[256,1024]{1,0:T(8,128)(2,1)S(1)} %copy-done.3, f32[8,256]{1,0:T(8,128)S(1)} %bitcast.2), custom_call_target="tpu_custom_call" | custom-call | flops 67108864 | bytes 1048576 | tf_op jit(solution)/shard_map/pallas_call | solution.py:302
  4.8 0.0 copy-start.1
  4.8 0.0 copy-start.4
  4.8 3.0 %collective-permute-start.3 = (bf16[8,128,128]{2,1,0:T(8,128)(2,1)S(1)}, bf16[8,128,128]{2,1,0:T(8,128)(2,1)S(1)}, u32[]{:S(2)}, u32[]{:S(2)}) collective-permute-start(bf16[8,128,128]{2,1,0:T(8,128)(2,1)S(1)} %get-tuple-element.32.mine_ref), channel_id=1, source_target_pairs={{0,4},{4,0},{8,12},{12,8},{16,20},{20,16},{24,28},{28,24},{1,5},{5... | collective-permute-start | bytes 786440 | tf_op jit(solution)/shard_map/ppermute | solution.py:272
  7.8 2.8 %shard_map.73 = (bf16[528,128]{1,0:T(8,128)(2,1)S(1)}, bf16[8,128,256]{2,1,0:T(8,128)(2,1)S(1)}) custom-call(bf16[256,1024]{1,0:T(8,128)(2,1)S(1)} %copy-done, f32[8,256]{1,0:T(8,128)S(1)} %bitcast.3), custom_call_target="tpu_custom_call" | custom-call | flops 67108864 | bytes 1048576 | tf_op jit(solution)/shard_map/pallas_call | solution.py:291
  10.6 0.0 copy-start.7
  10.6 0.1 collective-permute-start
  10.7 6.3 %collective-permute-done.other_ref.refs_0_ = bf16[528,128]{1,0:T(8,128)(2,1)S(1)} collective-permute-done((bf16[528,128]{1,0:T(8,128)(2,1)S(1)}, bf16[528,128]{1,0:T(8,128)(2,1)S(1)}, u32[]{:S(2)}, u32[]{:S(2)}) %collective-permute-start) | collective-permute-done | bytes 135200 | tf_op jit(solution)/shard_map/ppermute | solution.py:272
  17.1 1.9 %collective-permute-start.1 = (bf16[528,128]{1,0:T(8,128)(2,1)S(1)}, bf16[528,128]{1,0:T(8,128)(2,1)S(1)}, u32[]{:S(2)}, u32[]{:S(2)}) collective-permute-start(bf16[528,128]{1,0:T(8,128)(2,1)S(1)} %shard_map.75.mine_ref), channel_id=1, source_target_pairs={{0,8},{4,12},{8,0},{12,4},{16,24},{20,28},{24,16},{28,20},{1,9},{5... | collective-permute-start | bytes 405512 | tf_op jit(solution)/shard_map/ppermute | solution.py:272
  19.0 0.0 collective-permute-done.3.other_ref.near_ref
  19.0 0.3 collective-permute-start.4
  19.3 5.4 %collective-permute-done.4.other_ref.refs_0_ = bf16[4,128,128]{2,1,0:T(8,128)(2,1)S(1)} collective-permute-done((bf16[4,128,128]{2,1,0:T(8,128)(2,1)S(1)}, bf16[4,128,128]{2,1,0:T(8,128)(2,1)S(1)}, u32[]{:S(2)}, u32[]{:S(2)}) %collective-permute-start.4) | collective-permute-done | bytes 131104 | tf_op jit(solution)/shard_map/ppermute | solution.py:272
  24.7 2.6 %collective-permute-start.5 = (bf16[4,128,128]{2,1,0:T(8,128)(2,1)S(1)}, bf16[4,128,128]{2,1,0:T(8,128)(2,1)S(1)}, u32[]{:S(2)}, u32[]{:S(2)}) collective-permute-start(bf16[4,128,128]{2,1,0:T(8,128)(2,1)S(1)} %shard_map.81), channel_id=1, source_target_pairs={{0,16},{4,20},{8,24},{12,28},{16,0},{20,4},{24,8},{28,12},{1,17},{... | collective-permute-start | bytes 393224 | tf_op jit(solution)/shard_map/ppermute | solution.py:272
  27.4 0.0 collective-permute-done.1.other_ref.refs_1_
  27.4 0.4 collective-permute-start.2
  27.8 8.5 %collective-permute-done.5.refs_1_ = bf16[4,128,128]{2,1,0:T(8,128)(2,1)S(1)} collective-permute-done((bf16[4,128,128]{2,1,0:T(8,128)(2,1)S(1)}, bf16[4,128,128]{2,1,0:T(8,128)(2,1)S(1)}, u32[]{:S(2)}, u32[]{:S(2)}) %collective-permute-start.5) | collective-permute-done | bytes 131104 | tf_op jit(solution)/shard_map/ppermute | solution.py:272
  36.4 0.1 shard_map.82.own_ref
  36.4 1.5 %collective-permute-start.6 = (bf16[4,128,128]{2,1,0:T(8,128)(2,1)S(1)}, bf16[4,128,128]{2,1,0:T(8,128)(2,1)S(1)}, u32[]{:S(2)}, u32[]{:S(2)}) collective-permute-start(bf16[4,128,128]{2,1,0:T(8,128)(2,1)S(1)} %shard_map.82.own_ref), channel_id=1, source_target_pairs={{0,4},{4,0},{8,12},{12,8},{16,20},{20,16},{24,28},{28,24},{1,5},{5... | collective-permute-start | bytes 393224 | tf_op jit(solution)/shard_map/ppermute | solution.py:272
  38.0 0.0 copy-done.1
  38.0 0.0 copy-done.4
  38.0 1.4 %shard_map.74 = (f32[8,128,256]{2,1,0:T(8,128)S(1)}, f32[8,3,128,128]{3,2,1,0:T(8,128)S(1)}) custom-call(bf16[256,1024]{1,0:T(8,128)(2,1)S(1)} %copy-done.4, bf16[256,1024]{1,0:T(8,128)(2,1)S(1)} %copy-done.1, f32[8,256]{1,0:T(8,128)S(1)} %bitcast.4), custom_call_target="tpu_custom_call" | custom-call | flops 67108864 | bytes 1048576 | tf_op jit(solution)/shard_map/pallas_call | solution.py:308
  39.4 0.0 collective-permute-done.2.refs_2_
  39.4 0.0 copy-done.7
  39.4 6.2 %shard_map.77 = (bf16[8,384,128]{2,1,0:T(8,128)(2,1)S(1)}, f32[8,128,128]{2,1,0:T(8,128)S(1)}, f32[8,256]{1,0:T(8,128)S(1)}, f32[8,128,256]{2,1,0:T(8,128)S(1)},...) custom-call(bf16[256,1024]{1,0:T(8,128)(2,1)S(1)} %copy-done.1, ...), custom_call_target="tpu_custom_call" | custom-call | flops 671088640 | bytes 1048576 | tf_op jit(solution)/shard_map/pallas_call | solution.py:341
  45.6 5.4 %shard_map.78.x_ref = bf16[256,1024]{1,0:T(8,128)(2,1)S(1)} custom-call(bf16[8,128,256]{2,1,0:T(8,128)(2,1)S(1)} %get-tuple-element.21.kt_ref, f32[8,3,128,128]{3,2,1,0:T(8,128)S(1)} %get-tuple-element.22.wt_ref, bf16[8,384,128]{2,1,0:T(8,128)(2,1)S(1)} %get-tuple-element.25.lhs, f32[8,128,128]{2,1,0:T(8,128)S(1)} %get-tuple-element.26.ridges, ...), custom_call_target="tpu_custom_call" | custom-call | flops 671088640 | bytes 1048576 | tf_op jit(solution)/shard_map/pallas_call | solution.py:353
  51.0 0.0 copy-start.2
  51.1 0.0 copy-start.6
  51.1 0.0 collective-permute-done.6.far_ref
  51.1 1.6 %shard_map.83 = (bf16[64,1024]{1,0:T(8,128)(2,1)S(1)}, bf16[64,1024]{1,0:T(8,128)(2,1)S(1)}, bf16[64,1024]{1,0:T(8,128)(2,1)S(1)}, bf16[64,1024]{1,0:T(8,128)(2,1)S(1)}) custom-call(bf16[256,1024]{1,0:T(8,128)(2,1)S(1)} %shard_map.78.x_ref, bf16[256,1024]{1,0:T(8,128)(2,1)S(1)} %copy-done.1, bf16[256,1024]{1,0:T(8,128)(2,1)S(1)} %get-tuple-element.31.val_ref, ...), custom_call_target="tpu_custom_call" | custom-call | flops 67108864 | bytes 1048576 | tf_op jit(solution)/shard_map/pallas_call | solution.py:362
  52.7 0.1 collective-permute-start.7
  52.8 1.6 %collective-permute-start.8 = (bf16[64,1024]{1,0:T(8,128)(2,1)S(1)}, bf16[64,1024]{1,0:T(8,128)(2,1)S(1)}, u32[]{:S(2)}, u32[]{:S(2)}) collective-permute-start(bf16[64,1024]{1,0:T(8,128)(2,1)S(1)} %get-tuple-element.35), channel_id=1, source_target_pairs={{0,2},{1,3},{2,0},{3,1},{4,6},{5,7},{6,4},{7,5},{8,10},{9,11},{10,... | collective-permute-start | bytes 393224 | tf_op jit(solution)/shard_map/ppermute | solution.py:272
  54.4 0.3 collective-permute-start.9
  54.6 0.0 copy-done.2
  54.6 0.0 copy-done.6
  54.6 0.1 shard_map.84.refs_4_
  54.8 0.0 collective-permute-done.7.refs_1_
  54.8 4.4 %collective-permute-done.8.refs_2_ = bf16[64,1024]{1,0:T(8,128)(2,1)S(1)} collective-permute-done((bf16[64,1024]{1,0:T(8,128)(2,1)S(1)}, bf16[64,1024]{1,0:T(8,128)(2,1)S(1)}, u32[]{:S(2)}, u32[]{:S(2)}) %collective-permute-start.8) | collective-permute-done | bytes 131104 | tf_op jit(solution)/shard_map/ppermute | solution.py:272
  59.2 1.7 %collective-permute-done.9.refs_3_ = bf16[64,1024]{1,0:T(8,128)(2,1)S(1)} collective-permute-done((bf16[64,1024]{1,0:T(8,128)(2,1)S(1)}, bf16[64,1024]{1,0:T(8,128)(2,1)S(1)}, u32[]{:S(2)}, u32[]{:S(2)}) %collective-permute-start.9) | collective-permute-done | bytes 131104 | tf_op jit(solution)/shard_map/ppermute | solution.py:272
  60.9 1.1 %shard_map.85 = bf16[64,4096]{1,0:T(8,128)(2,1)} custom-call(bf16[64,1024]{1,0:T(8,128)(2,1)S(1)} %get-tuple-element.33.refs_0_, bf16[64,1024]{1,0:T(8,128)(2,1)S(1)} %collective-permute-done.7.refs_1_, bf16[64,1024]{1,0:T(8,128)(2,1)S(1)} %collective-permute-done.8.refs_2_, bf16[64,1024]{1,0:T(8,128)(2,1)S(1)} %collective-permute-done.9.refs_3_, ...), custom_call_target="tpu_custom_call" | custom-call | flops 67108864 | bytes 1048576 | tf_op jit(solution)/shard_map/pallas_call | solution.py:370
  (4 shorter events, 0.1 us)
Async XLA Ops:
  0.0 1.0 %copy-start = (bf16[256,1024]{1,0:T(8,128)(2,1)S(1)}, bf16[256,1024]{1,0:T(8,128)(2,1)}, u32[]{:S(2)}) copy-start(bf16[256,1024]{1,0:T(8,128)(2,1)} %k_ref.7) | copy-start | bytes 1572868
  1.0 1.0 %copy-start.3 = (bf16[256,1024]{1,0:T(8,128)(2,1)S(1)}, bf16[256,1024]{1,0:T(8,128)(2,1)}, u32[]{:S(2)}) copy-start(bf16[256,1024]{1,0:T(8,128)(2,1)} %v_ref.1) | copy-start | bytes 1572868
  2.1 0.7 %copy-start.5 = (f32[256,8]{0,1:T(8,128)S(1)}, f32[256,8]{0,1:T(8,128)}, u32[]{:S(2)}) copy-start(f32[256,8]{0,1:T(8,128)} %param.10) | copy-start | bytes 24580
  4.8 33.2 %copy-start.1 = (bf16[256,1024]{1,0:T(8,128)(2,1)S(1)}, bf16[256,1024]{1,0:T(8,128)(2,1)}, u32[]{:S(2)}) copy-start(bf16[256,1024]{1,0:T(8,128)(2,1)} %k_ref.7) | copy-start | bytes 1572868
  4.8 33.2 %copy-start.4 = (bf16[256,1024]{1,0:T(8,128)(2,1)S(1)}, bf16[256,1024]{1,0:T(8,128)(2,1)}, u32[]{:S(2)}) copy-start(bf16[256,1024]{1,0:T(8,128)(2,1)} %q_ref.1) | copy-start | bytes 1572868
  4.8 14.2 %collective-permute-start.3 = (bf16[8,128,128]{2,1,0:T(8,128)(2,1)S(1)}, bf16[8,128,128]{2,1,0:T(8,128)(2,1)S(1)}, u32[]{:S(2)}, u32[]{:S(2)}) collective-permute-start(bf16[8,128,128]{2,1,0:T(8,128)(2,1)S(1)} %get-tuple-element.32.mine_ref), channel_id=1, source_target_pairs={{0,4},{4,0},{8,12},{12,8},{16,20},{20,16},{24,28},{28,24},{1,5},{5... | collective-permute-start | bytes 786440 | tf_op jit(solution)/shard_map/ppermute | solution.py:272
  10.6 28.8 %copy-start.7 = (f32[8,128]{1,0:T(8,128)S(1)}, f32[8,128]{1,0:T(8,128)}, u32[]{:S(2)}) copy-start(f32[8,128]{1,0:T(8,128)} %ridge_ref.1) | copy-start | bytes 12292
  10.6 6.4 %collective-permute-start = (bf16[528,128]{1,0:T(8,128)(2,1)S(1)}, bf16[528,128]{1,0:T(8,128)(2,1)S(1)}, u32[]{:S(2)}, u32[]{:S(2)}) collective-permute-start(bf16[528,128]{1,0:T(8,128)(2,1)S(1)} %get-tuple-element.24.mine_ref), channel_id=1, source_target_pairs={{0,4},{4,0},{8,12},{12,8},{16,20},{20,16},{24,28},{28,24},{1,5},{5... | collective-permute-start | bytes 405512 | tf_op jit(solution)/shard_map/ppermute | solution.py:272
  17.1 10.3 %collective-permute-start.1 = (bf16[528,128]{1,0:T(8,128)(2,1)S(1)}, bf16[528,128]{1,0:T(8,128)(2,1)S(1)}, u32[]{:S(2)}, u32[]{:S(2)}) collective-permute-start(bf16[528,128]{1,0:T(8,128)(2,1)S(1)} %shard_map.75.mine_ref), channel_id=1, source_target_pairs={{0,8},{4,12},{8,0},{12,4},{16,24},{20,28},{24,16},{28,20},{1,9},{5... | collective-permute-start | bytes 405512 | tf_op jit(solution)/shard_map/ppermute | solution.py:272
  19.0 5.7 %collective-permute-start.4 = (bf16[4,128,128]{2,1,0:T(8,128)(2,1)S(1)}, bf16[4,128,128]{2,1,0:T(8,128)(2,1)S(1)}, u32[]{:S(2)}, u32[]{:S(2)}) collective-permute-start(bf16[4,128,128]{2,1,0:T(8,128)(2,1)S(1)} %shard_map.80.mine_ref), channel_id=1, source_target_pairs={{0,8},{4,12},{8,0},{12,4},{16,24},{20,28},{24,16},{28,20},{1,9},{5... | collective-permute-start | bytes 393224 | tf_op jit(solution)/shard_map/ppermute | solution.py:272
  24.7 11.6 %collective-permute-start.5 = (bf16[4,128,128]{2,1,0:T(8,128)(2,1)S(1)}, bf16[4,128,128]{2,1,0:T(8,128)(2,1)S(1)}, u32[]{:S(2)}, u32[]{:S(2)}) collective-permute-start(bf16[4,128,128]{2,1,0:T(8,128)(2,1)S(1)} %shard_map.81), channel_id=1, source_target_pairs={{0,16},{4,20},{8,24},{12,28},{16,0},{20,4},{24,8},{28,12},{1,17},{... | collective-permute-start | bytes 393224 | tf_op jit(solution)/shard_map/ppermute | solution.py:272
  27.4 12.0 %collective-permute-start.2 = (bf16[528,128]{1,0:T(8,128)(2,1)S(1)}, bf16[528,128]{1,0:T(8,128)(2,1)S(1)}, u32[]{:S(2)}, u32[]{:S(2)}) collective-permute-start(bf16[528,128]{1,0:T(8,128)(2,1)S(1)} %shard_map.76), channel_id=1, source_target_pairs={{0,16},{4,20},{8,24},{12,28},{16,0},{20,4},{24,8},{28,12},{1,17},{... | collective-permute-start | bytes 405512 | tf_op jit(solution)/shard_map/ppermute | solution.py:272
  36.4 14.6 %collective-permute-start.6 = (bf16[4,128,128]{2,1,0:T(8,128)(2,1)S(1)}, bf16[4,128,128]{2,1,0:T(8,128)(2,1)S(1)}, u32[]{:S(2)}, u32[]{:S(2)}) collective-permute-start(bf16[4,128,128]{2,1,0:T(8,128)(2,1)S(1)} %shard_map.82.own_ref), channel_id=1, source_target_pairs={{0,4},{4,0},{8,12},{12,8},{16,20},{20,16},{24,28},{28,24},{1,5},{5... | collective-permute-start | bytes 393224 | tf_op jit(solution)/shard_map/ppermute | solution.py:272
  51.0 3.6 %copy-start.2 = (bf16[64,4096]{1,0:T(8,128)(2,1)S(1)}, bf16[64,4096]{1,0:T(8,128)(2,1)}, u32[]{:S(2)}) copy-start(bf16[64,4096]{1,0:T(8,128)(2,1)} %logit_ref.1) | copy-start | bytes 1572868
  51.1 3.6 %copy-start.6 = (f32[4096]{0:T(1024)S(1)}, f32[4096]{0:T(1024)}, u32[]{:S(2)}) copy-start(f32[4096]{0:T(1024)} %param.12) | copy-start | bytes 49156
  52.7 2.1 %collective-permute-start.7 = (bf16[64,1024]{1,0:T(8,128)(2,1)S(1)}, bf16[64,1024]{1,0:T(8,128)(2,1)S(1)}, u32[]{:S(2)}, u32[]{:S(2)}) collective-permute-start(bf16[64,1024]{1,0:T(8,128)(2,1)S(1)} %get-tuple-element.34), channel_id=1, source_target_pairs={{0,1},{1,0},{2,3},{3,2},{4,5},{5,4},{6,7},{7,6},{8,9},{9,8},{10,11... | collective-permute-start | bytes 393224 | tf_op jit(solution)/shard_map/ppermute | solution.py:272
  52.8 6.4 %collective-permute-start.8 = (bf16[64,1024]{1,0:T(8,128)(2,1)S(1)}, bf16[64,1024]{1,0:T(8,128)(2,1)S(1)}, u32[]{:S(2)}, u32[]{:S(2)}) collective-permute-start(bf16[64,1024]{1,0:T(8,128)(2,1)S(1)} %get-tuple-element.35), channel_id=1, source_target_pairs={{0,2},{1,3},{2,0},{3,1},{4,6},{5,7},{6,4},{7,5},{8,10},{9,11},{10,... | collective-permute-start | bytes 393224 | tf_op jit(solution)/shard_map/ppermute | solution.py:272
  54.4 6.6 %collective-permute-start.9 = (bf16[64,1024]{1,0:T(8,128)(2,1)S(1)}, bf16[64,1024]{1,0:T(8,128)(2,1)S(1)}, u32[]{:S(2)}, u32[]{:S(2)}) collective-permute-start(bf16[64,1024]{1,0:T(8,128)(2,1)S(1)} %get-tuple-element.36), channel_id=1, source_target_pairs={{0,3},{1,2},{2,1},{3,0},{4,7},{5,6},{6,5},{7,4},{8,11},{9,10},{10,... | collective-permute-start | bytes 393224 | tf_op jit(solution)/shard_map/ppermute | solution.py:272

commit v3 on v2

--- a/solution.py
+++ b/solution.py
@@ -38,13 +38,14 @@
     return jnp.sum(block * block, axis=axis, keepdims=True)
 
 
-def key_state_kernel(width, k_hbm, gate_hbm, kk_ref, kt_ref, k_ref, gate_ref, sems):
+def key_state_kernel(width, k_hbm, v_hbm, gate_hbm, kk_ref, kt_ref, k_ref, v_ref, scale_ref, gate_ref, sems):
     heads = gate_ref.shape[0]
     half = width // 2
     loads = [pltpu.make_async_copy(gate_hbm, gate_ref, sems.at[heads])]
     for h in range(heads):
         cols = slice(h * width, (h + 1) * width)
         loads.append(pltpu.make_async_copy(k_hbm.at[:, cols], k_ref.at[:, cols], sems.at[h]))
+    loads.append(pltpu.make_async_copy(v_hbm, v_ref, sems.at[heads + 1]))
     for load in loads:
         load.start()
     row = lax.broadcasted_iota(jnp.int32, (half, width), 0)
@@ -54,17 +55,19 @@
     for h in range(heads):
         loads[1 + h].wait()
         key = k_ref[:, h * width : (h + 1) * width]
-        turned = key.T
-        kt_ref[h] = turned
-        turned = turned.astype(F32)
-        wide = turned * (gate_ref[h : h + 1] / (square_sum(turned, 0) + EPS))
-        kk = dot(wide.astype(BF16), key)
+        turned = key.T.astype(F32)
+        total = square_sum(turned, 0) + EPS
+        scale_ref[h : h + 1] = gate_ref[h : h + 1] * lax.rsqrt(total)
+        wide = (turned * (gate_ref[h : h + 1] / total)).astype(BF16)
+        kt_ref[h] = wide
+        kk = dot(wide, key)
         diag = jnp.where(row == col, kk[:half], jnp.where(row + half == col, kk[half:], 0.0))
         diags.append(jnp.sum(diag, axis=0, keepdims=True))
         other = pltpu.roll(kk[half:], half, 1)
         packed = jnp.where(row > col, other, jnp.where(row == col, 0.0, kk[:half]))
         kk_ref[h * half : (h + 1) * half] = packed.astype(BF16)
     store_diag(kk_ref, heads * half, jnp.concatenate(diags, axis=0))
+    loads[-1].wait()
 
 
 def store_diag(ref, at, diag):
@@ -100,32 +103,18 @@
     refs[-1][...] = prefix(refs[:-1], lambda ref: ref[...].astype(F32), 1).astype(BF16)
 
 
-def value_state_kernel(width, k_ref, v_ref, gate_ref, val_ref, vk_ref):
-    gates = gate_ref[...].T
-    for h in range(gate_ref.shape[0]):
+def value_state_kernel(width, k_ref, v_ref, scale_ref, val_ref, vk_ref):
+    scales = scale_ref[...].T
+    for h in range(scale_ref.shape[0]):
         cols = slice(h * width, (h + 1) * width)
-        key = k_ref[:, cols]
-        scale = lax.rsqrt(square_sum(key.astype(F32), 1) + EPS)
-        val = (v_ref[:, cols].astype(F32) * (gates[:, h : h + 1] * scale)).astype(BF16)
+        val = (v_ref[:, cols].astype(F32) * scales[:, h : h + 1]).astype(BF16)
         val_ref[:, cols] = val
-        vk_ref[h] = dot(val, key, ((0,), (0,))).astype(BF16)
-
-
-def prepare_kernel(width, q_ref, k_ref, gate_ref, qt_ref, wt_ref):
-    heads, toks = gate_ref.shape
-    half = toks // 2
-    gates = gate_ref[...].T
-    keep = lax.broadcasted_iota(jnp.int32, (half, half), 0) <= lax.broadcasted_iota(
-        jnp.int32, (half, half), 1
-    )
-    for h in range(heads):
-        cols = slice(h * width, (h + 1) * width)
-        key = k_ref[:, cols]
-        weight = gates[:, h : h + 1] / (square_sum(key.astype(F32), 1) + EPS)
-        wt_ref[h, 0] = jnp.where(keep, weight[:half], 0.0)
-        wt_ref[h, 1] = jnp.broadcast_to(weight[:half], (half, half))
-        wt_ref[h, 2] = jnp.where(keep, weight[half:], 0.0)
-        query = q_ref[:, cols].T.astype(F32)
+        vk_ref[h] = dot(val, k_ref[:, cols], ((0,), (0,))).astype(BF16)
+
+
+def prepare_kernel(width, q_ref, qt_ref):
+    for h in range(qt_ref.shape[0]):
+        query = q_ref[:, h * width : (h + 1) * width].T.astype(F32)
         qt_ref[h] = query * lax.rsqrt(square_sum(query, 0) + EPS)
 
 
@@ -141,49 +130,47 @@
     return total
 
 
-def project(lhs, ridges, ps, h):
-    toks = ps.shape[2]
-    direction = ps[h]
-    out = dot(lhs[h], direction.astype(BF16))
-    ridge = jnp.concatenate([ridges[h]] * (toks // ridges.shape[2]), axis=1)
-    return direction, out, out[toks:] + ridge * direction
-
-
-def sweep(kt_ref, wt_ref, lhs, ridges, old, new, norms):
-    half = old[0].shape[2] // 2
+def operator(k_ref, lhs, directions, h):
+    _, width, toks = directions.shape
+    half = toks // 2
+    low = directions[h].astype(BF16)
+    score = dot(k_ref[:, h * width : (h + 1) * width], low).astype(BF16)
+    keep = lax.broadcasted_iota(jnp.int32, (half, half), 0) <= lax.broadcasted_iota(
+        jnp.int32, (half, half), 1
+    )
+    none = jnp.zeros((half, half), BF16)
+    upper = jnp.concatenate([jnp.where(keep, score[:half, :half], none), score[:half, half:]], axis=1)
+    lower = jnp.concatenate([none, jnp.where(keep, score[half:, half:], none)], axis=1)
+    return dot(lhs[h], jnp.concatenate([low, upper, lower], axis=0))
+
+
+def sweep(k_ref, lhs, ridges, old, new, norms):
     after = []
-    for h in range(kt_ref.shape[0]):
-        direction, out, image = project(lhs, ridges, old[1], h)
-        top = jnp.concatenate(
-            [
-                (wt_ref[h, 0] * out[:half, :half]).astype(BF16),
-                (wt_ref[h, 1] * out[:half, half:]).astype(BF16),
-            ],
-            axis=1,
-        )
-        low = jnp.concatenate(
-            [
-                jnp.zeros((half, half), BF16),
-                (wt_ref[h, 2] * out[half : 2 * half, half:]).astype(BF16),
-            ],
-            axis=1,
-        )
-        image = image + dot(kt_ref[h], jnp.concatenate([top, low], axis=0))
-        alpha = norms[h] / jnp.sum(direction * image, axis=0, keepdims=True)
-        residual = old[0][h] - alpha * image
-        new[0][h] = residual
-        following = square_sum(residual, 0)
-        new[1][h] = residual + (following / norms[h]) * direction
-        step = alpha * direction
-        new[2][h] = step if old[2] is None else old[2][h] + step
-        after.append(following)
+    width, toks = old[0].shape[1:]
+    for h in range(lhs.shape[0]):
+        image = operator(k_ref, lhs, old[1], h)
+        parts = []
+        for c in range(0, toks, width):
+            at = slice(c, c + width)
+            direction = old[1][h, :, at]
+            applied = image[:, at] + ridges[h] * direction
+            norm = norms[h][:, at]
+            alpha = norm / jnp.sum(direction * applied, axis=0, keepdims=True)
+            residual = old[0][h, :, at] - alpha * applied
+            new[0][h, :, at] = residual
+            following = square_sum(residual, 0)
+            step = alpha * direction
+            new[2][h, :, at] = step if old[2] is None else old[2][h, :, at] + step
+            new[1][h, :, at] = residual + (following / norm) * direction
+            parts.append(following)
+        after.append(jnp.concatenate(parts, axis=1))
     return tuple(after)
 
 
-def cg_first_kernel(width, rounds, sweeps, k_ref, kt_ref, qt_ref, wt_ref, ridge_ref, *refs):
+def cg_first_kernel(width, rounds, sweeps, k_ref, kt_ref, qt_ref, ridge_ref, *refs):
     totals = refs[:rounds]
     lhs, ridges, norm_ref, *state = refs[rounds:]
-    heads, _, toks = qt_ref.shape
+    heads, _, _ = qt_ref.shape
     part = width // 2
     inner = lax.broadcasted_iota(jnp.int32, (part, part), 0) < lax.broadcasted_iota(
         jnp.int32, (part, part), 1
@@ -196,38 +183,33 @@
         turned = upper.T
         tri = upper[:, :part]
         tri_t = turned[:part]
-        lhs[h, :toks] = k_ref[:, h * width : (h + 1) * width]
-        lhs[h, toks : toks + part] = jnp.concatenate(
+        lhs[h, :part, :width] = jnp.concatenate(
             [jnp.where(inner, tri, tri_t), upper[:, part:]], axis=1
         ).astype(BF16)
-        lhs[h, toks + part :] = jnp.concatenate(
+        lhs[h, part:, :width] = jnp.concatenate(
             [turned[part:], jnp.where(inner, tri_t, tri)], axis=1
         ).astype(BF16)
+        lhs[h, :, width:] = kt_ref[h]
         ridges[h] = jnp.broadcast_to(ridge_t[:, h : h + 1], (width, width))
         norms.append(square_sum(qt_ref[h], 0))
-    fixed = (kt_ref, wt_ref, lhs, ridges)
+    fixed = (k_ref, lhs, ridges)
     norms = sweep(*fixed, (qt_ref, qt_ref, None), state, norms)
     norms = lax.fori_loop(1, sweeps, lambda _, now: sweep(*fixed, state, state, now), norms)
     norm_ref[...] = jnp.concatenate(norms, axis=0)
 
 
-def cg_last_kernel(width, sweeps, kt_ref, wt_ref, lhs, ridges, norm_ref, *refs):
+def cg_last_kernel(width, sweeps, k_ref, lhs, ridges, norm_ref, *refs):
     given, x_ref, state = refs[:3], refs[3], refs[4:]
-    heads = kt_ref.shape[0]
-    half = wt_ref.shape[2]
-    fixed = (kt_ref, wt_ref, lhs, ridges)
+    heads = lhs.shape[0]
+    fixed = (k_ref, lhs, ridges)
     norms = tuple(norm_ref[h : h + 1] for h in range(heads))
     norms = sweep(*fixed, given, state, norms)
     norms = lax.fori_loop(1, sweeps, lambda _, now: sweep(*fixed, state, state, now), norms)
     for h in range(heads):
-        direction, out, image = project(lhs, ridges, state[1], h)
-        curve = jnp.sum(direction * image, axis=0, keepdims=True)
-        score = out[:half]
-        left = jnp.sum(score[:, :half] * score[:, :half] * wt_ref[h, 0], axis=0, keepdims=True)
-        right = jnp.sum(score[:, half:] * score[:, half:] * wt_ref[h, 1], axis=0, keepdims=True)
-        score = out[half : 2 * half, half:]
-        right = right + jnp.sum(score * score * wt_ref[h, 2], axis=0, keepdims=True)
-        alpha = norms[h] / (curve + jnp.concatenate([left, right], axis=1))
+        direction = state[1][h]
+        ridge = jnp.concatenate([ridges[h]] * (direction.shape[1] // width), axis=1)
+        image = operator(k_ref, lhs, state[1], h) + ridge * direction
+        alpha = norms[h] / jnp.sum(direction * image, axis=0, keepdims=True)
         x = state[2][h] + alpha * direction
         x_ref[:, h * width : (h + 1) * width] = x.astype(BF16).T
 
@@ -288,33 +270,37 @@
     packed = heads * width // 2 + 2 * heads
     work = 2 * toks * width * width * heads
 
-    kk, kt = call(
+    kk, kt, keys, vals, scales = call(
         functools.partial(key_state_kernel, width),
-        [shape(packed, width), shape(heads, width, toks)],
-        [pl.BlockSpec(memory_space=pltpu.MemorySpace.HBM)] * 2,
         [
-            pltpu.VMEM((toks, cols), BF16),
-            pltpu.VMEM((heads, toks), F32),
-            pltpu.SemaphoreType.DMA((heads + 1,)),
+            shape(packed, width),
+            shape(heads, width, toks),
+            shape(toks, cols),
+            shape(toks, cols),
+            shape(heads, toks, dtype=F32),
         ],
-        flops=work,
-    )(key_rows, gates)
+        [pl.BlockSpec(memory_space=pltpu.MemorySpace.HBM)] * 3,
+        [pltpu.VMEM((heads, toks), F32), pltpu.SemaphoreType.DMA((heads + 2,))],
+        flops=work,
+    )(
+        *(
+            pltpu.with_memory_space_constraint(x, pltpu.MemorySpace.HBM)
+            for x in (key_rows, values, gates)
+        )
+    )
     vals, vk = call(
         functools.partial(value_state_kernel, width),
         [shape(toks, cols), shape(heads, width, width)],
         [VMEM] * 3,
         flops=work,
-    )(key_rows, values, gates)
-    qt, wt = call(
+    )(keys, vals, scales)
+    qt = call(
         functools.partial(prepare_kernel, width),
-        [
-            shape(heads, width, toks, dtype=F32),
-            shape(heads, 3, toks // 2, toks // 2, dtype=F32),
-        ],
-        [VMEM] * 3,
+        shape(heads, width, toks, dtype=F32),
+        [VMEM],
         mib=4,
         flops=work,
-    )(queries, key_rows, gates)
+    )(queries)
     gated = call(gate_kernel, shape(*gate_logits.shape, dtype=F32), [VMEM] * 2, flops=work)(
         norm_gain[None, :], gate_logits
     )
@@ -341,23 +327,23 @@
     lhs, ridges, norms, *state = call(
         functools.partial(cg_first_kernel, width, rounds, FIRST),
         [
-            shape(heads, toks + width, width),
+            shape(heads, width, width + toks),
             shape(heads, width, width, dtype=F32),
             shape(heads, toks, dtype=F32),
         ]
         + [shape(heads, width, toks, dtype=F32)] * 3,
-        [VMEM] * (5 + rounds),
+        [VMEM] * (4 + rounds),
         mib=4,
         flops=10 * work,
-    )(key_rows, kt, qt, wt, ridge_diag, *key_in)
+    )(keys, kt, qt, ridge_diag, *key_in)
     x = call(
         functools.partial(cg_last_kernel, width, ITERS - 1 - FIRST),
         shape(toks, cols),
-        [VMEM] * 8,
+        [VMEM] * 7,
         [pltpu.VMEM((heads, width, toks), F32)] * 3,
         mib=8,
         flops=10 * work,
-    )(kt, wt, lhs, ridges, norms, *state)
+    )(keys, lhs, ridges, norms, *state)
 
     pieces = call(
         functools.partial(read_kernel, width, spots),
@@ -365,7 +351,7 @@
         [VMEM] * 6,
         [pltpu.VMEM((toks, cols), BF16)],
         flops=work,
-    )(x, key_rows, vals, near, own, far)
+    )(x, keys, vals, near, own, far)
     arrived = [pieces[0]] + [swap(pieces[k], "head", spots, k) for k in range(1, spots)]
     return call(
         functools.partial(norm_kernel, spots),

time: 62.2 us -> 59.2 us (0.952)
  Pallas kernels: 20.8 us -> 17.4 us
  waiting for transfers between devices: 26.5 us -> 29.2 us
  local copies, waits for them, and re-layouts: 2.81 us -> 0.44 us
    ppermute x10, waiting for transfers between devices: 26.5 us -> 29.2 us  [swap(): return lax.ppermute(x, axis, [(i, i ^ step) for i in range(size)])]
    unnamed x16 -> x8, local copies, waits for them, and re-layouts: 2.81 us -> 0.44 us
    pallas_call x1, Pallas kernels: 1.45 us -> 0.25 us  [shards(): call(functools.partial(prepare_kernel, width), shape(heads, width, toks,...]
    pallas_call x1, Pallas kernels: 5.39 us -> 4.33 us  [shards(): call(functools.partial(cg_last_kernel, width, ITERS - 1 - FIRST), shape(t...]
    pallas_call x1, Pallas kernels: 6.19 us -> 5.17 us  [shards(): call(functools.partial(cg_first_kernel, width, rounds, FIRST), [shape(hea...]
    pallas_call x1, Pallas kernels: 2 us -> 1.11 us  [shards(): call(functools.partial(value_state_kernel, width), [shape(toks, cols), sh...]
    pallas_call x1, Pallas kernels: 2.76 us -> 3.48 us  [shards(): call(functools.partial(key_state_kernel, width), [shape(packed, width), s...]
  transfers between devices with their start and end apart: 10 -> 10, of which waited for: 5 -> 5; matrix products, arithmetic and copies ran while one was open for 0% -> 0% of each run, Pallas kernels for 26% -> 17%
where the time goes in v3:
time: 59.2 us; the launch traced here: 58.9 us
  waiting for transfers between devices  29.2 us (49%)
  Pallas kernels  17.4 us (29%)
  starting transfers between devices  11.8 us (20%)
    ppermute x10, waiting for transfers between devices, swap(): return lax.ppermute(x, axis, [(i, i ^ step) for i in range(size)])  29.2 us
    ppermute x10, starting transfers between devices, swap(): return lax.ppermute(x, axis, [(i, i ^ step) for i in range(size)])  11.8 us
    pallas_call x1, Pallas kernels, shards(): call(functools.partial(cg_first_kernel, width, rounds, FIRST), [shape(hea...  5.17 us
    pallas_call x1, Pallas kernels, shards(): call(functools.partial(cg_last_kernel, width, ITERS - 1 - FIRST), shape(t...  4.33 us
    pallas_call x1, Pallas kernels, shards(): call(functools.partial(key_state_kernel, width), [shape(packed, width), s...  3.48 us
    pallas_call x1, Pallas kernels, shards(): call(functools.partial(read_kernel, width, spots), [shape(rows, cols)] *...  1.6 us
  transfers between devices with their start and end apart: 10, of which 5 were waited for; matrix products, arithmetic and copies ran while one was open for 0% of the time, Pallas kernels for 17%

profile of v3, /device:TPU:0, one launch (start us, length us, event | category | flops | bytes accessed | tf_op | source)
XLA Modules:
  0.0 58.9 jit_solution(9244268141549481524)
XLA Ops:
  0.0 3.5 %shard_map.73 = (bf16[528,128]{1,0:T(8,128)(2,1)S(1)}, bf16[8,128,256]{2,1,0:T(8,128)(2,1)S(1)}, bf16[256,1024]{1,0:T(8,128)(2,1)S(1)}, bf16[256,1024]{1,0:T(8,128)(2,1)S(1)}, f32[8,256]{1,0:T(8,128)S(1)}) custom-call(bf16[256,1024]{1,0:T(8,128)(2,1)} %k_hbm.1, bf16[256,1024]{1,0:T(8,128)(2,1)} %v_hbm.1, f32[8,256]{1,0:T(8,128)} %bitcast.3), custom_call_target="tpu_custom_call" | custom-call | flops 67108864 | bytes 1048576 | tf_op jit(solution)/shard_map/pallas_call | solution.py:273
  3.5 1.1 %shard_map.79 = (bf16[256,1024]{1,0:T(8,128)(2,1)S(1)}, bf16[8,128,128]{2,1,0:T(8,128)(2,1)S(1)}) custom-call(bf16[256,1024]{1,0:T(8,128)(2,1)S(1)} %get-tuple-element.22.k_ref, bf16[256,1024]{1,0:T(8,128)(2,1)S(1)} %get-tuple-element.31.v_ref, f32[8,256]{1,0:T(8,128)S(1)} %get-tuple-element.32.scale_ref), custom_call_target="tpu_custom_call" | custom-call | flops 67108864 | bytes 1048576 | tf_op jit(solution)/shard_map/pallas_call | solution.py:291
  4.6 3.0 %collective-permute-start.3 = (bf16[8,128,128]{2,1,0:T(8,128)(2,1)S(1)}, bf16[8,128,128]{2,1,0:T(8,128)(2,1)S(1)}, u32[]{:S(2)}, u32[]{:S(2)}) collective-permute-start(bf16[8,128,128]{2,1,0:T(8,128)(2,1)S(1)} %get-tuple-element.34.mine_ref), channel_id=1, source_target_pairs={{0,4},{4,0},{8,12},{12,8},{16,20},{20,16},{24,28},{28,24},{1,5},{5... | collective-permute-start | bytes 786440 | tf_op jit(solution)/shard_map/ppermute | solution.py:254
  7.6 0.1 collective-permute-start
  7.7 9.1 %collective-permute-done.other_ref.refs_0_ = bf16[528,128]{1,0:T(8,128)(2,1)S(1)} collective-permute-done((bf16[528,128]{1,0:T(8,128)(2,1)S(1)}, bf16[528,128]{1,0:T(8,128)(2,1)S(1)}, u32[]{:S(2)}, u32[]{:S(2)}) %collective-permute-start) | collective-permute-done | bytes 135200 | tf_op jit(solution)/shard_map/ppermute | solution.py:254
  16.9 1.9 %collective-permute-start.1 = (bf16[528,128]{1,0:T(8,128)(2,1)S(1)}, bf16[528,128]{1,0:T(8,128)(2,1)S(1)}, u32[]{:S(2)}, u32[]{:S(2)}) collective-permute-start(bf16[528,128]{1,0:T(8,128)(2,1)S(1)} %shard_map.75.mine_ref), channel_id=1, source_target_pairs={{0,8},{4,12},{8,0},{12,4},{16,24},{20,28},{24,16},{28,20},{1,9},{5... | collective-permute-start | bytes 405512 | tf_op jit(solution)/shard_map/ppermute | solution.py:254
  18.8 0.0 collective-permute-done.3.other_ref.near_ref
  18.8 0.0 copy-start
  18.8 0.3 collective-permute-start.4
  19.1 5.4 %collective-permute-done.4.other_ref.refs_0_ = bf16[4,128,128]{2,1,0:T(8,128)(2,1)S(1)} collective-permute-done((bf16[4,128,128]{2,1,0:T(8,128)(2,1)S(1)}, bf16[4,128,128]{2,1,0:T(8,128)(2,1)S(1)}, u32[]{:S(2)}, u32[]{:S(2)}) %collective-permute-start.4) | collective-permute-done | bytes 131104 | tf_op jit(solution)/shard_map/ppermute | solution.py:254
  24.5 2.6 %collective-permute-start.5 = (bf16[4,128,128]{2,1,0:T(8,128)(2,1)S(1)}, bf16[4,128,128]{2,1,0:T(8,128)(2,1)S(1)}, u32[]{:S(2)}, u32[]{:S(2)}) collective-permute-start(bf16[4,128,128]{2,1,0:T(8,128)(2,1)S(1)} %shard_map.81), channel_id=1, source_target_pairs={{0,16},{4,20},{8,24},{12,28},{16,0},{20,4},{24,8},{28,12},{1,17},{... | collective-permute-start | bytes 393224 | tf_op jit(solution)/shard_map/ppermute | solution.py:254
  27.2 0.0 collective-permute-done.1.other_ref.refs_1_
  27.2 0.4 collective-permute-start.2
  27.6 8.5 %collective-permute-done.5.refs_1_ = bf16[4,128,128]{2,1,0:T(8,128)(2,1)S(1)} collective-permute-done((bf16[4,128,128]{2,1,0:T(8,128)(2,1)S(1)}, bf16[4,128,128]{2,1,0:T(8,128)(2,1)S(1)}, u32[]{:S(2)}, u32[]{:S(2)}) %collective-permute-start.5) | collective-permute-done | bytes 131104 | tf_op jit(solution)/shard_map/ppermute | solution.py:254
  36.2 0.1 shard_map.82.own_ref
  36.2 1.5 %collective-permute-start.6 = (bf16[4,128,128]{2,1,0:T(8,128)(2,1)S(1)}, bf16[4,128,128]{2,1,0:T(8,128)(2,1)S(1)}, u32[]{:S(2)}, u32[]{:S(2)}) collective-permute-start(bf16[4,128,128]{2,1,0:T(8,128)(2,1)S(1)} %shard_map.82.own_ref), channel_id=1, source_target_pairs={{0,4},{4,0},{8,12},{12,8},{16,20},{20,16},{24,28},{28,24},{1,5},{5... | collective-permute-start | bytes 393224 | tf_op jit(solution)/shard_map/ppermute | solution.py:254
  37.8 0.0 copy-done
  37.8 0.0 copy-start.3
  37.8 0.2 shard_map.74.qt_ref
  38.0 0.0 collective-permute-done.2.refs_2_
  38.0 0.4 copy-done.3
  38.5 5.2 %shard_map.77 = (bf16[8,128,384]{2,1,0:T(8,128)(2,1)S(1)}, f32[8,128,128]{2,1,0:T(8,128)S(1)}, f32[8,256]{1,0:T(8,128)S(1)}, f32[8,128,256]{2,1,0:T(8,128)S(1)},...) custom-call(bf16[256,1024]{1,0:T(8,128)(2,1)S(1)} %get-tuple-element.22.k_ref, ...), custom_call_target="tpu_custom_call" | custom-call | flops 671088640 | bytes 1048576 | tf_op jit(solution)/shard_map/pallas_call | solution.py:327
  43.6 4.3 %shard_map.78.x_ref = bf16[256,1024]{1,0:T(8,128)(2,1)S(1)} custom-call(bf16[256,1024]{1,0:T(8,128)(2,1)S(1)} %get-tuple-element.22.k_ref, bf16[8,128,384]{2,1,0:T(8,128)(2,1)S(1)} %get-tuple-element.25.lhs, f32[8,128,128]{2,1,0:T(8,128)S(1)} %get-tuple-element.26.ridges, f32[8,256]{1,0:T(8,128)S(1)} %get-tuple-element.27.norm_ref, ...), custom_call_target="tpu_custom_call" | custom-call | flops 671088640 | bytes 1048576 | tf_op jit(solution)/shard_map/pallas_call | solution.py:339
  48.0 0.0 collective-permute-done.6.far_ref
  48.0 0.0 copy-start.1
  48.0 0.0 copy-start.2
  48.0 1.6 %shard_map.83 = (bf16[64,1024]{1,0:T(8,128)(2,1)S(1)}, bf16[64,1024]{1,0:T(8,128)(2,1)S(1)}, bf16[64,1024]{1,0:T(8,128)(2,1)S(1)}, bf16[64,1024]{1,0:T(8,128)(2,1)S(1)}) custom-call(bf16[256,1024]{1,0:T(8,128)(2,1)S(1)} %shard_map.78.x_ref, bf16[256,1024]{1,0:T(8,128)(2,1)S(1)} %get-tuple-element.22.k_ref, bf16[256,1024]{1,0:T(8,128)(2,1)S(1)} %get-tuple-element.33.val_ref, ...), custom_call_target="tpu_custom_call" | custom-call | flops 67108864 | bytes 1048576 | tf_op jit(solution)/shard_map/pallas_call | solution.py:348
  49.6 0.1 collective-permute-start.7
  49.7 1.6 %collective-permute-start.8 = (bf16[64,1024]{1,0:T(8,128)(2,1)S(1)}, bf16[64,1024]{1,0:T(8,128)(2,1)S(1)}, u32[]{:S(2)}, u32[]{:S(2)}) collective-permute-start(bf16[64,1024]{1,0:T(8,128)(2,1)S(1)} %get-tuple-element.37), channel_id=1, source_target_pairs={{0,2},{1,3},{2,0},{3,1},{4,6},{5,7},{6,4},{7,5},{8,10},{9,11},{10,... | collective-permute-start | bytes 393224 | tf_op jit(solution)/shard_map/ppermute | solution.py:254
  51.3 0.3 collective-permute-start.9
  51.5 0.0 copy-done.1
  51.5 0.0 copy-done.2
  51.5 0.1 shard_map.84.refs_4_
  51.7 0.0 collective-permute-done.7.refs_1_
  51.7 4.4 %collective-permute-done.8.refs_2_ = bf16[64,1024]{1,0:T(8,128)(2,1)S(1)} collective-permute-done((bf16[64,1024]{1,0:T(8,128)(2,1)S(1)}, bf16[64,1024]{1,0:T(8,128)(2,1)S(1)}, u32[]{:S(2)}, u32[]{:S(2)}) %collective-permute-start.8) | collective-permute-done | bytes 131104 | tf_op jit(solution)/shard_map/ppermute | solution.py:254
  56.1 1.7 %collective-permute-done.9.refs_3_ = bf16[64,1024]{1,0:T(8,128)(2,1)S(1)} collective-permute-done((bf16[64,1024]{1,0:T(8,128)(2,1)S(1)}, bf16[64,1024]{1,0:T(8,128)(2,1)S(1)}, u32[]{:S(2)}, u32[]{:S(2)}) %collective-permute-start.9) | collective-permute-done | bytes 131104 | tf_op jit(solution)/shard_map/ppermute | solution.py:254
  57.9 1.1 %shard_map.85 = bf16[64,4096]{1,0:T(8,128)(2,1)} custom-call(bf16[64,1024]{1,0:T(8,128)(2,1)S(1)} %get-tuple-element.35.refs_0_, bf16[64,1024]{1,0:T(8,128)(2,1)S(1)} %collective-permute-done.7.refs_1_, bf16[64,1024]{1,0:T(8,128)(2,1)S(1)} %collective-permute-done.8.refs_2_, bf16[64,1024]{1,0:T(8,128)(2,1)S(1)} %collective-permute-done.9.refs_3_, ...), custom_call_target="tpu_custom_call" | custom-call | flops 67108864 | bytes 1048576 | tf_op jit(solution)/shard_map/pallas_call | solution.py:356
  (4 shorter events, 0.1 us)
Async XLA Ops:
  4.6 14.2 %collective-permute-start.3 = (bf16[8,128,128]{2,1,0:T(8,128)(2,1)S(1)}, bf16[8,128,128]{2,1,0:T(8,128)(2,1)S(1)}, u32[]{:S(2)}, u32[]{:S(2)}) collective-permute-start(bf16[8,128,128]{2,1,0:T(8,128)(2,1)S(1)} %get-tuple-element.34.mine_ref), channel_id=1, source_target_pairs={{0,4},{4,0},{8,12},{12,8},{16,20},{20,16},{24,28},{28,24},{1,5},{5... | collective-permute-start | bytes 786440 | tf_op jit(solution)/shard_map/ppermute | solution.py:254
  7.6 9.2 %collective-permute-start = (bf16[528,128]{1,0:T(8,128)(2,1)S(1)}, bf16[528,128]{1,0:T(8,128)(2,1)S(1)}, u32[]{:S(2)}, u32[]{:S(2)}) collective-permute-start(bf16[528,128]{1,0:T(8,128)(2,1)S(1)} %get-tuple-element.24.mine_ref), channel_id=1, source_target_pairs={{0,4},{4,0},{8,12},{12,8},{16,20},{20,16},{24,28},{28,24},{1,5},{5... | collective-permute-start | bytes 405512 | tf_op jit(solution)/shard_map/ppermute | solution.py:254
  16.9 10.3 %collective-permute-start.1 = (bf16[528,128]{1,0:T(8,128)(2,1)S(1)}, bf16[528,128]{1,0:T(8,128)(2,1)S(1)}, u32[]{:S(2)}, u32[]{:S(2)}) collective-permute-start(bf16[528,128]{1,0:T(8,128)(2,1)S(1)} %shard_map.75.mine_ref), channel_id=1, source_target_pairs={{0,8},{4,12},{8,0},{12,4},{16,24},{20,28},{24,16},{28,20},{1,9},{5... | collective-permute-start | bytes 405512 | tf_op jit(solution)/shard_map/ppermute | solution.py:254
  18.8 19.0 %copy-start = (bf16[256,1024]{1,0:T(8,128)(2,1)S(1)}, bf16[256,1024]{1,0:T(8,128)(2,1)}, u32[]{:S(2)}) copy-start(bf16[256,1024]{1,0:T(8,128)(2,1)} %q_ref.1) | copy-start | bytes 1572868
  18.8 5.7 %collective-permute-start.4 = (bf16[4,128,128]{2,1,0:T(8,128)(2,1)S(1)}, bf16[4,128,128]{2,1,0:T(8,128)(2,1)S(1)}, u32[]{:S(2)}, u32[]{:S(2)}) collective-permute-start(bf16[4,128,128]{2,1,0:T(8,128)(2,1)S(1)} %shard_map.80.mine_ref), channel_id=1, source_target_pairs={{0,8},{4,12},{8,0},{12,4},{16,24},{20,28},{24,16},{28,20},{1,9},{5... | collective-permute-start | bytes 393224 | tf_op jit(solution)/shard_map/ppermute | solution.py:254
  24.5 11.6 %collective-permute-start.5 = (bf16[4,128,128]{2,1,0:T(8,128)(2,1)S(1)}, bf16[4,128,128]{2,1,0:T(8,128)(2,1)S(1)}, u32[]{:S(2)}, u32[]{:S(2)}) collective-permute-start(bf16[4,128,128]{2,1,0:T(8,128)(2,1)S(1)} %shard_map.81), channel_id=1, source_target_pairs={{0,16},{4,20},{8,24},{12,28},{16,0},{20,4},{24,8},{28,12},{1,17},{... | collective-permute-start | bytes 393224 | tf_op jit(solution)/shard_map/ppermute | solution.py:254
  27.2 10.8 %collective-permute-start.2 = (bf16[528,128]{1,0:T(8,128)(2,1)S(1)}, bf16[528,128]{1,0:T(8,128)(2,1)S(1)}, u32[]{:S(2)}, u32[]{:S(2)}) collective-permute-start(bf16[528,128]{1,0:T(8,128)(2,1)S(1)} %shard_map.76), channel_id=1, source_target_pairs={{0,16},{4,20},{8,24},{12,28},{16,0},{20,4},{24,8},{28,12},{1,17},{... | collective-permute-start | bytes 405512 | tf_op jit(solution)/shard_map/ppermute | solution.py:254
  36.2 11.7 %collective-permute-start.6 = (bf16[4,128,128]{2,1,0:T(8,128)(2,1)S(1)}, bf16[4,128,128]{2,1,0:T(8,128)(2,1)S(1)}, u32[]{:S(2)}, u32[]{:S(2)}) collective-permute-start(bf16[4,128,128]{2,1,0:T(8,128)(2,1)S(1)} %shard_map.82.own_ref), channel_id=1, source_target_pairs={{0,4},{4,0},{8,12},{12,8},{16,20},{20,16},{24,28},{28,24},{1,5},{5... | collective-permute-start | bytes 393224 | tf_op jit(solution)/shard_map/ppermute | solution.py:254
  37.8 0.7 %copy-start.3 = (f32[8,128]{1,0:T(8,128)S(1)}, f32[8,128]{1,0:T(8,128)}, u32[]{:S(2)}) copy-start(f32[8,128]{1,0:T(8,128)} %ridge_ref.1) | copy-start | bytes 12292
  48.0 3.6 %copy-start.1 = (bf16[64,4096]{1,0:T(8,128)(2,1)S(1)}, bf16[64,4096]{1,0:T(8,128)(2,1)}, u32[]{:S(2)}) copy-start(bf16[64,4096]{1,0:T(8,128)(2,1)} %logit_ref.1) | copy-start | bytes 1572868
  48.0 3.6 %copy-start.2 = (f32[4096]{0:T(1024)S(1)}, f32[4096]{0:T(1024)}, u32[]{:S(2)}) copy-start(f32[4096]{0:T(1024)} %param.12) | copy-start | bytes 49156
  49.6 2.1 %collective-permute-start.7 = (bf16[64,1024]{1,0:T(8,128)(2,1)S(1)}, bf16[64,1024]{1,0:T(8,128)(2,1)S(1)}, u32[]{:S(2)}, u32[]{:S(2)}) collective-permute-start(bf16[64,1024]{1,0:T(8,128)(2,1)S(1)} %get-tuple-element.36), channel_id=1, source_target_pairs={{0,1},{1,0},{2,3},{3,2},{4,5},{5,4},{6,7},{7,6},{8,9},{9,8},{10,11... | collective-permute-start | bytes 393224 | tf_op jit(solution)/shard_map/ppermute | solution.py:254
  49.7 6.4 %collective-permute-start.8 = (bf16[64,1024]{1,0:T(8,128)(2,1)S(1)}, bf16[64,1024]{1,0:T(8,128)(2,1)S(1)}, u32[]{:S(2)}, u32[]{:S(2)}) collective-permute-start(bf16[64,1024]{1,0:T(8,128)(2,1)S(1)} %get-tuple-element.37), channel_id=1, source_target_pairs={{0,2},{1,3},{2,0},{3,1},{4,6},{5,7},{6,4},{7,5},{8,10},{9,11},{10,... | collective-permute-start | bytes 393224 | tf_op jit(solution)/shard_map/ppermute | solution.py:254
  51.3 6.6 %collective-permute-start.9 = (bf16[64,1024]{1,0:T(8,128)(2,1)S(1)}, bf16[64,1024]{1,0:T(8,128)(2,1)S(1)}, u32[]{:S(2)}, u32[]{:S(2)}) collective-permute-start(bf16[64,1024]{1,0:T(8,128)(2,1)S(1)} %get-tuple-element.38), channel_id=1, source_target_pairs={{0,3},{1,2},{2,1},{3,0},{4,7},{5,6},{6,5},{7,4},{8,11},{9,10},{10,... | collective-permute-start | bytes 393224 | tf_op jit(solution)/shard_map/ppermute | solution.py:254

commit v4 on v3

--- a/solution.py
+++ b/solution.py
@@ -89,27 +89,30 @@
     store_diag(total_ref, at, load_diag(mine_ref, at) + load_diag(other_ref, at))
 
 
-def value_fold_kernel(mine_ref, other_ref, total_ref):
-    count = total_ref.shape[0]
-    part = pl.ds((lax.axis_index("seq") & 1) * count, count)
-    total_ref[...] = (mine_ref[part].astype(F32) + other_ref[part].astype(F32)).astype(BF16)
-
-
 def value_join_kernel(mine_ref, other_ref, total_ref):
     total_ref[...] = (mine_ref[...].astype(F32) + other_ref[...].astype(F32)).astype(BF16)
 
 
-def value_prefix_kernel(*refs):
-    refs[-1][...] = prefix(refs[:-1], lambda ref: ref[...].astype(F32), 1).astype(BF16)
-
-
-def value_state_kernel(width, k_ref, v_ref, scale_ref, val_ref, vk_ref):
+def value_prefix_kernel(keep_ref, near_ref, *refs):
+    later = (lax.axis_index("seq") & 1).astype(F32)
+    before = prefix(refs[:-2], lambda ref: ref[...].astype(F32), 1)
+    refs[-2][...] = (before + later * near_ref[...].astype(F32)).astype(BF16)
+    refs[-1][...] = (before + (1.0 - later) * keep_ref[...].astype(F32)).astype(BF16)
+
+
+def value_state_kernel(width, k_ref, v_ref, scale_ref, val_ref, keep_ref, give_ref):
     scales = scale_ref[...].T
-    for h in range(scale_ref.shape[0]):
-        cols = slice(h * width, (h + 1) * width)
-        val = (v_ref[:, cols].astype(F32) * scales[:, h : h + 1]).astype(BF16)
-        val_ref[:, cols] = val
-        vk_ref[h] = dot(val, k_ref[:, cols], ((0,), (0,))).astype(BF16)
+    later = (lax.axis_index("seq") & 1) == 1
+    count = keep_ref.shape[0]
+    for h in range(count):
+        pair = []
+        for head in (h, count + h):
+            cols = slice(head * width, (head + 1) * width)
+            val = (v_ref[:, cols].astype(F32) * scales[:, head : head + 1]).astype(BF16)
+            val_ref[:, cols] = val
+            pair.append(dot(val, k_ref[:, cols], ((0,), (0,))))
+        keep_ref[h] = jnp.where(later, pair[1], pair[0]).astype(BF16)
+        give_ref[h] = jnp.where(later, pair[0], pair[1]).astype(BF16)
 
 
 def prepare_kernel(width, q_ref, qt_ref):
@@ -214,7 +217,7 @@
         x_ref[:, h * width : (h + 1) * width] = x.astype(BF16).T
 
 
-def read_kernel(width, spots, x_ref, k_ref, val_ref, near_ref, own_ref, far_ref, *refs):
+def read_kernel(width, spots, x_ref, k_ref, val_ref, own_ref, far_ref, *refs):
     outs, tmp = refs[:spots], refs[spots]
     count = own_ref.shape[0]
     later = lax.axis_index("seq") & 1
@@ -228,8 +231,6 @@
         cols = slice(h * width, (h + 1) * width)
         x = x_ref[:, cols]
         state = jnp.where(later == h // count, own_ref[h % count], far_ref[h % count])
-        near = near_ref[h].astype(F32) * later.astype(F32)
-        state = (state.astype(F32) + near).astype(BF16)
         score = jnp.where(keep, dot(x, k_ref[:, cols], ((1,), (1,))), 0.0).astype(BF16)
         out = dot(x, state, ((1,), (1,))) + dot(score, val_ref[:, cols])
         tmp[:, cols] = out.astype(BF16)
@@ -288,9 +289,9 @@
             for x in (key_rows, values, gates)
         )
     )
-    vals, vk = call(
+    vals, keep, give = call(
         functools.partial(value_state_kernel, width),
-        [shape(toks, cols), shape(heads, width, width)],
+        [shape(toks, cols)] + [shape(heads // 2, width, width)] * 2,
         [VMEM] * 3,
         flops=work,
     )(keys, vals, scales)
@@ -315,14 +316,16 @@
                 [VMEM] * 2,
                 mib=4,
             )(kk, key_in[-1])
-    near = swap(vk, "seq", size, 1)
-    vk = call(value_fold_kernel, shape(heads // 2, width, width), [VMEM] * 2)(vk, near)
+    near = swap(give, "seq", size, 1)
+    vk = call(value_join_kernel, shape(*keep.shape), [VMEM] * 2)(keep, near)
     for k in range(1, rounds):
         value_in.append(swap(vk, "seq", size, 1 << k))
         if k + 1 < rounds:
             vk = call(value_join_kernel, shape(*vk.shape), [VMEM] * 2)(vk, value_in[-1])
-    own = call(value_prefix_kernel, shape(*vk.shape), [VMEM] * (rounds - 1))(*value_in)
-    far = swap(own, "seq", size, 1)
+    own, share = call(
+        value_prefix_kernel, [shape(*vk.shape)] * 2, [VMEM] * (rounds + 1)
+    )(keep, near, *value_in)
+    far = swap(share, "seq", size, 1)
 
     lhs, ridges, norms, *state = call(
         functools.partial(cg_first_kernel, width, rounds, FIRST),
@@ -348,10 +351,10 @@
     pieces = call(
         functools.partial(read_kernel, width, spots),
         [shape(rows, cols)] * spots,
-        [VMEM] * 6,
+        [VMEM] * 5,
         [pltpu.VMEM((toks, cols), BF16)],
         flops=work,
-    )(x, keys, vals, near, own, far)
+    )(x, keys, vals, own, far)
     arrived = [pieces[0]] + [swap(pieces[k], "head", spots, k) for k in range(1, spots)]
     return call(
         functools.partial(norm_kernel, spots),

time: 59.2 us -> 53.8 us (0.909)
  waiting for transfers between devices: 29.2 us -> 22.7 us
  starting transfers between devices: 11.8 us -> 13.2 us
    ppermute x10, waiting for transfers between devices: 29.2 us -> 22.7 us  [swap(): return lax.ppermute(x, axis, [(i, i ^ step) for i in range(size)])]
    ppermute x10, starting transfers between devices: 11.8 us -> 13.2 us  [swap(): return lax.ppermute(x, axis, [(i, i ^ step) for i in range(size)])]
  transfers between devices with their start and end apart: 10 -> 10, of which waited for: 5 -> 7; matrix products, arithmetic and copies ran while one was open for 0% -> 0% of each run, Pallas kernels for 17% -> 21%
where the time goes in v4:
time: 53.8 us; the launch traced here: 53.6 us
  waiting for transfers between devices  22.7 us (42%)
  Pallas kernels  17.4 us (32%)
  starting transfers between devices  13.2 us (25%)
    ppermute x10, waiting for transfers between devices, swap(): return lax.ppermute(x, axis, [(i, i ^ step) for i in range(size)])  22.7 us
    ppermute x10, starting transfers between devices, swap(): return lax.ppermute(x, axis, [(i, i ^ step) for i in range(size)])  13.2 us
    pallas_call x1, Pallas kernels, shards(): call(functools.partial(cg_first_kernel, width, rounds, FIRST), [shape(hea...  5.18 us
    pallas_call x1, Pallas kernels, shards(): call(functools.partial(cg_last_kernel, width, ITERS - 1 - FIRST), shape(t...  4.32 us
    pallas_call x1, Pallas kernels, shards(): call(functools.partial(key_state_kernel, width), [shape(packed, width), s...  3.48 us
    pallas_call x1, Pallas kernels, shards(): call(functools.partial(read_kernel, width, spots), [shape(rows, cols)] *...  1.6 us
    pallas_call x1, Pallas kernels, shards(): call(functools.partial(value_state_kernel, width), [shape(toks, cols)] +...  1.1 us
  transfers between devices with their start and end apart: 10, of which 7 were waited for; matrix products, arithmetic and copies ran while one was open for 0% of the time, Pallas kernels for 21%

profile of v4, /device:TPU:0, one launch (start us, length us, event | category | flops | bytes accessed | tf_op | source)
XLA Modules:
  0.0 53.6 jit_solution(11584004935013494528)
XLA Ops:
  0.0 3.5 %shard_map.73 = (bf16[528,128]{1,0:T(8,128)(2,1)S(1)}, bf16[8,128,256]{2,1,0:T(8,128)(2,1)S(1)}, bf16[256,1024]{1,0:T(8,128)(2,1)S(1)}, bf16[256,1024]{1,0:T(8,128)(2,1)S(1)}, f32[8,256]{1,0:T(8,128)S(1)}) custom-call(bf16[256,1024]{1,0:T(8,128)(2,1)} %k_hbm.1, bf16[256,1024]{1,0:T(8,128)(2,1)} %v_hbm.1, f32[8,256]{1,0:T(8,128)} %bitcast.3), custom_call_target="tpu_custom_call" | custom-call | flops 67108864 | bytes 1048576 | tf_op jit(solution)/shard_map/pallas_call | solution.py:274
  3.5 3.0 %collective-permute-start = (bf16[528,128]{1,0:T(8,128)(2,1)S(1)}, bf16[528,128]{1,0:T(8,128)(2,1)S(1)}, u32[]{:S(2)}, u32[]{:S(2)}) collective-permute-start(bf16[528,128]{1,0:T(8,128)(2,1)S(1)} %get-tuple-element.27.mine_ref), channel_id=1, source_target_pairs={{0,4},{4,0},{8,12},{12,8},{16,20},{20,16},{24,28},{28,24},{1,5},{5... | collective-permute-start | bytes 405512 | tf_op jit(solution)/shard_map/ppermute | solution.py:255
  6.5 1.1 %shard_map.79 = (bf16[256,1024]{1,0:T(8,128)(2,1)S(1)}, bf16[4,128,128]{2,1,0:T(8,128)(2,1)S(1)}, bf16[4,128,128]{2,1,0:T(8,128)(2,1)S(1)}) custom-call(bf16[256,1024]{1,0:T(8,128)(2,1)S(1)} %get-tuple-element.25.k_ref, bf16[256,1024]{1,0:T(8,128)(2,1)S(1)} %get-tuple-element.34.v_ref, f32[8,256]{1,0:T(8,128)S(1)} %get-tuple-element.35.scale_ref), custom_call_target="tpu_custom_call" | custom-call | flops 67108864 | bytes 1048576 | tf_op jit(solution)/shard_map/pallas_call | solution.py:292
  7.6 0.1 collective-permute-start.3
  7.7 2.8 %collective-permute-done.other_ref.refs_0_ = bf16[528,128]{1,0:T(8,128)(2,1)S(1)} collective-permute-done((bf16[528,128]{1,0:T(8,128)(2,1)S(1)}, bf16[528,128]{1,0:T(8,128)(2,1)S(1)}, u32[]{:S(2)}, u32[]{:S(2)}) %collective-permute-start) | collective-permute-done | bytes 135200 | tf_op jit(solution)/shard_map/ppermute | solution.py:255
  10.5 2.0 %collective-permute-start.1 = (bf16[528,128]{1,0:T(8,128)(2,1)S(1)}, bf16[528,128]{1,0:T(8,128)(2,1)S(1)}, u32[]{:S(2)}, u32[]{:S(2)}) collective-permute-start(bf16[528,128]{1,0:T(8,128)(2,1)S(1)} %shard_map.75.mine_ref), channel_id=1, source_target_pairs={{0,8},{4,12},{8,0},{12,4},{16,24},{20,28},{24,16},{28,20},{1,9},{5... | collective-permute-start | bytes 405512 | tf_op jit(solution)/shard_map/ppermute | solution.py:255
  12.6 0.4 collective-permute-done.3.other_ref.near_ref
  13.0 1.9 %collective-permute-start.4 = (bf16[4,128,128]{2,1,0:T(8,128)(2,1)S(1)}, bf16[4,128,128]{2,1,0:T(8,128)(2,1)S(1)}, u32[]{:S(2)}, u32[]{:S(2)}) collective-permute-start(bf16[4,128,128]{2,1,0:T(8,128)(2,1)S(1)} %shard_map.80.mine_ref), channel_id=1, source_target_pairs={{0,8},{4,12},{8,0},{12,4},{16,24},{20,28},{24,16},{28,20},{1,9},{5... | collective-permute-start | bytes 393224 | tf_op jit(solution)/shard_map/ppermute | solution.py:255
  14.8 3.6 %collective-permute-done.4.other_ref.refs_0_ = bf16[4,128,128]{2,1,0:T(8,128)(2,1)S(1)} collective-permute-done((bf16[4,128,128]{2,1,0:T(8,128)(2,1)S(1)}, bf16[4,128,128]{2,1,0:T(8,128)(2,1)S(1)}, u32[]{:S(2)}, u32[]{:S(2)}) %collective-permute-start.4) | collective-permute-done | bytes 131104 | tf_op jit(solution)/shard_map/ppermute | solution.py:255
  18.5 0.0 copy-start
  18.5 3.0 %collective-permute-start.5 = (bf16[4,128,128]{2,1,0:T(8,128)(2,1)S(1)}, bf16[4,128,128]{2,1,0:T(8,128)(2,1)S(1)}, u32[]{:S(2)}, u32[]{:S(2)}) collective-permute-start(bf16[4,128,128]{2,1,0:T(8,128)(2,1)S(1)} %shard_map.81), channel_id=1, source_target_pairs={{0,16},{4,20},{8,24},{12,28},{16,0},{20,4},{24,8},{28,12},{1,17},{... | collective-permute-start | bytes 393224 | tf_op jit(solution)/shard_map/ppermute | solution.py:255
  21.5 0.0 collective-permute-done.1.other_ref.refs_1_
  21.5 0.1 collective-permute-start.2
  21.6 9.6 %collective-permute-done.5.refs_1_ = bf16[4,128,128]{2,1,0:T(8,128)(2,1)S(1)} collective-permute-done((bf16[4,128,128]{2,1,0:T(8,128)(2,1)S(1)}, bf16[4,128,128]{2,1,0:T(8,128)(2,1)S(1)}, u32[]{:S(2)}, u32[]{:S(2)}) %collective-permute-start.5) | collective-permute-done | bytes 131104 | tf_op jit(solution)/shard_map/ppermute | solution.py:255
  31.2 0.1 shard_map.82
  31.3 1.1 %collective-permute-start.6 = (bf16[4,128,128]{2,1,0:T(8,128)(2,1)S(1)}, bf16[4,128,128]{2,1,0:T(8,128)(2,1)S(1)}, u32[]{:S(2)}, u32[]{:S(2)}) collective-permute-start(bf16[4,128,128]{2,1,0:T(8,128)(2,1)S(1)} %get-tuple-element.40), channel_id=1, source_target_pairs={{0,4},{4,0},{8,12},{12,8},{16,20},{20,16},{24,28},{28,24},{1,5},{5... | collective-permute-start | bytes 393224 | tf_op jit(solution)/shard_map/ppermute | solution.py:255
  32.5 0.0 copy-done
  32.5 0.0 copy-start.3
  32.5 0.2 shard_map.74.qt_ref
  32.7 0.2 collective-permute-done.2.refs_2_
  33.0 0.2 copy-done.3
  33.1 5.2 %shard_map.77 = (bf16[8,128,384]{2,1,0:T(8,128)(2,1)S(1)}, f32[8,128,128]{2,1,0:T(8,128)S(1)}, f32[8,256]{1,0:T(8,128)S(1)}, f32[8,128,256]{2,1,0:T(8,128)S(1)},...) custom-call(bf16[256,1024]{1,0:T(8,128)(2,1)S(1)} %get-tuple-element.25.k_ref, ...), custom_call_target="tpu_custom_call" | custom-call | flops 671088640 | bytes 1048576 | tf_op jit(solution)/shard_map/pallas_call | solution.py:330
  38.3 4.3 %shard_map.78.x_ref = bf16[256,1024]{1,0:T(8,128)(2,1)S(1)} custom-call(bf16[256,1024]{1,0:T(8,128)(2,1)S(1)} %get-tuple-element.25.k_ref, bf16[8,128,384]{2,1,0:T(8,128)(2,1)S(1)} %get-tuple-element.28.lhs, f32[8,128,128]{2,1,0:T(8,128)S(1)} %get-tuple-element.29.ridges, f32[8,256]{1,0:T(8,128)S(1)} %get-tuple-element.30.norm_ref, ...), custom_call_target="tpu_custom_call" | custom-call | flops 671088640 | bytes 1048576 | tf_op jit(solution)/shard_map/pallas_call | solution.py:342
  42.7 0.0 collective-permute-done.6.far_ref
  42.7 0.0 copy-start.1
  42.7 0.0 copy-start.2
  42.7 1.6 %shard_map.83 = (bf16[64,1024]{1,0:T(8,128)(2,1)S(1)}, bf16[64,1024]{1,0:T(8,128)(2,1)S(1)}, bf16[64,1024]{1,0:T(8,128)(2,1)S(1)}, bf16[64,1024]{1,0:T(8,128)(2,1)S(1)}) custom-call(bf16[256,1024]{1,0:T(8,128)(2,1)S(1)} %shard_map.78.x_ref, bf16[256,1024]{1,0:T(8,128)(2,1)S(1)} %get-tuple-element.25.k_ref, bf16[256,1024]{1,0:T(8,128)(2,1)S(1)} %get-tuple-element.36.val_ref, ...), custom_call_target="tpu_custom_call" | custom-call | flops 67108864 | bytes 1048576 | tf_op jit(solution)/shard_map/pallas_call | solution.py:351
  44.3 0.1 collective-permute-start.7
  44.4 1.6 %collective-permute-start.8 = (bf16[64,1024]{1,0:T(8,128)(2,1)S(1)}, bf16[64,1024]{1,0:T(8,128)(2,1)S(1)}, u32[]{:S(2)}, u32[]{:S(2)}) collective-permute-start(bf16[64,1024]{1,0:T(8,128)(2,1)S(1)} %get-tuple-element.43), channel_id=1, source_target_pairs={{0,2},{1,3},{2,0},{3,1},{4,6},{5,7},{6,4},{7,5},{8,10},{9,11},{10,... | collective-permute-start | bytes 393224 | tf_op jit(solution)/shard_map/ppermute | solution.py:255
  46.0 0.3 collective-permute-start.9
  46.2 0.0 copy-done.1
  46.2 0.0 copy-done.2
  46.2 0.1 shard_map.84.refs_4_
  46.4 0.0 collective-permute-done.7.refs_1_
  46.4 4.4 %collective-permute-done.8.refs_2_ = bf16[64,1024]{1,0:T(8,128)(2,1)S(1)} collective-permute-done((bf16[64,1024]{1,0:T(8,128)(2,1)S(1)}, bf16[64,1024]{1,0:T(8,128)(2,1)S(1)}, u32[]{:S(2)}, u32[]{:S(2)}) %collective-permute-start.8) | collective-permute-done | bytes 131104 | tf_op jit(solution)/shard_map/ppermute | solution.py:255
  50.8 1.7 %collective-permute-done.9.refs_3_ = bf16[64,1024]{1,0:T(8,128)(2,1)S(1)} collective-permute-done((bf16[64,1024]{1,0:T(8,128)(2,1)S(1)}, bf16[64,1024]{1,0:T(8,128)(2,1)S(1)}, u32[]{:S(2)}, u32[]{:S(2)}) %collective-permute-start.9) | collective-permute-done | bytes 131104 | tf_op jit(solution)/shard_map/ppermute | solution.py:255
  52.5 1.1 %shard_map.85 = bf16[64,4096]{1,0:T(8,128)(2,1)} custom-call(bf16[64,1024]{1,0:T(8,128)(2,1)S(1)} %get-tuple-element.41.refs_0_, bf16[64,1024]{1,0:T(8,128)(2,1)S(1)} %collective-permute-done.7.refs_1_, bf16[64,1024]{1,0:T(8,128)(2,1)S(1)} %collective-permute-done.8.refs_2_, bf16[64,1024]{1,0:T(8,128)(2,1)S(1)} %collective-permute-done.9.refs_3_, ...), custom_call_target="tpu_custom_call" | custom-call | flops 67108864 | bytes 1048576 | tf_op jit(solution)/shard_map/pallas_call | solution.py:359
  (4 shorter events, 0.2 us)
Async XLA Ops:
  3.5 7.0 %collective-permute-start = (bf16[528,128]{1,0:T(8,128)(2,1)S(1)}, bf16[528,128]{1,0:T(8,128)(2,1)S(1)}, u32[]{:S(2)}, u32[]{:S(2)}) collective-permute-start(bf16[528,128]{1,0:T(8,128)(2,1)S(1)} %get-tuple-element.27.mine_ref), channel_id=1, source_target_pairs={{0,4},{4,0},{8,12},{12,8},{16,20},{20,16},{24,28},{28,24},{1,5},{5... | collective-permute-start | bytes 405512 | tf_op jit(solution)/shard_map/ppermute | solution.py:255
  7.6 5.3 %collective-permute-start.3 = (bf16[4,128,128]{2,1,0:T(8,128)(2,1)S(1)}, bf16[4,128,128]{2,1,0:T(8,128)(2,1)S(1)}, u32[]{:S(2)}, u32[]{:S(2)}) collective-permute-start(bf16[4,128,128]{2,1,0:T(8,128)(2,1)S(1)} %get-tuple-element.38), channel_id=1, source_target_pairs={{0,4},{4,0},{8,12},{12,8},{16,20},{20,16},{24,28},{28,24},{1,5},{5... | collective-permute-start | bytes 393224 | tf_op jit(solution)/shard_map/ppermute | solution.py:255
  10.5 11.0 %collective-permute-start.1 = (bf16[528,128]{1,0:T(8,128)(2,1)S(1)}, bf16[528,128]{1,0:T(8,128)(2,1)S(1)}, u32[]{:S(2)}, u32[]{:S(2)}) collective-permute-start(bf16[528,128]{1,0:T(8,128)(2,1)S(1)} %shard_map.75.mine_ref), channel_id=1, source_target_pairs={{0,8},{4,12},{8,0},{12,4},{16,24},{20,28},{24,16},{28,20},{1,9},{5... | collective-permute-start | bytes 405512 | tf_op jit(solution)/shard_map/ppermute | solution.py:255
  13.0 5.5 %collective-permute-start.4 = (bf16[4,128,128]{2,1,0:T(8,128)(2,1)S(1)}, bf16[4,128,128]{2,1,0:T(8,128)(2,1)S(1)}, u32[]{:S(2)}, u32[]{:S(2)}) collective-permute-start(bf16[4,128,128]{2,1,0:T(8,128)(2,1)S(1)} %shard_map.80.mine_ref), channel_id=1, source_target_pairs={{0,8},{4,12},{8,0},{12,4},{16,24},{20,28},{24,16},{28,20},{1,9},{5... | collective-permute-start | bytes 393224 | tf_op jit(solution)/shard_map/ppermute | solution.py:255
  18.5 14.0 %copy-start = (bf16[256,1024]{1,0:T(8,128)(2,1)S(1)}, bf16[256,1024]{1,0:T(8,128)(2,1)}, u32[]{:S(2)}) copy-start(bf16[256,1024]{1,0:T(8,128)(2,1)} %q_ref.1) | copy-start | bytes 1572868
  18.5 12.7 %collective-permute-start.5 = (bf16[4,128,128]{2,1,0:T(8,128)(2,1)S(1)}, bf16[4,128,128]{2,1,0:T(8,128)(2,1)S(1)}, u32[]{:S(2)}, u32[]{:S(2)}) collective-permute-start(bf16[4,128,128]{2,1,0:T(8,128)(2,1)S(1)} %shard_map.81), channel_id=1, source_target_pairs={{0,16},{4,20},{8,24},{12,28},{16,0},{20,4},{24,8},{28,12},{1,17},{... | collective-permute-start | bytes 393224 | tf_op jit(solution)/shard_map/ppermute | solution.py:255
  21.5 11.4 %collective-permute-start.2 = (bf16[528,128]{1,0:T(8,128)(2,1)S(1)}, bf16[528,128]{1,0:T(8,128)(2,1)S(1)}, u32[]{:S(2)}, u32[]{:S(2)}) collective-permute-start(bf16[528,128]{1,0:T(8,128)(2,1)S(1)} %shard_map.76), channel_id=1, source_target_pairs={{0,16},{4,20},{8,24},{12,28},{16,0},{20,4},{24,8},{28,12},{1,17},{... | collective-permute-start | bytes 405512 | tf_op jit(solution)/shard_map/ppermute | solution.py:255
  31.3 11.3 %collective-permute-start.6 = (bf16[4,128,128]{2,1,0:T(8,128)(2,1)S(1)}, bf16[4,128,128]{2,1,0:T(8,128)(2,1)S(1)}, u32[]{:S(2)}, u32[]{:S(2)}) collective-permute-start(bf16[4,128,128]{2,1,0:T(8,128)(2,1)S(1)} %get-tuple-element.40), channel_id=1, source_target_pairs={{0,4},{4,0},{8,12},{12,8},{16,20},{20,16},{24,28},{28,24},{1,5},{5... | collective-permute-start | bytes 393224 | tf_op jit(solution)/shard_map/ppermute | solution.py:255
  32.5 0.7 %copy-start.3 = (f32[8,128]{1,0:T(8,128)S(1)}, f32[8,128]{1,0:T(8,128)}, u32[]{:S(2)}) copy-start(f32[8,128]{1,0:T(8,128)} %ridge_ref.1) | copy-start | bytes 12292
  42.7 3.6 %copy-start.1 = (bf16[64,4096]{1,0:T(8,128)(2,1)S(1)}, bf16[64,4096]{1,0:T(8,128)(2,1)}, u32[]{:S(2)}) copy-start(bf16[64,4096]{1,0:T(8,128)(2,1)} %logit_ref.1) | copy-start | bytes 1572868
  42.7 3.5 %copy-start.2 = (f32[4096]{0:T(1024)S(1)}, f32[4096]{0:T(1024)}, u32[]{:S(2)}) copy-start(f32[4096]{0:T(1024)} %param.12) | copy-start | bytes 49156
  44.3 2.1 %collective-permute-start.7 = (bf16[64,1024]{1,0:T(8,128)(2,1)S(1)}, bf16[64,1024]{1,0:T(8,128)(2,1)S(1)}, u32[]{:S(2)}, u32[]{:S(2)}) collective-permute-start(bf16[64,1024]{1,0:T(8,128)(2,1)S(1)} %get-tuple-element.42), channel_id=1, source_target_pairs={{0,1},{1,0},{2,3},{3,2},{4,5},{5,4},{6,7},{7,6},{8,9},{9,8},{10,11... | collective-permute-start | bytes 393224 | tf_op jit(solution)/shard_map/ppermute | solution.py:255
  44.4 6.4 %collective-permute-start.8 = (bf16[64,1024]{1,0:T(8,128)(2,1)S(1)}, bf16[64,1024]{1,0:T(8,128)(2,1)S(1)}, u32[]{:S(2)}, u32[]{:S(2)}) collective-permute-start(bf16[64,1024]{1,0:T(8,128)(2,1)S(1)} %get-tuple-element.43), channel_id=1, source_target_pairs={{0,2},{1,3},{2,0},{3,1},{4,6},{5,7},{6,4},{7,5},{8,10},{9,11},{10,... | collective-permute-start | bytes 393224 | tf_op jit(solution)/shard_map/ppermute | solution.py:255
  46.0 6.6 %collective-permute-start.9 = (bf16[64,1024]{1,0:T(8,128)(2,1)S(1)}, bf16[64,1024]{1,0:T(8,128)(2,1)S(1)}, u32[]{:S(2)}, u32[]{:S(2)}) collective-permute-start(bf16[64,1024]{1,0:T(8,128)(2,1)S(1)} %get-tuple-element.44), channel_id=1, source_target_pairs={{0,3},{1,2},{2,1},{3,0},{4,7},{5,6},{6,5},{7,4},{8,11},{9,10},{10,... | collective-permute-start | bytes 393224 | tf_op jit(solution)/shard_map/ppermute | solution.py:255

commit v5 on v4

--- a/solution.py
+++ b/solution.py
@@ -9,7 +9,7 @@
 
 
 ITERS = 8
-FIRST = 4
+FIRST = 5
 EPS = 1e-06
 
 F32 = jnp.float32
@@ -41,19 +41,17 @@
 def key_state_kernel(width, k_hbm, v_hbm, gate_hbm, kk_ref, kt_ref, k_ref, v_ref, scale_ref, gate_ref, sems):
     heads = gate_ref.shape[0]
     half = width // 2
-    loads = [pltpu.make_async_copy(gate_hbm, gate_ref, sems.at[heads])]
-    for h in range(heads):
-        cols = slice(h * width, (h + 1) * width)
-        loads.append(pltpu.make_async_copy(k_hbm.at[:, cols], k_ref.at[:, cols], sems.at[h]))
-    loads.append(pltpu.make_async_copy(v_hbm, v_ref, sems.at[heads + 1]))
+    loads = [pltpu.make_async_copy(gate_hbm, gate_ref, sems.at[0])]
+    loads.append(pltpu.make_async_copy(k_hbm, k_ref, sems.at[1]))
+    loads.append(pltpu.make_async_copy(v_hbm, v_ref, sems.at[2]))
     for load in loads:
         load.start()
     row = lax.broadcasted_iota(jnp.int32, (half, width), 0)
     col = lax.broadcasted_iota(jnp.int32, (half, width), 1)
     loads[0].wait()
+    loads[1].wait()
     diags = []
     for h in range(heads):
-        loads[1 + h].wait()
         key = k_ref[:, h * width : (h + 1) * width]
         turned = key.T.astype(F32)
         total = square_sum(turned, 0) + EPS
@@ -67,7 +65,7 @@
         packed = jnp.where(row > col, other, jnp.where(row == col, 0.0, kk[:half]))
         kk_ref[h * half : (h + 1) * half] = packed.astype(BF16)
     store_diag(kk_ref, heads * half, jnp.concatenate(diags, axis=0))
-    loads[-1].wait()
+    loads[2].wait()
 
 
 def store_diag(ref, at, diag):
@@ -115,10 +113,26 @@
         give_ref[h] = jnp.where(later, pair[0], pair[1]).astype(BF16)
 
 
-def prepare_kernel(width, q_ref, qt_ref):
+def causal(k_ref, low, h):
+    width, toks = low.shape
+    half = toks // 2
+    score = dot(k_ref[:, h * width : (h + 1) * width], low).astype(BF16)
+    keep = lax.broadcasted_iota(jnp.int32, (half, half), 0) <= lax.broadcasted_iota(
+        jnp.int32, (half, half), 1
+    )
+    none = jnp.zeros((half, half), BF16)
+    upper = jnp.concatenate([jnp.where(keep, score[:half, :half], none), score[:half, half:]], axis=1)
+    lower = jnp.concatenate([none, jnp.where(keep, score[half:, half:], none)], axis=1)
+    return [upper, lower]
+
+
+def prepare_kernel(width, q_ref, k_ref, kt_ref, qt_ref, local_ref):
     for h in range(qt_ref.shape[0]):
         query = q_ref[:, h * width : (h + 1) * width].T.astype(F32)
-        qt_ref[h] = query * lax.rsqrt(square_sum(query, 0) + EPS)
+        query = query * lax.rsqrt(square_sum(query, 0) + EPS)
+        qt_ref[h] = query
+        scores = jnp.concatenate(causal(k_ref, query.astype(BF16), h), axis=0)
+        local_ref[h] = dot(kt_ref[h], scores)
 
 
 def gate_kernel(gain_ref, logit_ref, out_ref):
@@ -133,25 +147,20 @@
     return total
 
 
-def operator(k_ref, lhs, directions, h):
-    _, width, toks = directions.shape
-    half = toks // 2
+def operator(k_ref, kt_ref, mat_ref, directions, h):
     low = directions[h].astype(BF16)
-    score = dot(k_ref[:, h * width : (h + 1) * width], low).astype(BF16)
-    keep = lax.broadcasted_iota(jnp.int32, (half, half), 0) <= lax.broadcasted_iota(
-        jnp.int32, (half, half), 1
-    )
-    none = jnp.zeros((half, half), BF16)
-    upper = jnp.concatenate([jnp.where(keep, score[:half, :half], none), score[:half, half:]], axis=1)
-    lower = jnp.concatenate([none, jnp.where(keep, score[half:, half:], none)], axis=1)
-    return dot(lhs[h], jnp.concatenate([low, upper, lower], axis=0))
-
-
-def sweep(k_ref, lhs, ridges, old, new, norms):
+    both = jnp.concatenate([mat_ref[h], kt_ref[h]], axis=1)
+    return dot(both, jnp.concatenate([low] + causal(k_ref, low, h), axis=0))
+
+
+def sweep(k_ref, kt_ref, mat_ref, ridges, old, new, norms, local=None):
     after = []
     width, toks = old[0].shape[1:]
-    for h in range(lhs.shape[0]):
-        image = operator(k_ref, lhs, old[1], h)
+    for h in range(mat_ref.shape[0]):
+        if local is None:
+            image = operator(k_ref, kt_ref, mat_ref, old[1], h)
+        else:
+            image = local[h] + dot(mat_ref[h], old[1][h].astype(BF16))
         parts = []
         for c in range(0, toks, width):
             at = slice(c, c + width)
@@ -170,9 +179,9 @@
     return tuple(after)
 
 
-def cg_first_kernel(width, rounds, sweeps, k_ref, kt_ref, qt_ref, ridge_ref, *refs):
+def cg_first_kernel(width, rounds, sweeps, k_ref, kt_ref, qt_ref, local_ref, ridge_ref, *refs):
     totals = refs[:rounds]
-    lhs, ridges, norm_ref, *state = refs[rounds:]
+    mat_ref, ridges, norm_ref, *state = refs[rounds:]
     heads, _, _ = qt_ref.shape
     part = width // 2
     inner = lax.broadcasted_iota(jnp.int32, (part, part), 0) < lax.broadcasted_iota(
@@ -186,32 +195,31 @@
         turned = upper.T
         tri = upper[:, :part]
         tri_t = turned[:part]
-        lhs[h, :part, :width] = jnp.concatenate(
+        mat_ref[h, :part] = jnp.concatenate(
             [jnp.where(inner, tri, tri_t), upper[:, part:]], axis=1
         ).astype(BF16)
-        lhs[h, part:, :width] = jnp.concatenate(
+        mat_ref[h, part:] = jnp.concatenate(
             [turned[part:], jnp.where(inner, tri_t, tri)], axis=1
         ).astype(BF16)
-        lhs[h, :, width:] = kt_ref[h]
         ridges[h] = jnp.broadcast_to(ridge_t[:, h : h + 1], (width, width))
         norms.append(square_sum(qt_ref[h], 0))
-    fixed = (k_ref, lhs, ridges)
-    norms = sweep(*fixed, (qt_ref, qt_ref, None), state, norms)
+    fixed = (k_ref, kt_ref, mat_ref, ridges)
+    norms = sweep(*fixed, (qt_ref, qt_ref, None), state, norms, local_ref)
     norms = lax.fori_loop(1, sweeps, lambda _, now: sweep(*fixed, state, state, now), norms)
     norm_ref[...] = jnp.concatenate(norms, axis=0)
 
 
-def cg_last_kernel(width, sweeps, k_ref, lhs, ridges, norm_ref, *refs):
+def cg_last_kernel(width, sweeps, k_ref, kt_ref, mat_ref, ridges, norm_ref, *refs):
     given, x_ref, state = refs[:3], refs[3], refs[4:]
-    heads = lhs.shape[0]
-    fixed = (k_ref, lhs, ridges)
+    heads = mat_ref.shape[0]
+    fixed = (k_ref, kt_ref, mat_ref, ridges)
     norms = tuple(norm_ref[h : h + 1] for h in range(heads))
     norms = sweep(*fixed, given, state, norms)
     norms = lax.fori_loop(1, sweeps, lambda _, now: sweep(*fixed, state, state, now), norms)
     for h in range(heads):
         direction = state[1][h]
         ridge = jnp.concatenate([ridges[h]] * (direction.shape[1] // width), axis=1)
-        image = operator(k_ref, lhs, state[1], h) + ridge * direction
+        image = operator(k_ref, kt_ref, mat_ref, state[1], h) + ridge * direction
         alpha = norms[h] / jnp.sum(direction * image, axis=0, keepdims=True)
         x = state[2][h] + alpha * direction
         x_ref[:, h * width : (h + 1) * width] = x.astype(BF16).T
@@ -281,7 +289,7 @@
             shape(heads, toks, dtype=F32),
         ],
         [pl.BlockSpec(memory_space=pltpu.MemorySpace.HBM)] * 3,
-        [pltpu.VMEM((heads, toks), F32), pltpu.SemaphoreType.DMA((heads + 2,))],
+        [pltpu.VMEM((heads, toks), F32), pltpu.SemaphoreType.DMA((3,))],
         flops=work,
     )(
         *(
@@ -295,13 +303,13 @@
         [VMEM] * 3,
         flops=work,
     )(keys, vals, scales)
-    qt = call(
+    qt, local = call(
         functools.partial(prepare_kernel, width),
-        shape(heads, width, toks, dtype=F32),
-        [VMEM],
+        [shape(heads, width, toks, dtype=F32)] * 2,
+        [VMEM] * 3,
         mib=4,
         flops=work,
-    )(queries)
+    )(queries, keys, kt)
     gated = call(gate_kernel, shape(*gate_logits.shape, dtype=F32), [VMEM] * 2, flops=work)(
         norm_gain[None, :], gate_logits
     )
@@ -327,26 +335,26 @@
     )(keep, near, *value_in)
     far = swap(share, "seq", size, 1)
 
-    lhs, ridges, norms, *state = call(
+    mat, ridges, norms, *state = call(
         functools.partial(cg_first_kernel, width, rounds, FIRST),
         [
-            shape(heads, width, width + toks),
+            shape(heads, width, width),
             shape(heads, width, width, dtype=F32),
             shape(heads, toks, dtype=F32),
         ]
         + [shape(heads, width, toks, dtype=F32)] * 3,
-        [VMEM] * (4 + rounds),
+        [VMEM] * (5 + rounds),
         mib=4,
         flops=10 * work,
-    )(keys, kt, qt, ridge_diag, *key_in)
+    )(keys, kt, qt, local, ridge_diag, *key_in)
     x = call(
         functools.partial(cg_last_kernel, width, ITERS - 1 - FIRST),
         shape(toks, cols),
-        [VMEM] * 7,
+        [VMEM] * 8,
         [pltpu.VMEM((heads, width, toks), F32)] * 3,
         mib=8,
         flops=10 * work,
-    )(keys, lhs, ridges, norms, *state)
+    )(keys, kt, mat, ridges, norms, *state)
 
     pieces = call(
         functools.partial(read_kernel, width, spots),

time: 53.8 us -> 52 us (0.967)
  Pallas kernels: 17.4 us -> 16 us
    pallas_call x1, Pallas kernels: 3.48 us -> 1.58 us  [shards(): call(functools.partial(key_state_kernel, width), [shape(packed, width), s...]
    pallas_call x1, Pallas kernels: 4.32 us -> 2.49 us  [shards(): call(functools.partial(cg_last_kernel, width, ITERS - 1 - FIRST), shape(t...]
    pallas_call x1, Pallas kernels: 0.25 us -> 1.95 us  [shards(): call(functools.partial(prepare_kernel, width), [shape(heads, width, toks,...]
    pallas_call x1, Pallas kernels: 5.18 us -> 5.81 us  [shards(): call(functools.partial(cg_first_kernel, width, rounds, FIRST), [shape(hea...]
  transfers between devices with their start and end apart: 10 -> 10, of which waited for: 7 -> 6; matrix products, arithmetic and copies ran while one was open for 0% -> 0% of each run, Pallas kernels for 21% -> 23%
where the time goes in v5:
time: 52 us; the launch traced here: 51.8 us
  waiting for transfers between devices  22.5 us (43%)
  Pallas kernels  16 us (31%)
  starting transfers between devices  13.1 us (25%)
    ppermute x10, waiting for transfers between devices, swap(): return lax.ppermute(x, axis, [(i, i ^ step) for i in range(size)])  22.5 us
    ppermute x10, starting transfers between devices, swap(): return lax.ppermute(x, axis, [(i, i ^ step) for i in range(size)])  13.1 us
    pallas_call x1, Pallas kernels, shards(): call(functools.partial(cg_first_kernel, width, rounds, FIRST), [shape(hea...  5.81 us
    pallas_call x1, Pallas kernels, shards(): call(functools.partial(cg_last_kernel, width, ITERS - 1 - FIRST), shape(t...  2.49 us
    pallas_call x1, Pallas kernels, shards(): call(functools.partial(prepare_kernel, width), [shape(heads, width, toks,...  1.95 us
    pallas_call x1, Pallas kernels, shards(): call(functools.partial(read_kernel, width, spots), [shape(rows, cols)] *...  1.6 us
    pallas_call x1, Pallas kernels, shards(): call(functools.partial(key_state_kernel, width), [shape(packed, width), s...  1.58 us
    pallas_call x1, Pallas kernels, shards(): call(functools.partial(value_state_kernel, width), [shape(toks, cols)] +...  1.1 us
  transfers between devices with their start and end apart: 10, of which 6 were waited for; matrix products, arithmetic and copies ran while one was open for 0% of the time, Pallas kernels for 23%

profile of v5, /device:TPU:0, one launch (start us, length us, event | category | flops | bytes accessed | tf_op | source)
XLA Modules:
  0.0 51.8 jit_solution(8622534648378064830)
XLA Ops:
  0.0 1.6 %shard_map.73 = (bf16[528,128]{1,0:T(8,128)(2,1)S(1)}, bf16[8,128,256]{2,1,0:T(8,128)(2,1)S(1)}, bf16[256,1024]{1,0:T(8,128)(2,1)S(1)}, bf16[256,1024]{1,0:T(8,128)(2,1)S(1)}, f32[8,256]{1,0:T(8,128)S(1)}) custom-call(bf16[256,1024]{1,0:T(8,128)(2,1)} %k_hbm.1, bf16[256,1024]{1,0:T(8,128)(2,1)} %v_hbm.1, f32[8,256]{1,0:T(8,128)} %bitcast.3), custom_call_target="tpu_custom_call" | custom-call | flops 67108864 | bytes 1048576 | tf_op jit(solution)/shard_map/pallas_call | solution.py:282
  1.6 3.0 %collective-permute-start = (bf16[528,128]{1,0:T(8,128)(2,1)S(1)}, bf16[528,128]{1,0:T(8,128)(2,1)S(1)}, u32[]{:S(2)}, u32[]{:S(2)}) collective-permute-start(bf16[528,128]{1,0:T(8,128)(2,1)S(1)} %get-tuple-element.31.mine_ref), channel_id=1, source_target_pairs={{0,4},{4,0},{8,12},{12,8},{16,20},{20,16},{24,28},{28,24},{1,5},{5... | collective-permute-start | bytes 405512 | tf_op jit(solution)/shard_map/ppermute | solution.py:263
  4.6 1.1 %shard_map.79 = (bf16[256,1024]{1,0:T(8,128)(2,1)S(1)}, bf16[4,128,128]{2,1,0:T(8,128)(2,1)S(1)}, bf16[4,128,128]{2,1,0:T(8,128)(2,1)S(1)}) custom-call(bf16[256,1024]{1,0:T(8,128)(2,1)S(1)} %get-tuple-element.27.k_ref, bf16[256,1024]{1,0:T(8,128)(2,1)S(1)} %get-tuple-element.38.v_ref, f32[8,256]{1,0:T(8,128)S(1)} %get-tuple-element.39.scale_ref), custom_call_target="tpu_custom_call" | custom-call | flops 67108864 | bytes 1048576 | tf_op jit(solution)/shard_map/pallas_call | solution.py:300
  5.7 0.1 collective-permute-start.3
  5.8 2.8 %collective-permute-done.other_ref.refs_0_ = bf16[528,128]{1,0:T(8,128)(2,1)S(1)} collective-permute-done((bf16[528,128]{1,0:T(8,128)(2,1)S(1)}, bf16[528,128]{1,0:T(8,128)(2,1)S(1)}, u32[]{:S(2)}, u32[]{:S(2)}) %collective-permute-start) | collective-permute-done | bytes 135200 | tf_op jit(solution)/shard_map/ppermute | solution.py:263
  8.6 2.0 %collective-permute-start.1 = (bf16[528,128]{1,0:T(8,128)(2,1)S(1)}, bf16[528,128]{1,0:T(8,128)(2,1)S(1)}, u32[]{:S(2)}, u32[]{:S(2)}) collective-permute-start(bf16[528,128]{1,0:T(8,128)(2,1)S(1)} %shard_map.75.mine_ref), channel_id=1, source_target_pairs={{0,8},{4,12},{8,0},{12,4},{16,24},{20,28},{24,16},{28,20},{1,9},{5... | collective-permute-start | bytes 405512 | tf_op jit(solution)/shard_map/ppermute | solution.py:263
  10.6 0.4 collective-permute-done.3.other_ref.near_ref
  11.1 1.9 %collective-permute-start.4 = (bf16[4,128,128]{2,1,0:T(8,128)(2,1)S(1)}, bf16[4,128,128]{2,1,0:T(8,128)(2,1)S(1)}, u32[]{:S(2)}, u32[]{:S(2)}) collective-permute-start(bf16[4,128,128]{2,1,0:T(8,128)(2,1)S(1)} %shard_map.80.mine_ref), channel_id=1, source_target_pairs={{0,8},{4,12},{8,0},{12,4},{16,24},{20,28},{24,16},{28,20},{1,9},{5... | collective-permute-start | bytes 393224 | tf_op jit(solution)/shard_map/ppermute | solution.py:263
  12.9 3.6 %collective-permute-done.4.other_ref.refs_0_ = bf16[4,128,128]{2,1,0:T(8,128)(2,1)S(1)} collective-permute-done((bf16[4,128,128]{2,1,0:T(8,128)(2,1)S(1)}, bf16[4,128,128]{2,1,0:T(8,128)(2,1)S(1)}, u32[]{:S(2)}, u32[]{:S(2)}) %collective-permute-start.4) | collective-permute-done | bytes 131104 | tf_op jit(solution)/shard_map/ppermute | solution.py:263
  16.6 0.0 copy-start
  16.6 3.0 %collective-permute-start.5 = (bf16[4,128,128]{2,1,0:T(8,128)(2,1)S(1)}, bf16[4,128,128]{2,1,0:T(8,128)(2,1)S(1)}, u32[]{:S(2)}, u32[]{:S(2)}) collective-permute-start(bf16[4,128,128]{2,1,0:T(8,128)(2,1)S(1)} %shard_map.81), channel_id=1, source_target_pairs={{0,16},{4,20},{8,24},{12,28},{16,0},{20,4},{24,8},{28,12},{1,17},{... | collective-permute-start | bytes 393224 | tf_op jit(solution)/shard_map/ppermute | solution.py:263
  19.6 0.0 collective-permute-done.1.other_ref.refs_1_
  19.6 0.1 collective-permute-start.2
  19.7 9.6 %collective-permute-done.5.refs_1_ = bf16[4,128,128]{2,1,0:T(8,128)(2,1)S(1)} collective-permute-done((bf16[4,128,128]{2,1,0:T(8,128)(2,1)S(1)}, bf16[4,128,128]{2,1,0:T(8,128)(2,1)S(1)}, u32[]{:S(2)}, u32[]{:S(2)}) %collective-permute-start.5) | collective-permute-done | bytes 131104 | tf_op jit(solution)/shard_map/ppermute | solution.py:263
  29.3 0.1 shard_map.82
  29.4 1.1 %collective-permute-start.6 = (bf16[4,128,128]{2,1,0:T(8,128)(2,1)S(1)}, bf16[4,128,128]{2,1,0:T(8,128)(2,1)S(1)}, u32[]{:S(2)}, u32[]{:S(2)}) collective-permute-start(bf16[4,128,128]{2,1,0:T(8,128)(2,1)S(1)} %get-tuple-element.44), channel_id=1, source_target_pairs={{0,4},{4,0},{8,12},{12,8},{16,20},{20,16},{24,28},{28,24},{1,5},{5... | collective-permute-start | bytes 393224 | tf_op jit(solution)/shard_map/ppermute | solution.py:263
  30.5 0.0 copy-done
  30.6 0.0 copy-start.3
  30.6 2.0 %shard_map.74 = (f32[8,128,256]{2,1,0:T(8,128)S(1)}, f32[8,128,256]{2,1,0:T(8,128)S(1)}) custom-call(bf16[256,1024]{1,0:T(8,128)(2,1)S(1)} %copy-done, bf16[256,1024]{1,0:T(8,128)(2,1)S(1)} %get-tuple-element.27.k_ref, bf16[8,128,256]{2,1,0:T(8,128)(2,1)S(1)} %get-tuple-element.28.kt_ref), custom_call_target="tpu_custom_call" | custom-call | flops 67108864 | bytes 1048576 | tf_op jit(solution)/shard_map/pallas_call | solution.py:306
  32.5 0.0 collective-permute-done.2.refs_2_
  32.5 0.0 copy-done.3
  32.5 5.8 %shard_map.77 = (bf16[8,128,128]{2,1,0:T(8,128)(2,1)S(1)}, f32[8,128,128]{2,1,0:T(8,128)S(1)}, f32[8,256]{1,0:T(8,128)S(1)}, f32[8,128,256]{2,1,0:T(8,128)S(1)},...) custom-call(bf16[256,1024]{1,0:T(8,128)(2,1)S(1)} %get-tuple-element.27.k_ref, ...), custom_call_target="tpu_custom_call" | custom-call | flops 671088640 | bytes 1048576 | tf_op jit(solution)/shard_map/pallas_call | solution.py:338
  38.3 2.5 %shard_map.78.x_ref = bf16[256,1024]{1,0:T(8,128)(2,1)S(1)} custom-call(bf16[256,1024]{1,0:T(8,128)(2,1)S(1)} %get-tuple-element.27.k_ref, bf16[8,128,256]{2,1,0:T(8,128)(2,1)S(1)} %get-tuple-element.28.kt_ref, bf16[8,128,128]{2,1,0:T(8,128)(2,1)S(1)} %get-tuple-element.32.mat_ref, f32[8,128,128]{2,1,0:T(8,128)S(1)} %get-tuple-element.33.ridges, ...), custom_call_target="tpu_custom_call" | custom-call | flops 671088640 | bytes 1048576 | tf_op jit(solution)/shard_map/pallas_call | solution.py:350
  40.8 0.0 collective-permute-done.6.far_ref
  40.9 0.0 copy-start.1
  40.9 0.0 copy-start.2
  40.9 1.6 %shard_map.83 = (bf16[64,1024]{1,0:T(8,128)(2,1)S(1)}, bf16[64,1024]{1,0:T(8,128)(2,1)S(1)}, bf16[64,1024]{1,0:T(8,128)(2,1)S(1)}, bf16[64,1024]{1,0:T(8,128)(2,1)S(1)}) custom-call(bf16[256,1024]{1,0:T(8,128)(2,1)S(1)} %shard_map.78.x_ref, bf16[256,1024]{1,0:T(8,128)(2,1)S(1)} %get-tuple-element.27.k_ref, bf16[256,1024]{1,0:T(8,128)(2,1)S(1)} %get-tuple-element.40.val_ref, ...), custom_call_target="tpu_custom_call" | custom-call | flops 67108864 | bytes 1048576 | tf_op jit(solution)/shard_map/pallas_call | solution.py:359
  42.5 0.1 collective-permute-start.7
  42.6 1.6 %collective-permute-start.8 = (bf16[64,1024]{1,0:T(8,128)(2,1)S(1)}, bf16[64,1024]{1,0:T(8,128)(2,1)S(1)}, u32[]{:S(2)}, u32[]{:S(2)}) collective-permute-start(bf16[64,1024]{1,0:T(8,128)(2,1)S(1)} %get-tuple-element.47), channel_id=1, source_target_pairs={{0,2},{1,3},{2,0},{3,1},{4,6},{5,7},{6,4},{7,5},{8,10},{9,11},{10,... | collective-permute-start | bytes 393224 | tf_op jit(solution)/shard_map/ppermute | solution.py:263
  44.2 0.3 collective-permute-start.9
  44.4 0.0 copy-done.1
  44.4 0.0 copy-done.2
  44.4 0.1 shard_map.84.refs_4_
  44.6 0.0 collective-permute-done.7.refs_1_
  44.6 4.4 %collective-permute-done.8.refs_2_ = bf16[64,1024]{1,0:T(8,128)(2,1)S(1)} collective-permute-done((bf16[64,1024]{1,0:T(8,128)(2,1)S(1)}, bf16[64,1024]{1,0:T(8,128)(2,1)S(1)}, u32[]{:S(2)}, u32[]{:S(2)}) %collective-permute-start.8) | collective-permute-done | bytes 131104 | tf_op jit(solution)/shard_map/ppermute | solution.py:263
  49.0 1.7 %collective-permute-done.9.refs_3_ = bf16[64,1024]{1,0:T(8,128)(2,1)S(1)} collective-permute-done((bf16[64,1024]{1,0:T(8,128)(2,1)S(1)}, bf16[64,1024]{1,0:T(8,128)(2,1)S(1)}, u32[]{:S(2)}, u32[]{:S(2)}) %collective-permute-start.9) | collective-permute-done | bytes 131104 | tf_op jit(solution)/shard_map/ppermute | solution.py:263
  50.7 1.1 %shard_map.85 = bf16[64,4096]{1,0:T(8,128)(2,1)} custom-call(bf16[64,1024]{1,0:T(8,128)(2,1)S(1)} %get-tuple-element.45.refs_0_, bf16[64,1024]{1,0:T(8,128)(2,1)S(1)} %collective-permute-done.7.refs_1_, bf16[64,1024]{1,0:T(8,128)(2,1)S(1)} %collective-permute-done.8.refs_2_, bf16[64,1024]{1,0:T(8,128)(2,1)S(1)} %collective-permute-done.9.refs_3_, ...), custom_call_target="tpu_custom_call" | custom-call | flops 67108864 | bytes 1048576 | tf_op jit(solution)/shard_map/pallas_call | solution.py:367
  (4 shorter events, 0.1 us)
Async XLA Ops:
  1.6 7.0 %collective-permute-start = (bf16[528,128]{1,0:T(8,128)(2,1)S(1)}, bf16[528,128]{1,0:T(8,128)(2,1)S(1)}, u32[]{:S(2)}, u32[]{:S(2)}) collective-permute-start(bf16[528,128]{1,0:T(8,128)(2,1)S(1)} %get-tuple-element.31.mine_ref), channel_id=1, source_target_pairs={{0,4},{4,0},{8,12},{12,8},{16,20},{20,16},{24,28},{28,24},{1,5},{5... | collective-permute-start | bytes 405512 | tf_op jit(solution)/shard_map/ppermute | solution.py:263
  5.7 5.3 %collective-permute-start.3 = (bf16[4,128,128]{2,1,0:T(8,128)(2,1)S(1)}, bf16[4,128,128]{2,1,0:T(8,128)(2,1)S(1)}, u32[]{:S(2)}, u32[]{:S(2)}) collective-permute-start(bf16[4,128,128]{2,1,0:T(8,128)(2,1)S(1)} %get-tuple-element.42), channel_id=1, source_target_pairs={{0,4},{4,0},{8,12},{12,8},{16,20},{20,16},{24,28},{28,24},{1,5},{5... | collective-permute-start | bytes 393224 | tf_op jit(solution)/shard_map/ppermute | solution.py:263
  8.6 10.9 %collective-permute-start.1 = (bf16[528,128]{1,0:T(8,128)(2,1)S(1)}, bf16[528,128]{1,0:T(8,128)(2,1)S(1)}, u32[]{:S(2)}, u32[]{:S(2)}) collective-permute-start(bf16[528,128]{1,0:T(8,128)(2,1)S(1)} %shard_map.75.mine_ref), channel_id=1, source_target_pairs={{0,8},{4,12},{8,0},{12,4},{16,24},{20,28},{24,16},{28,20},{1,9},{5... | collective-permute-start | bytes 405512 | tf_op jit(solution)/shard_map/ppermute | solution.py:263
  11.1 5.5 %collective-permute-start.4 = (bf16[4,128,128]{2,1,0:T(8,128)(2,1)S(1)}, bf16[4,128,128]{2,1,0:T(8,128)(2,1)S(1)}, u32[]{:S(2)}, u32[]{:S(2)}) collective-permute-start(bf16[4,128,128]{2,1,0:T(8,128)(2,1)S(1)} %shard_map.80.mine_ref), channel_id=1, source_target_pairs={{0,8},{4,12},{8,0},{12,4},{16,24},{20,28},{24,16},{28,20},{1,9},{5... | collective-permute-start | bytes 393224 | tf_op jit(solution)/shard_map/ppermute | solution.py:263
  16.6 14.0 %copy-start = (bf16[256,1024]{1,0:T(8,128)(2,1)S(1)}, bf16[256,1024]{1,0:T(8,128)(2,1)}, u32[]{:S(2)}) copy-start(bf16[256,1024]{1,0:T(8,128)(2,1)} %q_ref.1) | copy-start | bytes 1572868
  16.6 12.7 %collective-permute-start.5 = (bf16[4,128,128]{2,1,0:T(8,128)(2,1)S(1)}, bf16[4,128,128]{2,1,0:T(8,128)(2,1)S(1)}, u32[]{:S(2)}, u32[]{:S(2)}) collective-permute-start(bf16[4,128,128]{2,1,0:T(8,128)(2,1)S(1)} %shard_map.81), channel_id=1, source_target_pairs={{0,16},{4,20},{8,24},{12,28},{16,0},{20,4},{24,8},{28,12},{1,17},{... | collective-permute-start | bytes 393224 | tf_op jit(solution)/shard_map/ppermute | solution.py:263
  19.6 12.9 %collective-permute-start.2 = (bf16[528,128]{1,0:T(8,128)(2,1)S(1)}, bf16[528,128]{1,0:T(8,128)(2,1)S(1)}, u32[]{:S(2)}, u32[]{:S(2)}) collective-permute-start(bf16[528,128]{1,0:T(8,128)(2,1)S(1)} %shard_map.76), channel_id=1, source_target_pairs={{0,16},{4,20},{8,24},{12,28},{16,0},{20,4},{24,8},{28,12},{1,17},{... | collective-permute-start | bytes 405512 | tf_op jit(solution)/shard_map/ppermute | solution.py:263
  29.4 11.4 %collective-permute-start.6 = (bf16[4,128,128]{2,1,0:T(8,128)(2,1)S(1)}, bf16[4,128,128]{2,1,0:T(8,128)(2,1)S(1)}, u32[]{:S(2)}, u32[]{:S(2)}) collective-permute-start(bf16[4,128,128]{2,1,0:T(8,128)(2,1)S(1)} %get-tuple-element.44), channel_id=1, source_target_pairs={{0,4},{4,0},{8,12},{12,8},{16,20},{20,16},{24,28},{28,24},{1,5},{5... | collective-permute-start | bytes 393224 | tf_op jit(solution)/shard_map/ppermute | solution.py:263
  30.6 2.0 %copy-start.3 = (f32[8,128]{1,0:T(8,128)S(1)}, f32[8,128]{1,0:T(8,128)}, u32[]{:S(2)}) copy-start(f32[8,128]{1,0:T(8,128)} %ridge_ref.1) | copy-start | bytes 12292
  40.9 3.6 %copy-start.1 = (bf16[64,4096]{1,0:T(8,128)(2,1)S(1)}, bf16[64,4096]{1,0:T(8,128)(2,1)}, u32[]{:S(2)}) copy-start(bf16[64,4096]{1,0:T(8,128)(2,1)} %logit_ref.1) | copy-start | bytes 1572868
  40.9 3.6 %copy-start.2 = (f32[4096]{0:T(1024)S(1)}, f32[4096]{0:T(1024)}, u32[]{:S(2)}) copy-start(f32[4096]{0:T(1024)} %param.12) | copy-start | bytes 49156
  42.5 2.1 %collective-permute-start.7 = (bf16[64,1024]{1,0:T(8,128)(2,1)S(1)}, bf16[64,1024]{1,0:T(8,128)(2,1)S(1)}, u32[]{:S(2)}, u32[]{:S(2)}) collective-permute-start(bf16[64,1024]{1,0:T(8,128)(2,1)S(1)} %get-tuple-element.46), channel_id=1, source_target_pairs={{0,1},{1,0},{2,3},{3,2},{4,5},{5,4},{6,7},{7,6},{8,9},{9,8},{10,11... | collective-permute-start | bytes 393224 | tf_op jit(solution)/shard_map/ppermute | solution.py:263
  42.6 6.4 %collective-permute-start.8 = (bf16[64,1024]{1,0:T(8,128)(2,1)S(1)}, bf16[64,1024]{1,0:T(8,128)(2,1)S(1)}, u32[]{:S(2)}, u32[]{:S(2)}) collective-permute-start(bf16[64,1024]{1,0:T(8,128)(2,1)S(1)} %get-tuple-element.47), channel_id=1, source_target_pairs={{0,2},{1,3},{2,0},{3,1},{4,6},{5,7},{6,4},{7,5},{8,10},{9,11},{10,... | collective-permute-start | bytes 393224 | tf_op jit(solution)/shard_map/ppermute | solution.py:263
  44.2 6.6 %collective-permute-start.9 = (bf16[64,1024]{1,0:T(8,128)(2,1)S(1)}, bf16[64,1024]{1,0:T(8,128)(2,1)S(1)}, u32[]{:S(2)}, u32[]{:S(2)}) collective-permute-start(bf16[64,1024]{1,0:T(8,128)(2,1)S(1)} %get-tuple-element.48), channel_id=1, source_target_pairs={{0,3},{1,2},{2,1},{3,0},{4,7},{5,6},{6,5},{7,4},{8,11},{9,10},{10,... | collective-permute-start | bytes 393224 | tf_op jit(solution)/shard_map/ppermute | solution.py:263

commit v6 on v5

--- a/solution.py
+++ b/solution.py
@@ -38,7 +38,7 @@
     return jnp.sum(block * block, axis=axis, keepdims=True)
 
 
-def key_state_kernel(width, k_hbm, v_hbm, gate_hbm, kk_ref, kt_ref, k_ref, v_ref, scale_ref, gate_ref, sems):
+def key_state_kernel(width, k_hbm, v_hbm, gate_hbm, keep_ref, give_ref, kt_ref, k_ref, v_ref, scale_ref, gate_ref, sems):
     heads = gate_ref.shape[0]
     half = width // 2
     loads = [pltpu.make_async_copy(gate_hbm, gate_ref, sems.at[0])]
@@ -50,7 +50,9 @@
     col = lax.broadcasted_iota(jnp.int32, (half, width), 1)
     loads[0].wait()
     loads[1].wait()
-    diags = []
+    later = (lax.axis_index("seq") & 1) == 1
+    count = heads // 2
+    blocks, diags = [], []
     for h in range(heads):
         key = k_ref[:, h * width : (h + 1) * width]
         turned = key.T.astype(F32)
@@ -63,8 +65,14 @@
         diags.append(jnp.sum(diag, axis=0, keepdims=True))
         other = pltpu.roll(kk[half:], half, 1)
         packed = jnp.where(row > col, other, jnp.where(row == col, 0.0, kk[:half]))
-        kk_ref[h * half : (h + 1) * half] = packed.astype(BF16)
-    store_diag(kk_ref, heads * half, jnp.concatenate(diags, axis=0))
+        blocks.append(packed.astype(BF16))
+    for h in range(count):
+        rows = slice(h * half, (h + 1) * half)
+        keep_ref[rows] = jnp.where(later, blocks[count + h], blocks[h])
+        give_ref[rows] = jnp.where(later, blocks[h], blocks[count + h])
+    low, high = jnp.concatenate(diags[:count], axis=0), jnp.concatenate(diags[count:], axis=0)
+    store_diag(keep_ref, count * half, jnp.where(later, high, low))
+    store_diag(give_ref, count * half, jnp.where(later, low, high))
     loads[2].wait()
 
 
@@ -85,6 +93,17 @@
 def key_join_kernel(at, mine_ref, other_ref, total_ref):
     total_ref[:at] = (mine_ref[:at].astype(F32) + other_ref[:at].astype(F32)).astype(BF16)
     store_diag(total_ref, at, load_diag(mine_ref, at) + load_diag(other_ref, at))
+
+
+def key_prefix_kernel(at, keep_ref, near_ref, *refs):
+    later = (lax.axis_index("seq") & 1).astype(F32)
+    for load, store in (
+        (lambda ref: ref[:at].astype(F32), lambda ref, x: ref.__setitem__(slice(0, at), x.astype(BF16))),
+        (lambda ref: load_diag(ref, at), lambda ref, x: store_diag(ref, at, x)),
+    ):
+        before = prefix(refs[:-2], load, 1)
+        store(refs[-2], before + later * load(near_ref))
+        store(refs[-1], before + (1.0 - later) * load(keep_ref))
 
 
 def value_join_kernel(mine_ref, other_ref, total_ref):
@@ -179,19 +198,24 @@
     return tuple(after)
 
 
-def cg_first_kernel(width, rounds, sweeps, k_ref, kt_ref, qt_ref, local_ref, ridge_ref, *refs):
-    totals = refs[:rounds]
-    mat_ref, ridges, norm_ref, *state = refs[rounds:]
+def cg_first_kernel(width, sweeps, k_ref, kt_ref, qt_ref, local_ref, ridge_ref, own_ref, far_ref, *refs):
+    mat_ref, ridges, norm_ref, *state = refs
     heads, _, _ = qt_ref.shape
     part = width // 2
     inner = lax.broadcasted_iota(jnp.int32, (part, part), 0) < lax.broadcasted_iota(
         jnp.int32, (part, part), 1
     )
-    ridge_t = (ridge_ref[...] + prefix(totals, lambda ref: load_diag(ref, heads * part))).T
+    count = heads // 2
+    own_diag, far_diag = load_diag(own_ref, count * part), load_diag(far_ref, count * part)
+    later = (lax.axis_index("seq") & 1) == 1
+    low = jnp.where(later, far_diag, own_diag)
+    high = jnp.where(later, own_diag, far_diag)
+    ridge_t = (ridge_ref[...] + jnp.concatenate([low, high], axis=0)).T
     norms = []
     for h in range(heads):
-        rows = slice(h * part, (h + 1) * part)
-        upper = prefix(totals, lambda ref: ref[rows].astype(F32))
+        rows = slice(h % count * part, (h % count + 1) * part)
+        first, second = (own_ref, far_ref) if h < count else (far_ref, own_ref)
+        upper = jnp.where(later, second[rows], first[rows]).astype(F32)
         turned = upper.T
         tri = upper[:, :part]
         tri_t = turned[:part]
@@ -225,22 +249,27 @@
         x_ref[:, h * width : (h + 1) * width] = x.astype(BF16).T
 
 
-def read_kernel(width, spots, x_ref, k_ref, val_ref, own_ref, far_ref, *refs):
+def local_read_kernel(width, x_ref, k_ref, val_ref, local_ref):
+    toks = k_ref.shape[0]
+    keep = lax.broadcasted_iota(jnp.int32, (toks, toks), 0) >= lax.broadcasted_iota(
+        jnp.int32, (toks, toks), 1
+    )
+    for h in range(k_ref.shape[1] // width):
+        cols = slice(h * width, (h + 1) * width)
+        score = jnp.where(keep, dot(x_ref[:, cols], k_ref[:, cols], ((1,), (1,))), 0.0)
+        local_ref[:, cols] = dot(score.astype(BF16), val_ref[:, cols])
+
+
+def read_kernel(width, spots, x_ref, local_ref, own_ref, far_ref, *refs):
     outs, tmp = refs[:spots], refs[spots]
     count = own_ref.shape[0]
     later = lax.axis_index("seq") & 1
-    toks = k_ref.shape[0]
-    rows = toks // spots
+    rows = x_ref.shape[0] // spots
     me = lax.axis_index("head")
-    keep = lax.broadcasted_iota(jnp.int32, (toks, toks), 0) >= lax.broadcasted_iota(
-        jnp.int32, (toks, toks), 1
-    )
-    for h in range(k_ref.shape[1] // width):
+    for h in range(x_ref.shape[1] // width):
         cols = slice(h * width, (h + 1) * width)
-        x = x_ref[:, cols]
         state = jnp.where(later == h // count, own_ref[h % count], far_ref[h % count])
-        score = jnp.where(keep, dot(x, k_ref[:, cols], ((1,), (1,))), 0.0).astype(BF16)
-        out = dot(x, state, ((1,), (1,))) + dot(score, val_ref[:, cols])
+        out = dot(x_ref[:, cols], state, ((1,), (1,))) + local_ref[:, cols]
         tmp[:, cols] = out.astype(BF16)
     for k in range(spots):
         outs[k][...] = tmp[pl.ds(pl.multiple_of((me ^ k) * rows, rows), rows), :]
@@ -276,12 +305,14 @@
     rounds = size.bit_length() - 1
     rows = toks // spots
     gates = write_gate.T
-    packed = heads * width // 2 + 2 * heads
+    tall = heads // 2 * width // 2
+    packed = tall + heads
     work = 2 * toks * width * width * heads
 
-    kk, kt, keys, vals, scales = call(
+    keep, give, kt, keys, vals, scales = call(
         functools.partial(key_state_kernel, width),
         [
+            shape(packed, width),
             shape(packed, width),
             shape(heads, width, toks),
             shape(toks, cols),
@@ -297,7 +328,7 @@
             for x in (key_rows, values, gates)
         )
     )
-    vals, keep, give = call(
+    vals, value_keep, value_give = call(
         functools.partial(value_state_kernel, width),
         [shape(toks, cols)] + [shape(heads // 2, width, width)] * 2,
         [VMEM] * 3,
@@ -315,16 +346,22 @@
     )
 
     key_in, value_in = [], []
-    for k in range(rounds):
+    near = swap(give, "seq", size, 1)
+    kk = keep
+    for k in range(1, rounds):
+        kk = call(
+            functools.partial(key_join_kernel, tall), shape(packed, width), [VMEM] * 2
+        )(kk, key_in[-1] if key_in else near)
         key_in.append(swap(kk, "seq", size, 1 << k))
-        if k + 1 < rounds:
-            kk = call(
-                functools.partial(key_join_kernel, packed - 2 * heads),
-                shape(packed, width),
-                [VMEM] * 2,
-                mib=4,
-            )(kk, key_in[-1])
-    near = swap(give, "seq", size, 1)
+    key_own, share = call(
+        functools.partial(key_prefix_kernel, tall),
+        [shape(packed, width)] * 2,
+        [VMEM] * (rounds + 1),
+    )(keep, near, *key_in)
+    key_far = swap(share, "seq", size, 1)
+
+    keep = value_keep
+    near = swap(value_give, "seq", size, 1)
     vk = call(value_join_kernel, shape(*keep.shape), [VMEM] * 2)(keep, near)
     for k in range(1, rounds):
         value_in.append(swap(vk, "seq", size, 1 << k))
@@ -336,17 +373,17 @@
     far = swap(share, "seq", size, 1)
 
     mat, ridges, norms, *state = call(
-        functools.partial(cg_first_kernel, width, rounds, FIRST),
+        functools.partial(cg_first_kernel, width, FIRST),
         [
             shape(heads, width, width),
             shape(heads, width, width, dtype=F32),
             shape(heads, toks, dtype=F32),
         ]
         + [shape(heads, width, toks, dtype=F32)] * 3,
-        [VMEM] * (5 + rounds),
+        [VMEM] * 7,
         mib=4,
         flops=10 * work,
-    )(keys, kt, qt, local, ridge_diag, *key_in)
+    )(keys, kt, qt, local, ridge_diag, key_own, key_far)
     x = call(
         functools.partial(cg_last_kernel, width, ITERS - 1 - FIRST),
         shape(toks, cols),
@@ -356,13 +393,19 @@
         flops=10 * work,
     )(keys, kt, mat, ridges, norms, *state)
 
+    local = call(
+        functools.partial(local_read_kernel, width),
+        shape(toks, cols, dtype=F32),
+        [VMEM] * 3,
+        flops=work,
+    )(x, keys, vals)
     pieces = call(
         functools.partial(read_kernel, width, spots),
         [shape(rows, cols)] * spots,
-        [VMEM] * 5,
+        [VMEM] * 4,
         [pltpu.VMEM((toks, cols), BF16)],
         flops=work,
-    )(x, keys, vals, own, far)
+    )(x, local, own, far)
     arrived = [pieces[0]] + [swap(pieces[k], "head", spots, k) for k in range(1, spots)]
     return call(
         functools.partial(norm_kernel, spots),

time: 52 us -> 47.8 us (0.919)
  waiting for transfers between devices: 22.5 us -> 17.7 us
  starting transfers between devices: 13.1 us -> 13.9 us
    ppermute x10 -> x11, waiting for transfers between devices: 22.5 us -> 17.7 us  [swap(): return lax.ppermute(x, axis, [(i, i ^ step) for i in range(size)])]
    pallas_call x1, Pallas kernels: 1.6 us -> 0.37 us  [shards(): call(functools.partial(read_kernel, width, spots), [shape(rows, cols)] *...]
    pallas_call x3 -> x5, Pallas kernels: 5.89 us -> 6.93 us  [the longest x1 5.87 us: shards(): call(functools.partial(cg_first_kernel, width, FIRST), [shape(heads, widt...]
    ppermute x10 -> x11, starting transfers between devices: 13.1 us -> 13.9 us  [swap(): return lax.ppermute(x, axis, [(i, i ^ step) for i in range(size)])]
  transfers between devices with their start and end apart: 10 -> 11, of which waited for: 6 -> 5; matrix products, arithmetic and copies ran while one was open for 0% -> 0% of each run, Pallas kernels for 23% -> 25%
where the time goes in v6:
time: 47.8 us; the launch traced here: 47.6 us
  waiting for transfers between devices  17.7 us (37%)
  Pallas kernels  15.8 us (33%)
  starting transfers between devices  13.9 us (29%)
    ppermute x11, waiting for transfers between devices, swap(): return lax.ppermute(x, axis, [(i, i ^ step) for i in range(size)])  17.7 us
    ppermute x11, starting transfers between devices, swap(): return lax.ppermute(x, axis, [(i, i ^ step) for i in range(size)])  13.9 us
    pallas_call x1, Pallas kernels, shards(): call(functools.partial(cg_first_kernel, width, FIRST), [shape(heads, widt...  5.87 us
    pallas_call x1, Pallas kernels, shards(): call(functools.partial(cg_last_kernel, width, ITERS - 1 - FIRST), shape(t...  2.49 us
    pallas_call x1, Pallas kernels, shards(): call(functools.partial(prepare_kernel, width), [shape(heads, width, toks,...  1.95 us
    pallas_call x1, Pallas kernels, shards(): call(functools.partial(key_state_kernel, width), [shape(packed, width), s...  1.59 us
    pallas_call x1, Pallas kernels, shards(): call(functools.partial(value_state_kernel, width), [shape(toks, cols)] +...  1.11 us
    pallas_call x1, Pallas kernels, shards(): call(functools.partial(norm_kernel, spots), shape(rows, spots * cols), [V...  1.07 us
  transfers between devices with their start and end apart: 11, of which 5 were waited for; matrix products, arithmetic and copies ran while one was open for 0% of the time, Pallas kernels for 25%

profile of v6, /device:TPU:0, one launch (start us, length us, event | category | flops | bytes accessed | tf_op | source)
XLA Modules:
  0.0 47.6 jit_solution(16021543903687569161)
XLA Ops:
  0.0 1.6 %shard_map.73 = (bf16[264,128]{1,0:T(8,128)(2,1)S(1)}, bf16[264,128]{1,0:T(8,128)(2,1)S(1)}, bf16[8,128,256]{2,1,0:T(8,128)(2,1)S(1)}, bf16[256,1024]{1,0:T(8,12...) custom-call(bf16[256,1024]{1,0:T(8,128)(2,1)} %k_hbm.1, bf16[256,1024]{1,0:T(8,128)(2,1)} %v_hbm.1, ...), custom_call_target="tpu_custom_call" | custom-call | flops 67108864 | bytes 1048576 | tf_op jit(solution)/shard_map/pallas_call | solution.py:312
  1.6 1.1 %shard_map.80 = (bf16[256,1024]{1,0:T(8,128)(2,1)S(1)}, bf16[4,128,128]{2,1,0:T(8,128)(2,1)S(1)}, bf16[4,128,128]{2,1,0:T(8,128)(2,1)S(1)}) custom-call(bf16[256,1024]{1,0:T(8,128)(2,1)S(1)} %get-tuple-element.30.k_ref, bf16[256,1024]{1,0:T(8,128)(2,1)S(1)} %get-tuple-element.44.v_ref, f32[8,256]{1,0:T(8,128)S(1)} %get-tuple-element.45.scale_ref), custom_call_target="tpu_custom_call" | custom-call | flops 67108864 | bytes 1048576 | tf_op jit(solution)/shard_map/pallas_call | solution.py:331
  2.7 3.0 %collective-permute-start.4 = (bf16[4,128,128]{2,1,0:T(8,128)(2,1)S(1)}, bf16[4,128,128]{2,1,0:T(8,128)(2,1)S(1)}, u32[]{:S(2)}, u32[]{:S(2)}) collective-permute-start(bf16[4,128,128]{2,1,0:T(8,128)(2,1)S(1)} %get-tuple-element.48), channel_id=1, source_target_pairs={{0,4},{4,0},{8,12},{12,8},{16,20},{20,16},{24,28},{28,24},{1,5},{5... | collective-permute-start | bytes 393224 | tf_op jit(solution)/shard_map/ppermute | solution.py:292
  5.7 0.1 collective-permute-start
  5.8 4.1 %collective-permute-done.4.other_ref.near_ref = bf16[4,128,128]{2,1,0:T(8,128)(2,1)S(1)} collective-permute-done((bf16[4,128,128]{2,1,0:T(8,128)(2,1)S(1)}, bf16[4,128,128]{2,1,0:T(8,128)(2,1)S(1)}, u32[]{:S(2)}, u32[]{:S(2)}) %collective-permute-start.4) | collective-permute-done | bytes 131104 | tf_op jit(solution)/shard_map/ppermute | solution.py:292
  10.0 1.9 %collective-permute-start.5 = (bf16[4,128,128]{2,1,0:T(8,128)(2,1)S(1)}, bf16[4,128,128]{2,1,0:T(8,128)(2,1)S(1)}, u32[]{:S(2)}, u32[]{:S(2)}) collective-permute-start(bf16[4,128,128]{2,1,0:T(8,128)(2,1)S(1)} %shard_map.82.mine_ref), channel_id=1, source_target_pairs={{0,8},{4,12},{8,0},{12,4},{16,24},{20,28},{24,16},{28,20},{1,9},{5... | collective-permute-start | bytes 393224 | tf_op jit(solution)/shard_map/ppermute | solution.py:292
  11.9 0.0 collective-permute-done.other_ref.near_ref
  11.9 0.0 copy-start
  11.9 0.7 %collective-permute-start.1 = (bf16[264,128]{1,0:T(8,128)(2,1)S(1)}, bf16[264,128]{1,0:T(8,128)(2,1)S(1)}, u32[]{:S(2)}, u32[]{:S(2)}) collective-permute-start(bf16[264,128]{1,0:T(8,128)(2,1)S(1)} %shard_map.75.mine_ref), channel_id=1, source_target_pairs={{0,8},{4,12},{8,0},{12,4},{16,24},{20,28},{24,16},{28,20},{1,9},{5... | collective-permute-start | bytes 202760 | tf_op jit(solution)/shard_map/ppermute | solution.py:292
  12.6 3.7 %collective-permute-done.1.other_ref.refs_0_ = bf16[264,128]{1,0:T(8,128)(2,1)S(1)} collective-permute-done((bf16[264,128]{1,0:T(8,128)(2,1)S(1)}, bf16[264,128]{1,0:T(8,128)(2,1)S(1)}, u32[]{:S(2)}, u32[]{:S(2)}) %collective-permute-start.1) | collective-permute-done | bytes 67616 | tf_op jit(solution)/shard_map/ppermute | solution.py:292
  16.3 3.2 %collective-permute-start.2 = (bf16[264,128]{1,0:T(8,128)(2,1)S(1)}, bf16[264,128]{1,0:T(8,128)(2,1)S(1)}, u32[]{:S(2)}, u32[]{:S(2)}) collective-permute-start(bf16[264,128]{1,0:T(8,128)(2,1)S(1)} %shard_map.76), channel_id=1, source_target_pairs={{0,16},{4,20},{8,24},{12,28},{16,0},{20,4},{24,8},{28,12},{1,17},{... | collective-permute-start | bytes 202760 | tf_op jit(solution)/shard_map/ppermute | solution.py:292
  19.5 0.0 collective-permute-done.5.other_ref.refs_0_
  19.6 0.1 collective-permute-start.6
  19.6 3.8 %collective-permute-done.2.refs_1_ = bf16[264,128]{1,0:T(8,128)(2,1)S(1)} collective-permute-done((bf16[264,128]{1,0:T(8,128)(2,1)S(1)}, bf16[264,128]{1,0:T(8,128)(2,1)S(1)}, u32[]{:S(2)}, u32[]{:S(2)}) %collective-permute-start.2) | collective-permute-done | bytes 67616 | tf_op jit(solution)/shard_map/ppermute | solution.py:292
  23.4 0.1 shard_map.77
  23.5 1.6 %collective-permute-start.3 = (bf16[264,128]{1,0:T(8,128)(2,1)S(1)}, bf16[264,128]{1,0:T(8,128)(2,1)S(1)}, u32[]{:S(2)}, u32[]{:S(2)}) collective-permute-start(bf16[264,128]{1,0:T(8,128)(2,1)S(1)} %get-tuple-element.37), channel_id=1, source_target_pairs={{0,4},{4,0},{8,12},{12,8},{16,20},{20,16},{24,28},{28,24},{1,5},{5... | collective-permute-start | bytes 202760 | tf_op jit(solution)/shard_map/ppermute | solution.py:292
  25.0 0.0 copy-done
  25.0 2.0 %shard_map.74 = (f32[8,128,256]{2,1,0:T(8,128)S(1)}, f32[8,128,256]{2,1,0:T(8,128)S(1)}) custom-call(bf16[256,1024]{1,0:T(8,128)(2,1)S(1)} %copy-done, bf16[256,1024]{1,0:T(8,128)(2,1)S(1)} %get-tuple-element.30.k_ref, bf16[8,128,256]{2,1,0:T(8,128)(2,1)S(1)} %get-tuple-element.31.kt_ref), custom_call_target="tpu_custom_call" | custom-call | flops 67108864 | bytes 1048576 | tf_op jit(solution)/shard_map/pallas_call | solution.py:337
  27.0 0.0 collective-permute-done.6.refs_1_
  27.0 0.1 shard_map.84
  27.1 0.0 copy-start.3
  27.1 1.4 %collective-permute-start.7 = (bf16[4,128,128]{2,1,0:T(8,128)(2,1)S(1)}, bf16[4,128,128]{2,1,0:T(8,128)(2,1)S(1)}, u32[]{:S(2)}, u32[]{:S(2)}) collective-permute-start(bf16[4,128,128]{2,1,0:T(8,128)(2,1)S(1)} %get-tuple-element.50), channel_id=1, source_target_pairs={{0,4},{4,0},{8,12},{12,8},{16,20},{20,16},{24,28},{28,24},{1,5},{5... | collective-permute-start | bytes 393224 | tf_op jit(solution)/shard_map/ppermute | solution.py:292
  28.6 0.0 collective-permute-done.3.far_ref
  28.6 0.0 copy-done.3
  28.6 5.9 %shard_map.78 = (bf16[8,128,128]{2,1,0:T(8,128)(2,1)S(1)}, f32[8,128,128]{2,1,0:T(8,128)S(1)}, f32[8,256]{1,0:T(8,128)S(1)}, f32[8,128,256]{2,1,0:T(8,128)S(1)},...) custom-call(bf16[256,1024]{1,0:T(8,128)(2,1)S(1)} %get-tuple-element.30.k_ref, ...), custom_call_target="tpu_custom_call" | custom-call | flops 671088640 | bytes 1048576 | tf_op jit(solution)/shard_map/pallas_call | solution.py:375
  34.5 2.5 %shard_map.79.x_ref = bf16[256,1024]{1,0:T(8,128)(2,1)S(1)} custom-call(bf16[256,1024]{1,0:T(8,128)(2,1)S(1)} %get-tuple-element.30.k_ref, bf16[8,128,256]{2,1,0:T(8,128)(2,1)S(1)} %get-tuple-element.31.kt_ref, bf16[8,128,128]{2,1,0:T(8,128)(2,1)S(1)} %get-tuple-element.38.mat_ref, f32[8,128,128]{2,1,0:T(8,128)S(1)} %get-tuple-element.39.ridges, ...), custom_call_target="tpu_custom_call" | custom-call | flops 671088640 | bytes 1048576 | tf_op jit(solution)/shard_map/pallas_call | solution.py:387
  37.0 0.9 %shard_map.81.local_ref = f32[256,1024]{1,0:T(8,128)S(1)} custom-call(bf16[256,1024]{1,0:T(8,128)(2,1)S(1)} %shard_map.79.x_ref, bf16[256,1024]{1,0:T(8,128)(2,1)S(1)} %get-tuple-element.30.k_ref, bf16[256,1024]{1,0:T(8,128)(2,1)S(1)} %get-tuple-element.46.val_ref), custom_call_target="tpu_custom_call" | custom-call | flops 67108864 | bytes 1048576 | tf_op jit(solution)/shard_map/pallas_call | solution.py:396
  37.9 0.0 collective-permute-done.7.far_ref
  37.9 0.0 copy-start.1
  37.9 0.0 copy-start.2
  37.9 0.4 shard_map.85
  38.3 0.1 collective-permute-start.8
  38.4 1.6 %collective-permute-start.9 = (bf16[64,1024]{1,0:T(8,128)(2,1)S(1)}, bf16[64,1024]{1,0:T(8,128)(2,1)S(1)}, u32[]{:S(2)}, u32[]{:S(2)}) collective-permute-start(bf16[64,1024]{1,0:T(8,128)(2,1)S(1)} %get-tuple-element.53), channel_id=1, source_target_pairs={{0,2},{1,3},{2,0},{3,1},{4,6},{5,7},{6,4},{7,5},{8,10},{9,11},{10,... | collective-permute-start | bytes 393224 | tf_op jit(solution)/shard_map/ppermute | solution.py:292
  40.0 0.3 collective-permute-start.10
  40.2 0.0 copy-done.1
  40.2 0.0 copy-done.2
  40.2 0.1 shard_map.86.refs_4_
  40.4 0.0 collective-permute-done.8.refs_1_
  40.4 4.4 %collective-permute-done.9.refs_2_ = bf16[64,1024]{1,0:T(8,128)(2,1)S(1)} collective-permute-done((bf16[64,1024]{1,0:T(8,128)(2,1)S(1)}, bf16[64,1024]{1,0:T(8,128)(2,1)S(1)}, u32[]{:S(2)}, u32[]{:S(2)}) %collective-permute-start.9) | collective-permute-done | bytes 131104 | tf_op jit(solution)/shard_map/ppermute | solution.py:292
  44.8 1.7 %collective-permute-done.10.refs_3_ = bf16[64,1024]{1,0:T(8,128)(2,1)S(1)} collective-permute-done((bf16[64,1024]{1,0:T(8,128)(2,1)S(1)}, bf16[64,1024]{1,0:T(8,128)(2,1)S(1)}, u32[]{:S(2)}, u32[]{:S(2)}) %collective-permute-start.10) | collective-permute-done | bytes 131104 | tf_op jit(solution)/shard_map/ppermute | solution.py:292
  46.6 1.1 %shard_map.87 = bf16[64,4096]{1,0:T(8,128)(2,1)} custom-call(bf16[64,1024]{1,0:T(8,128)(2,1)S(1)} %get-tuple-element.51.refs_0_, bf16[64,1024]{1,0:T(8,128)(2,1)S(1)} %collective-permute-done.8.refs_1_, bf16[64,1024]{1,0:T(8,128)(2,1)S(1)} %collective-permute-done.9.refs_2_, bf16[64,1024]{1,0:T(8,128)(2,1)S(1)} %collective-permute-done.10.refs_3_, ...), custom_call_target="tpu_custom_call" | custom-call | flops 67108864 | bytes 1048576 | tf_op jit(solution)/shard_map/pallas_call | solution.py:410
  (4 shorter events, 0.1 us)
Async XLA Ops:
  2.7 7.3 %collective-permute-start.4 = (bf16[4,128,128]{2,1,0:T(8,128)(2,1)S(1)}, bf16[4,128,128]{2,1,0:T(8,128)(2,1)S(1)}, u32[]{:S(2)}, u32[]{:S(2)}) collective-permute-start(bf16[4,128,128]{2,1,0:T(8,128)(2,1)S(1)} %get-tuple-element.48), channel_id=1, source_target_pairs={{0,4},{4,0},{8,12},{12,8},{16,20},{20,16},{24,28},{28,24},{1,5},{5... | collective-permute-start | bytes 393224 | tf_op jit(solution)/shard_map/ppermute | solution.py:292
  5.7 6.2 %collective-permute-start = (bf16[264,128]{1,0:T(8,128)(2,1)S(1)}, bf16[264,128]{1,0:T(8,128)(2,1)S(1)}, u32[]{:S(2)}, u32[]{:S(2)}) collective-permute-start(bf16[264,128]{1,0:T(8,128)(2,1)S(1)} %get-tuple-element.35), channel_id=1, source_target_pairs={{0,4},{4,0},{8,12},{12,8},{16,20},{20,16},{24,28},{28,24},{1,5},{5... | collective-permute-start | bytes 202760 | tf_op jit(solution)/shard_map/ppermute | solution.py:292
  10.0 9.5 %collective-permute-start.5 = (bf16[4,128,128]{2,1,0:T(8,128)(2,1)S(1)}, bf16[4,128,128]{2,1,0:T(8,128)(2,1)S(1)}, u32[]{:S(2)}, u32[]{:S(2)}) collective-permute-start(bf16[4,128,128]{2,1,0:T(8,128)(2,1)S(1)} %shard_map.82.mine_ref), channel_id=1, source_target_pairs={{0,8},{4,12},{8,0},{12,4},{16,24},{20,28},{24,16},{28,20},{1,9},{5... | collective-permute-start | bytes 393224 | tf_op jit(solution)/shard_map/ppermute | solution.py:292
  11.9 13.1 %copy-start = (bf16[256,1024]{1,0:T(8,128)(2,1)S(1)}, bf16[256,1024]{1,0:T(8,128)(2,1)}, u32[]{:S(2)}) copy-start(bf16[256,1024]{1,0:T(8,128)(2,1)} %q_ref.1) | copy-start | bytes 1572868
  11.9 4.4 %collective-permute-start.1 = (bf16[264,128]{1,0:T(8,128)(2,1)S(1)}, bf16[264,128]{1,0:T(8,128)(2,1)S(1)}, u32[]{:S(2)}, u32[]{:S(2)}) collective-permute-start(bf16[264,128]{1,0:T(8,128)(2,1)S(1)} %shard_map.75.mine_ref), channel_id=1, source_target_pairs={{0,8},{4,12},{8,0},{12,4},{16,24},{20,28},{24,16},{28,20},{1,9},{5... | collective-permute-start | bytes 202760 | tf_op jit(solution)/shard_map/ppermute | solution.py:292
  16.3 7.1 %collective-permute-start.2 = (bf16[264,128]{1,0:T(8,128)(2,1)S(1)}, bf16[264,128]{1,0:T(8,128)(2,1)S(1)}, u32[]{:S(2)}, u32[]{:S(2)}) collective-permute-start(bf16[264,128]{1,0:T(8,128)(2,1)S(1)} %shard_map.76), channel_id=1, source_target_pairs={{0,16},{4,20},{8,24},{12,28},{16,0},{20,4},{24,8},{28,12},{1,17},{... | collective-permute-start | bytes 202760 | tf_op jit(solution)/shard_map/ppermute | solution.py:292
  19.6 7.4 %collective-permute-start.6 = (bf16[4,128,128]{2,1,0:T(8,128)(2,1)S(1)}, bf16[4,128,128]{2,1,0:T(8,128)(2,1)S(1)}, u32[]{:S(2)}, u32[]{:S(2)}) collective-permute-start(bf16[4,128,128]{2,1,0:T(8,128)(2,1)S(1)} %shard_map.83), channel_id=1, source_target_pairs={{0,16},{4,20},{8,24},{12,28},{16,0},{20,4},{24,8},{28,12},{1,17},{... | collective-permute-start | bytes 393224 | tf_op jit(solution)/shard_map/ppermute | solution.py:292
  23.5 5.1 %collective-permute-start.3 = (bf16[264,128]{1,0:T(8,128)(2,1)S(1)}, bf16[264,128]{1,0:T(8,128)(2,1)S(1)}, u32[]{:S(2)}, u32[]{:S(2)}) collective-permute-start(bf16[264,128]{1,0:T(8,128)(2,1)S(1)} %get-tuple-element.37), channel_id=1, source_target_pairs={{0,4},{4,0},{8,12},{12,8},{16,20},{20,16},{24,28},{28,24},{1,5},{5... | collective-permute-start | bytes 202760 | tf_op jit(solution)/shard_map/ppermute | solution.py:292
  27.1 1.5 %copy-start.3 = (f32[8,128]{1,0:T(8,128)S(1)}, f32[8,128]{1,0:T(8,128)}, u32[]{:S(2)}) copy-start(f32[8,128]{1,0:T(8,128)} %ridge_ref.1) | copy-start | bytes 12292
  27.1 10.8 %collective-permute-start.7 = (bf16[4,128,128]{2,1,0:T(8,128)(2,1)S(1)}, bf16[4,128,128]{2,1,0:T(8,128)(2,1)S(1)}, u32[]{:S(2)}, u32[]{:S(2)}) collective-permute-start(bf16[4,128,128]{2,1,0:T(8,128)(2,1)S(1)} %get-tuple-element.50), channel_id=1, source_target_pairs={{0,4},{4,0},{8,12},{12,8},{16,20},{20,16},{24,28},{28,24},{1,5},{5... | collective-permute-start | bytes 393224 | tf_op jit(solution)/shard_map/ppermute | solution.py:292
  37.9 2.3 %copy-start.1 = (bf16[64,4096]{1,0:T(8,128)(2,1)S(1)}, bf16[64,4096]{1,0:T(8,128)(2,1)}, u32[]{:S(2)}) copy-start(bf16[64,4096]{1,0:T(8,128)(2,1)} %logit_ref.1) | copy-start | bytes 1572868
  37.9 2.3 %copy-start.2 = (f32[4096]{0:T(1024)S(1)}, f32[4096]{0:T(1024)}, u32[]{:S(2)}) copy-start(f32[4096]{0:T(1024)} %param.12) | copy-start | bytes 49156
  38.3 2.1 %collective-permute-start.8 = (bf16[64,1024]{1,0:T(8,128)(2,1)S(1)}, bf16[64,1024]{1,0:T(8,128)(2,1)S(1)}, u32[]{:S(2)}, u32[]{:S(2)}) collective-permute-start(bf16[64,1024]{1,0:T(8,128)(2,1)S(1)} %get-tuple-element.52), channel_id=1, source_target_pairs={{0,1},{1,0},{2,3},{3,2},{4,5},{5,4},{6,7},{7,6},{8,9},{9,8},{10,11... | collective-permute-start | bytes 393224 | tf_op jit(solution)/shard_map/ppermute | solution.py:292
  38.4 6.4 %collective-permute-start.9 = (bf16[64,1024]{1,0:T(8,128)(2,1)S(1)}, bf16[64,1024]{1,0:T(8,128)(2,1)S(1)}, u32[]{:S(2)}, u32[]{:S(2)}) collective-permute-start(bf16[64,1024]{1,0:T(8,128)(2,1)S(1)} %get-tuple-element.53), channel_id=1, source_target_pairs={{0,2},{1,3},{2,0},{3,1},{4,6},{5,7},{6,4},{7,5},{8,10},{9,11},{10,... | collective-permute-start | bytes 393224 | tf_op jit(solution)/shard_map/ppermute | solution.py:292
  40.0 6.6 %collective-permute-start.10 = (bf16[64,1024]{1,0:T(8,128)(2,1)S(1)}, bf16[64,1024]{1,0:T(8,128)(2,1)S(1)}, u32[]{:S(2)}, u32[]{:S(2)}) collective-permute-start(bf16[64,1024]{1,0:T(8,128)(2,1)S(1)} %get-tuple-element.54), channel_id=1, source_target_pairs={{0,3},{1,2},{2,1},{3,0},{4,7},{5,6},{6,5},{7,4},{8,11},{9,10},{10,... | collective-permute-start | bytes 393224 | tf_op jit(solution)/shard_map/ppermute | solution.py:292

commit v7 on v6

--- a/solution.py
+++ b/solution.py
@@ -229,7 +229,7 @@
         norms.append(square_sum(qt_ref[h], 0))
     fixed = (k_ref, kt_ref, mat_ref, ridges)
     norms = sweep(*fixed, (qt_ref, qt_ref, None), state, norms, local_ref)
-    norms = lax.fori_loop(1, sweeps, lambda _, now: sweep(*fixed, state, state, now), norms)
+    norms = lax.fori_loop(1, sweeps, lambda _, now: sweep(*fixed, state, state, now), norms, unroll=True)
     norm_ref[...] = jnp.concatenate(norms, axis=0)
 
 
@@ -239,7 +239,7 @@
     fixed = (k_ref, kt_ref, mat_ref, ridges)
     norms = tuple(norm_ref[h : h + 1] for h in range(heads))
     norms = sweep(*fixed, given, state, norms)
-    norms = lax.fori_loop(1, sweeps, lambda _, now: sweep(*fixed, state, state, now), norms)
+    norms = lax.fori_loop(1, sweeps, lambda _, now: sweep(*fixed, state, state, now), norms, unroll=True)
     for h in range(heads):
         direction = state[1][h]
         ridge = jnp.concatenate([ridges[h]] * (direction.shape[1] // width), axis=1)
@@ -290,6 +290,10 @@
 
 def swap(x, axis, size, step):
     return lax.ppermute(x, axis, [(i, i ^ step) for i in range(size)])
+
+
+def route(k):
+    return [1 << b for b in reversed(range(k.bit_length())) if k >> b & 1]
 
 
 def shape(*dims, dtype=BF16):
@@ -406,7 +410,12 @@
         [pltpu.VMEM((toks, cols), BF16)],
         flops=work,
     )(x, local, own, far)
-    arrived = [pieces[0]] + [swap(pieces[k], "head", spots, k) for k in range(1, spots)]
+    arrived = [pieces[0]]
+    for k in range(1, spots):
+        piece = pieces[k]
+        for hop in route(k):
+            piece = swap(piece, "head", spots, hop)
+        arrived.append(piece)
     return call(
         functools.partial(norm_kernel, spots),
         shape(rows, spots * cols),

time: 47.8 us -> 46.5 us (0.973)
  Pallas kernels: 15.8 us -> 14.9 us
  waiting for transfers between devices: 17.7 us -> 17.2 us
    pallas_call x1, Pallas kernels: 5.87 us -> 4.93 us  [shards(): call(functools.partial(cg_first_kernel, width, FIRST), [shape(heads, widt...]
    ppermute x11 -> x12, waiting for transfers between devices: 17.7 us -> 17.2 us  [swap(): return lax.ppermute(x, axis, [(i, i ^ step) for i in range(size)])]
    ppermute x11 -> x12, starting transfers between devices: 13.9 us -> 14.1 us  [swap(): return lax.ppermute(x, axis, [(i, i ^ step) for i in range(size)])]
  transfers between devices with their start and end apart: 11 -> 12, of which waited for: 5 -> 5; matrix products, arithmetic and copies ran while one was open for 0% -> 0% of each run, Pallas kernels for 25% -> 23%
where the time goes in v7:
time: 46.5 us; the launch traced here: 46.3 us
  waiting for transfers between devices  17.2 us (37%)
  Pallas kernels  14.9 us (32%)
  starting transfers between devices  14.1 us (30%)
    ppermute x12, waiting for transfers between devices, swap(): return lax.ppermute(x, axis, [(i, i ^ step) for i in range(size)])  17.2 us
    ppermute x12, starting transfers between devices, swap(): return lax.ppermute(x, axis, [(i, i ^ step) for i in range(size)])  14.1 us
    pallas_call x1, Pallas kernels, shards(): call(functools.partial(cg_first_kernel, width, FIRST), [shape(heads, widt...  4.93 us
    pallas_call x1, Pallas kernels, shards(): call(functools.partial(cg_last_kernel, width, ITERS - 1 - FIRST), shape(t...  2.49 us
    pallas_call x1, Pallas kernels, shards(): call(functools.partial(prepare_kernel, width), [shape(heads, width, toks,...  1.95 us
    pallas_call x1, Pallas kernels, shards(): call(functools.partial(key_state_kernel, width), [shape(packed, width), s...  1.59 us
    pallas_call x1, Pallas kernels, shards(): call(functools.partial(value_state_kernel, width), [shape(toks, cols)] +...  1.11 us
    pallas_call x1, Pallas kernels, shards(): call(functools.partial(norm_kernel, spots), shape(rows, spots * cols), [V...  1.07 us
  transfers between devices with their start and end apart: 12, of which 5 were waited for; matrix products, arithmetic and copies ran while one was open for 0% of the time, Pallas kernels for 23%

profile of v7, /device:TPU:0, one launch (start us, length us, event | category | flops | bytes accessed | tf_op | source)
XLA Modules:
  0.0 46.3 jit_solution(10698865419240279096)
XLA Ops:
  0.0 1.6 %shard_map.73 = (bf16[264,128]{1,0:T(8,128)(2,1)S(1)}, bf16[264,128]{1,0:T(8,128)(2,1)S(1)}, bf16[8,128,256]{2,1,0:T(8,128)(2,1)S(1)}, bf16[256,1024]{1,0:T(8,12...) custom-call(bf16[256,1024]{1,0:T(8,128)(2,1)} %k_hbm.1, bf16[256,1024]{1,0:T(8,128)(2,1)} %v_hbm.1, ...), custom_call_target="tpu_custom_call" | custom-call | flops 67108864 | bytes 1048576 | tf_op jit(solution)/shard_map/pallas_call | solution.py:316
  1.6 1.1 %shard_map.80 = (bf16[256,1024]{1,0:T(8,128)(2,1)S(1)}, bf16[4,128,128]{2,1,0:T(8,128)(2,1)S(1)}, bf16[4,128,128]{2,1,0:T(8,128)(2,1)S(1)}) custom-call(bf16[256,1024]{1,0:T(8,128)(2,1)S(1)} %get-tuple-element.30.k_ref, bf16[256,1024]{1,0:T(8,128)(2,1)S(1)} %get-tuple-element.44.v_ref, f32[8,256]{1,0:T(8,128)S(1)} %get-tuple-element.45.scale_ref), custom_call_target="tpu_custom_call" | custom-call | flops 67108864 | bytes 1048576 | tf_op jit(solution)/shard_map/pallas_call | solution.py:335
  2.7 3.0 %collective-permute-start.4 = (bf16[4,128,128]{2,1,0:T(8,128)(2,1)S(1)}, bf16[4,128,128]{2,1,0:T(8,128)(2,1)S(1)}, u32[]{:S(2)}, u32[]{:S(2)}) collective-permute-start(bf16[4,128,128]{2,1,0:T(8,128)(2,1)S(1)} %get-tuple-element.48), channel_id=1, source_target_pairs={{0,4},{4,0},{8,12},{12,8},{16,20},{20,16},{24,28},{28,24},{1,5},{5... | collective-permute-start | bytes 393224 | tf_op jit(solution)/shard_map/ppermute | solution.py:292
  5.7 0.1 collective-permute-start
  5.8 4.1 %collective-permute-done.4.other_ref.near_ref = bf16[4,128,128]{2,1,0:T(8,128)(2,1)S(1)} collective-permute-done((bf16[4,128,128]{2,1,0:T(8,128)(2,1)S(1)}, bf16[4,128,128]{2,1,0:T(8,128)(2,1)S(1)}, u32[]{:S(2)}, u32[]{:S(2)}) %collective-permute-start.4) | collective-permute-done | bytes 131104 | tf_op jit(solution)/shard_map/ppermute | solution.py:292
  10.0 1.9 %collective-permute-start.5 = (bf16[4,128,128]{2,1,0:T(8,128)(2,1)S(1)}, bf16[4,128,128]{2,1,0:T(8,128)(2,1)S(1)}, u32[]{:S(2)}, u32[]{:S(2)}) collective-permute-start(bf16[4,128,128]{2,1,0:T(8,128)(2,1)S(1)} %shard_map.82.mine_ref), channel_id=1, source_target_pairs={{0,8},{4,12},{8,0},{12,4},{16,24},{20,28},{24,16},{28,20},{1,9},{5... | collective-permute-start | bytes 393224 | tf_op jit(solution)/shard_map/ppermute | solution.py:292
  11.9 0.0 collective-permute-done.other_ref.near_ref
  11.9 0.0 copy-start
  11.9 0.7 %collective-permute-start.1 = (bf16[264,128]{1,0:T(8,128)(2,1)S(1)}, bf16[264,128]{1,0:T(8,128)(2,1)S(1)}, u32[]{:S(2)}, u32[]{:S(2)}) collective-permute-start(bf16[264,128]{1,0:T(8,128)(2,1)S(1)} %shard_map.75.mine_ref), channel_id=1, source_target_pairs={{0,8},{4,12},{8,0},{12,4},{16,24},{20,28},{24,16},{28,20},{1,9},{5... | collective-permute-start | bytes 202760 | tf_op jit(solution)/shard_map/ppermute | solution.py:292
  12.6 3.7 %collective-permute-done.1.other_ref.refs_0_ = bf16[264,128]{1,0:T(8,128)(2,1)S(1)} collective-permute-done((bf16[264,128]{1,0:T(8,128)(2,1)S(1)}, bf16[264,128]{1,0:T(8,128)(2,1)S(1)}, u32[]{:S(2)}, u32[]{:S(2)}) %collective-permute-start.1) | collective-permute-done | bytes 67616 | tf_op jit(solution)/shard_map/ppermute | solution.py:292
  16.3 3.2 %collective-permute-start.2 = (bf16[264,128]{1,0:T(8,128)(2,1)S(1)}, bf16[264,128]{1,0:T(8,128)(2,1)S(1)}, u32[]{:S(2)}, u32[]{:S(2)}) collective-permute-start(bf16[264,128]{1,0:T(8,128)(2,1)S(1)} %shard_map.76), channel_id=1, source_target_pairs={{0,16},{4,20},{8,24},{12,28},{16,0},{20,4},{24,8},{28,12},{1,17},{... | collective-permute-start | bytes 202760 | tf_op jit(solution)/shard_map/ppermute | solution.py:292
  19.5 0.0 collective-permute-done.5.other_ref.refs_0_
  19.6 0.1 collective-permute-start.6
  19.6 3.8 %collective-permute-done.2.refs_1_ = bf16[264,128]{1,0:T(8,128)(2,1)S(1)} collective-permute-done((bf16[264,128]{1,0:T(8,128)(2,1)S(1)}, bf16[264,128]{1,0:T(8,128)(2,1)S(1)}, u32[]{:S(2)}, u32[]{:S(2)}) %collective-permute-start.2) | collective-permute-done | bytes 67616 | tf_op jit(solution)/shard_map/ppermute | solution.py:292
  23.4 0.1 shard_map.77
  23.5 1.6 %collective-permute-start.3 = (bf16[264,128]{1,0:T(8,128)(2,1)S(1)}, bf16[264,128]{1,0:T(8,128)(2,1)S(1)}, u32[]{:S(2)}, u32[]{:S(2)}) collective-permute-start(bf16[264,128]{1,0:T(8,128)(2,1)S(1)} %get-tuple-element.37), channel_id=1, source_target_pairs={{0,4},{4,0},{8,12},{12,8},{16,20},{20,16},{24,28},{28,24},{1,5},{5... | collective-permute-start | bytes 202760 | tf_op jit(solution)/shard_map/ppermute | solution.py:292
  25.0 0.0 copy-done
  25.0 2.0 %shard_map.74 = (f32[8,128,256]{2,1,0:T(8,128)S(1)}, f32[8,128,256]{2,1,0:T(8,128)S(1)}) custom-call(bf16[256,1024]{1,0:T(8,128)(2,1)S(1)} %copy-done, bf16[256,1024]{1,0:T(8,128)(2,1)S(1)} %get-tuple-element.30.k_ref, bf16[8,128,256]{2,1,0:T(8,128)(2,1)S(1)} %get-tuple-element.31.kt_ref), custom_call_target="tpu_custom_call" | custom-call | flops 67108864 | bytes 1048576 | tf_op jit(solution)/shard_map/pallas_call | solution.py:341
  27.0 0.0 collective-permute-done.6.refs_1_
  27.0 0.1 shard_map.84
  27.1 0.0 copy-start.3
  27.1 1.4 %collective-permute-start.7 = (bf16[4,128,128]{2,1,0:T(8,128)(2,1)S(1)}, bf16[4,128,128]{2,1,0:T(8,128)(2,1)S(1)}, u32[]{:S(2)}, u32[]{:S(2)}) collective-permute-start(bf16[4,128,128]{2,1,0:T(8,128)(2,1)S(1)} %get-tuple-element.50), channel_id=1, source_target_pairs={{0,4},{4,0},{8,12},{12,8},{16,20},{20,16},{24,28},{28,24},{1,5},{5... | collective-permute-start | bytes 393224 | tf_op jit(solution)/shard_map/ppermute | solution.py:292
  28.6 0.0 collective-permute-done.3.far_ref
  28.6 0.0 copy-done.3
  28.6 4.9 %shard_map.78 = (bf16[8,128,128]{2,1,0:T(8,128)(2,1)S(1)}, f32[8,128,128]{2,1,0:T(8,128)S(1)}, f32[8,256]{1,0:T(8,128)S(1)}, f32[8,128,256]{2,1,0:T(8,128)S(1)},...) custom-call(bf16[256,1024]{1,0:T(8,128)(2,1)S(1)} %get-tuple-element.30.k_ref, ...), custom_call_target="tpu_custom_call" | custom-call | flops 671088640 | bytes 1048576 | tf_op jit(solution)/shard_map/pallas_call | solution.py:379
  33.5 2.5 %shard_map.79.x_ref = bf16[256,1024]{1,0:T(8,128)(2,1)S(1)} custom-call(bf16[256,1024]{1,0:T(8,128)(2,1)S(1)} %get-tuple-element.30.k_ref, bf16[8,128,256]{2,1,0:T(8,128)(2,1)S(1)} %get-tuple-element.31.kt_ref, bf16[8,128,128]{2,1,0:T(8,128)(2,1)S(1)} %get-tuple-element.38.mat_ref, f32[8,128,128]{2,1,0:T(8,128)S(1)} %get-tuple-element.39.ridges, ...), custom_call_target="tpu_custom_call" | custom-call | flops 671088640 | bytes 1048576 | tf_op jit(solution)/shard_map/pallas_call | solution.py:391
  36.0 0.9 %shard_map.81.local_ref = f32[256,1024]{1,0:T(8,128)S(1)} custom-call(bf16[256,1024]{1,0:T(8,128)(2,1)S(1)} %shard_map.79.x_ref, bf16[256,1024]{1,0:T(8,128)(2,1)S(1)} %get-tuple-element.30.k_ref, bf16[256,1024]{1,0:T(8,128)(2,1)S(1)} %get-tuple-element.46.val_ref), custom_call_target="tpu_custom_call" | custom-call | flops 67108864 | bytes 1048576 | tf_op jit(solution)/shard_map/pallas_call | solution.py:400
  37.0 0.0 collective-permute-done.7.far_ref
  37.0 0.0 copy-start.1
  37.0 0.0 copy-start.2
  37.0 0.4 shard_map.85
  37.4 1.6 %collective-permute-start.10 = (bf16[64,1024]{1,0:T(8,128)(2,1)S(1)}, bf16[64,1024]{1,0:T(8,128)(2,1)S(1)}, u32[]{:S(2)}, u32[]{:S(2)}) collective-permute-start(bf16[64,1024]{1,0:T(8,128)(2,1)S(1)} %get-tuple-element.54), channel_id=1, source_target_pairs={{0,2},{1,3},{2,0},{3,1},{4,6},{5,7},{6,4},{7,5},{8,10},{9,11},{10,... | collective-permute-start | bytes 393224 | tf_op jit(solution)/shard_map/ppermute | solution.py:292
  38.9 0.0 collective-permute-start.8
  39.0 0.5 %collective-permute-start.9 = (bf16[64,1024]{1,0:T(8,128)(2,1)S(1)}, bf16[64,1024]{1,0:T(8,128)(2,1)S(1)}, u32[]{:S(2)}, u32[]{:S(2)}) collective-permute-start(bf16[64,1024]{1,0:T(8,128)(2,1)S(1)} %get-tuple-element.53), channel_id=1, source_target_pairs={{0,2},{1,3},{2,0},{3,1},{4,6},{5,7},{6,4},{7,5},{8,10},{9,11},{10,... | collective-permute-start | bytes 393224 | tf_op jit(solution)/shard_map/ppermute | solution.py:292
  39.5 3.3 %collective-permute-done.10 = bf16[64,1024]{1,0:T(8,128)(2,1)S(1)} collective-permute-done((bf16[64,1024]{1,0:T(8,128)(2,1)S(1)}, bf16[64,1024]{1,0:T(8,128)(2,1)S(1)}, u32[]{:S(2)}, u32[]{:S(2)}) %collective-permute-start.10) | collective-permute-done | bytes 131104 | tf_op jit(solution)/shard_map/ppermute | solution.py:292
  42.8 0.0 collective-permute-start.11
  42.8 0.0 copy-done.1
  42.8 0.0 copy-done.2
  42.8 0.1 shard_map.86.refs_4_
  43.0 0.0 collective-permute-done.8.refs_1_
  43.0 2.2 %collective-permute-done.9.refs_2_ = bf16[64,1024]{1,0:T(8,128)(2,1)S(1)} collective-permute-done((bf16[64,1024]{1,0:T(8,128)(2,1)S(1)}, bf16[64,1024]{1,0:T(8,128)(2,1)S(1)}, u32[]{:S(2)}, u32[]{:S(2)}) %collective-permute-start.9) | collective-permute-done | bytes 131104 | tf_op jit(solution)/shard_map/ppermute | solution.py:292
  45.2 0.0 collective-permute-done.11.refs_3_
  45.2 1.1 %shard_map.87 = bf16[64,4096]{1,0:T(8,128)(2,1)} custom-call(bf16[64,1024]{1,0:T(8,128)(2,1)S(1)} %get-tuple-element.51.refs_0_, bf16[64,1024]{1,0:T(8,128)(2,1)S(1)} %collective-permute-done.8.refs_1_, bf16[64,1024]{1,0:T(8,128)(2,1)S(1)} %collective-permute-done.9.refs_2_, bf16[64,1024]{1,0:T(8,128)(2,1)S(1)} %collective-permute-done.11.refs_3_, ...), custom_call_target="tpu_custom_call" | custom-call | flops 67108864 | bytes 1048576 | tf_op jit(solution)/shard_map/pallas_call | solution.py:419
  (4 shorter events, 0.1 us)
Async XLA Ops:
  2.7 7.3 %collective-permute-start.4 = (bf16[4,128,128]{2,1,0:T(8,128)(2,1)S(1)}, bf16[4,128,128]{2,1,0:T(8,128)(2,1)S(1)}, u32[]{:S(2)}, u32[]{:S(2)}) collective-permute-start(bf16[4,128,128]{2,1,0:T(8,128)(2,1)S(1)} %get-tuple-element.48), channel_id=1, source_target_pairs={{0,4},{4,0},{8,12},{12,8},{16,20},{20,16},{24,28},{28,24},{1,5},{5... | collective-permute-start | bytes 393224 | tf_op jit(solution)/shard_map/ppermute | solution.py:292
  5.7 6.2 %collective-permute-start = (bf16[264,128]{1,0:T(8,128)(2,1)S(1)}, bf16[264,128]{1,0:T(8,128)(2,1)S(1)}, u32[]{:S(2)}, u32[]{:S(2)}) collective-permute-start(bf16[264,128]{1,0:T(8,128)(2,1)S(1)} %get-tuple-element.35), channel_id=1, source_target_pairs={{0,4},{4,0},{8,12},{12,8},{16,20},{20,16},{24,28},{28,24},{1,5},{5... | collective-permute-start | bytes 202760 | tf_op jit(solution)/shard_map/ppermute | solution.py:292
  10.0 9.5 %collective-permute-start.5 = (bf16[4,128,128]{2,1,0:T(8,128)(2,1)S(1)}, bf16[4,128,128]{2,1,0:T(8,128)(2,1)S(1)}, u32[]{:S(2)}, u32[]{:S(2)}) collective-permute-start(bf16[4,128,128]{2,1,0:T(8,128)(2,1)S(1)} %shard_map.82.mine_ref), channel_id=1, source_target_pairs={{0,8},{4,12},{8,0},{12,4},{16,24},{20,28},{24,16},{28,20},{1,9},{5... | collective-permute-start | bytes 393224 | tf_op jit(solution)/shard_map/ppermute | solution.py:292
  11.9 13.1 %copy-start = (bf16[256,1024]{1,0:T(8,128)(2,1)S(1)}, bf16[256,1024]{1,0:T(8,128)(2,1)}, u32[]{:S(2)}) copy-start(bf16[256,1024]{1,0:T(8,128)(2,1)} %q_ref.1) | copy-start | bytes 1572868
  11.9 4.4 %collective-permute-start.1 = (bf16[264,128]{1,0:T(8,128)(2,1)S(1)}, bf16[264,128]{1,0:T(8,128)(2,1)S(1)}, u32[]{:S(2)}, u32[]{:S(2)}) collective-permute-start(bf16[264,128]{1,0:T(8,128)(2,1)S(1)} %shard_map.75.mine_ref), channel_id=1, source_target_pairs={{0,8},{4,12},{8,0},{12,4},{16,24},{20,28},{24,16},{28,20},{1,9},{5... | collective-permute-start | bytes 202760 | tf_op jit(solution)/shard_map/ppermute | solution.py:292
  16.3 7.1 %collective-permute-start.2 = (bf16[264,128]{1,0:T(8,128)(2,1)S(1)}, bf16[264,128]{1,0:T(8,128)(2,1)S(1)}, u32[]{:S(2)}, u32[]{:S(2)}) collective-permute-start(bf16[264,128]{1,0:T(8,128)(2,1)S(1)} %shard_map.76), channel_id=1, source_target_pairs={{0,16},{4,20},{8,24},{12,28},{16,0},{20,4},{24,8},{28,12},{1,17},{... | collective-permute-start | bytes 202760 | tf_op jit(solution)/shard_map/ppermute | solution.py:292
  19.6 7.4 %collective-permute-start.6 = (bf16[4,128,128]{2,1,0:T(8,128)(2,1)S(1)}, bf16[4,128,128]{2,1,0:T(8,128)(2,1)S(1)}, u32[]{:S(2)}, u32[]{:S(2)}) collective-permute-start(bf16[4,128,128]{2,1,0:T(8,128)(2,1)S(1)} %shard_map.83), channel_id=1, source_target_pairs={{0,16},{4,20},{8,24},{12,28},{16,0},{20,4},{24,8},{28,12},{1,17},{... | collective-permute-start | bytes 393224 | tf_op jit(solution)/shard_map/ppermute | solution.py:292
  23.5 5.1 %collective-permute-start.3 = (bf16[264,128]{1,0:T(8,128)(2,1)S(1)}, bf16[264,128]{1,0:T(8,128)(2,1)S(1)}, u32[]{:S(2)}, u32[]{:S(2)}) collective-permute-start(bf16[264,128]{1,0:T(8,128)(2,1)S(1)} %get-tuple-element.37), channel_id=1, source_target_pairs={{0,4},{4,0},{8,12},{12,8},{16,20},{20,16},{24,28},{28,24},{1,5},{5... | collective-permute-start | bytes 202760 | tf_op jit(solution)/shard_map/ppermute | solution.py:292
  27.1 1.5 %copy-start.3 = (f32[8,128]{1,0:T(8,128)S(1)}, f32[8,128]{1,0:T(8,128)}, u32[]{:S(2)}) copy-start(f32[8,128]{1,0:T(8,128)} %ridge_ref.1) | copy-start | bytes 12292
  27.1 9.8 %collective-permute-start.7 = (bf16[4,128,128]{2,1,0:T(8,128)(2,1)S(1)}, bf16[4,128,128]{2,1,0:T(8,128)(2,1)S(1)}, u32[]{:S(2)}, u32[]{:S(2)}) collective-permute-start(bf16[4,128,128]{2,1,0:T(8,128)(2,1)S(1)} %get-tuple-element.50), channel_id=1, source_target_pairs={{0,4},{4,0},{8,12},{12,8},{16,20},{20,16},{24,28},{28,24},{1,5},{5... | collective-permute-start | bytes 393224 | tf_op jit(solution)/shard_map/ppermute | solution.py:292
  37.0 5.8 %copy-start.1 = (bf16[64,4096]{1,0:T(8,128)(2,1)S(1)}, bf16[64,4096]{1,0:T(8,128)(2,1)}, u32[]{:S(2)}) copy-start(bf16[64,4096]{1,0:T(8,128)(2,1)} %logit_ref.1) | copy-start | bytes 1572868
  37.0 5.8 %copy-start.2 = (f32[4096]{0:T(1024)S(1)}, f32[4096]{0:T(1024)}, u32[]{:S(2)}) copy-start(f32[4096]{0:T(1024)} %param.12) | copy-start | bytes 49156
  37.4 5.4 %collective-permute-start.10 = (bf16[64,1024]{1,0:T(8,128)(2,1)S(1)}, bf16[64,1024]{1,0:T(8,128)(2,1)S(1)}, u32[]{:S(2)}, u32[]{:S(2)}) collective-permute-start(bf16[64,1024]{1,0:T(8,128)(2,1)S(1)} %get-tuple-element.54), channel_id=1, source_target_pairs={{0,2},{1,3},{2,0},{3,1},{4,6},{5,7},{6,4},{7,5},{8,10},{9,11},{10,... | collective-permute-start | bytes 393224 | tf_op jit(solution)/shard_map/ppermute | solution.py:292
  38.9 4.0 %collective-permute-start.8 = (bf16[64,1024]{1,0:T(8,128)(2,1)S(1)}, bf16[64,1024]{1,0:T(8,128)(2,1)S(1)}, u32[]{:S(2)}, u32[]{:S(2)}) collective-permute-start(bf16[64,1024]{1,0:T(8,128)(2,1)S(1)} %get-tuple-element.52), channel_id=1, source_target_pairs={{0,1},{1,0},{2,3},{3,2},{4,5},{5,4},{6,7},{7,6},{8,9},{9,8},{10,11... | collective-permute-start | bytes 393224 | tf_op jit(solution)/shard_map/ppermute | solution.py:292
  39.0 6.3 %collective-permute-start.9 = (bf16[64,1024]{1,0:T(8,128)(2,1)S(1)}, bf16[64,1024]{1,0:T(8,128)(2,1)S(1)}, u32[]{:S(2)}, u32[]{:S(2)}) collective-permute-start(bf16[64,1024]{1,0:T(8,128)(2,1)S(1)} %get-tuple-element.53), channel_id=1, source_target_pairs={{0,2},{1,3},{2,0},{3,1},{4,6},{5,7},{6,4},{7,5},{8,10},{9,11},{10,... | collective-permute-start | bytes 393224 | tf_op jit(solution)/shard_map/ppermute | solution.py:292
  42.8 2.4 %collective-permute-start.11 = (bf16[64,1024]{1,0:T(8,128)(2,1)S(1)}, bf16[64,1024]{1,0:T(8,128)(2,1)S(1)}, u32[]{:S(2)}, u32[]{:S(2)}) collective-permute-start(bf16[64,1024]{1,0:T(8,128)(2,1)S(1)} %collective-permute-done.10), channel_id=1, source_target_pairs={{0,1},{1,0},{2,3},{3,2},{4,5},{5,4},{6,7},{7,6},{8,9},{9,8},{10,11... | collective-permute-start | bytes 393224 | tf_op jit(solution)/shard_map/ppermute | solution.py:292

commit v8 on v7

--- a/solution.py
+++ b/solution.py
@@ -172,7 +172,7 @@
     return dot(both, jnp.concatenate([low] + causal(k_ref, low, h), axis=0))
 
 
-def sweep(k_ref, kt_ref, mat_ref, ridges, old, new, norms, local=None):
+def sweep(k_ref, kt_ref, mat_ref, ridges, old, new, norms, local=None, final=False):
     after = []
     width, toks = old[0].shape[1:]
     for h in range(mat_ref.shape[0]):
@@ -188,7 +188,8 @@
             norm = norms[h][:, at]
             alpha = norm / jnp.sum(direction * applied, axis=0, keepdims=True)
             residual = old[0][h, :, at] - alpha * applied
-            new[0][h, :, at] = residual
+            if not final:
+                new[0][h, :, at] = residual
             following = square_sum(residual, 0)
             step = alpha * direction
             new[2][h, :, at] = step if old[2] is None else old[2][h, :, at] + step
@@ -238,8 +239,8 @@
     heads = mat_ref.shape[0]
     fixed = (k_ref, kt_ref, mat_ref, ridges)
     norms = tuple(norm_ref[h : h + 1] for h in range(heads))
-    norms = sweep(*fixed, given, state, norms)
-    norms = lax.fori_loop(1, sweeps, lambda _, now: sweep(*fixed, state, state, now), norms, unroll=True)
+    for turn in range(sweeps):
+        norms = sweep(*fixed, state if turn else given, state, norms, final=turn + 1 == sweeps)
     for h in range(heads):
         direction = state[1][h]
         ridge = jnp.concatenate([ridges[h]] * (direction.shape[1] // width), axis=1)

time: 46.5 us -> 46.5 us (level)
  no operation moved by 1% of the time
where the time goes in v8:
time: 46.5 us; the launch traced here: 46.3 us
  waiting for transfers between devices  17.2 us (37%)
  Pallas kernels  14.9 us (32%)
  starting transfers between devices  14.1 us (30%)
    ppermute x12, waiting for transfers between devices, swap(): return lax.ppermute(x, axis, [(i, i ^ step) for i in range(size)])  17.2 us
    ppermute x12, starting transfers between devices, swap(): return lax.ppermute(x, axis, [(i, i ^ step) for i in range(size)])  14.1 us
    pallas_call x1, Pallas kernels, shards(): call(functools.partial(cg_first_kernel, width, FIRST), [shape(heads, widt...  4.93 us
    pallas_call x1, Pallas kernels, shards(): call(functools.partial(cg_last_kernel, width, ITERS - 1 - FIRST), shape(t...  2.49 us
    pallas_call x1, Pallas kernels, shards(): call(functools.partial(prepare_kernel, width), [shape(heads, width, toks,...  1.95 us
    pallas_call x1, Pallas kernels, shards(): call(functools.partial(key_state_kernel, width), [shape(packed, width), s...  1.59 us
    pallas_call x1, Pallas kernels, shards(): call(functools.partial(value_state_kernel, width), [shape(toks, cols)] +...  1.11 us
    pallas_call x1, Pallas kernels, shards(): call(functools.partial(norm_kernel, spots), shape(rows, spots * cols), [V...  1.07 us
  transfers between devices with their start and end apart: 12, of which 5 were waited for; matrix products, arithmetic and copies ran while one was open for 0% of the time, Pallas kernels for 23%

profile of v8, /device:TPU:0, one launch (start us, length us, event | category | flops | bytes accessed | tf_op | source)
XLA Modules:
  0.0 46.3 jit_solution(10698865419240279096)
XLA Ops:
  0.0 1.6 %shard_map.73 = (bf16[264,128]{1,0:T(8,128)(2,1)S(1)}, bf16[264,128]{1,0:T(8,128)(2,1)S(1)}, bf16[8,128,256]{2,1,0:T(8,128)(2,1)S(1)}, bf16[256,1024]{1,0:T(8,12...) custom-call(bf16[256,1024]{1,0:T(8,128)(2,1)} %k_hbm.1, bf16[256,1024]{1,0:T(8,128)(2,1)} %v_hbm.1, ...), custom_call_target="tpu_custom_call" | custom-call | flops 67108864 | bytes 1048576 | tf_op jit(solution)/shard_map/pallas_call | solution.py:317
  1.6 1.1 %shard_map.80 = (bf16[256,1024]{1,0:T(8,128)(2,1)S(1)}, bf16[4,128,128]{2,1,0:T(8,128)(2,1)S(1)}, bf16[4,128,128]{2,1,0:T(8,128)(2,1)S(1)}) custom-call(bf16[256,1024]{1,0:T(8,128)(2,1)S(1)} %get-tuple-element.30.k_ref, bf16[256,1024]{1,0:T(8,128)(2,1)S(1)} %get-tuple-element.44.v_ref, f32[8,256]{1,0:T(8,128)S(1)} %get-tuple-element.45.scale_ref), custom_call_target="tpu_custom_call" | custom-call | flops 67108864 | bytes 1048576 | tf_op jit(solution)/shard_map/pallas_call | solution.py:336
  2.7 3.0 %collective-permute-start.4 = (bf16[4,128,128]{2,1,0:T(8,128)(2,1)S(1)}, bf16[4,128,128]{2,1,0:T(8,128)(2,1)S(1)}, u32[]{:S(2)}, u32[]{:S(2)}) collective-permute-start(bf16[4,128,128]{2,1,0:T(8,128)(2,1)S(1)} %get-tuple-element.48), channel_id=1, source_target_pairs={{0,4},{4,0},{8,12},{12,8},{16,20},{20,16},{24,28},{28,24},{1,5},{5... | collective-permute-start | bytes 393224 | tf_op jit(solution)/shard_map/ppermute | solution.py:293
  5.7 0.1 collective-permute-start
  5.8 4.1 %collective-permute-done.4.other_ref.near_ref = bf16[4,128,128]{2,1,0:T(8,128)(2,1)S(1)} collective-permute-done((bf16[4,128,128]{2,1,0:T(8,128)(2,1)S(1)}, bf16[4,128,128]{2,1,0:T(8,128)(2,1)S(1)}, u32[]{:S(2)}, u32[]{:S(2)}) %collective-permute-start.4) | collective-permute-done | bytes 131104 | tf_op jit(solution)/shard_map/ppermute | solution.py:293
  10.0 1.9 %collective-permute-start.5 = (bf16[4,128,128]{2,1,0:T(8,128)(2,1)S(1)}, bf16[4,128,128]{2,1,0:T(8,128)(2,1)S(1)}, u32[]{:S(2)}, u32[]{:S(2)}) collective-permute-start(bf16[4,128,128]{2,1,0:T(8,128)(2,1)S(1)} %shard_map.82.mine_ref), channel_id=1, source_target_pairs={{0,8},{4,12},{8,0},{12,4},{16,24},{20,28},{24,16},{28,20},{1,9},{5... | collective-permute-start | bytes 393224 | tf_op jit(solution)/shard_map/ppermute | solution.py:293
  11.9 0.0 collective-permute-done.other_ref.near_ref
  11.9 0.0 copy-start
  11.9 0.7 %collective-permute-start.1 = (bf16[264,128]{1,0:T(8,128)(2,1)S(1)}, bf16[264,128]{1,0:T(8,128)(2,1)S(1)}, u32[]{:S(2)}, u32[]{:S(2)}) collective-permute-start(bf16[264,128]{1,0:T(8,128)(2,1)S(1)} %shard_map.75.mine_ref), channel_id=1, source_target_pairs={{0,8},{4,12},{8,0},{12,4},{16,24},{20,28},{24,16},{28,20},{1,9},{5... | collective-permute-start | bytes 202760 | tf_op jit(solution)/shard_map/ppermute | solution.py:293
  12.6 3.7 %collective-permute-done.1.other_ref.refs_0_ = bf16[264,128]{1,0:T(8,128)(2,1)S(1)} collective-permute-done((bf16[264,128]{1,0:T(8,128)(2,1)S(1)}, bf16[264,128]{1,0:T(8,128)(2,1)S(1)}, u32[]{:S(2)}, u32[]{:S(2)}) %collective-permute-start.1) | collective-permute-done | bytes 67616 | tf_op jit(solution)/shard_map/ppermute | solution.py:293
  16.3 3.2 %collective-permute-start.2 = (bf16[264,128]{1,0:T(8,128)(2,1)S(1)}, bf16[264,128]{1,0:T(8,128)(2,1)S(1)}, u32[]{:S(2)}, u32[]{:S(2)}) collective-permute-start(bf16[264,128]{1,0:T(8,128)(2,1)S(1)} %shard_map.76), channel_id=1, source_target_pairs={{0,16},{4,20},{8,24},{12,28},{16,0},{20,4},{24,8},{28,12},{1,17},{... | collective-permute-start | bytes 202760 | tf_op jit(solution)/shard_map/ppermute | solution.py:293
  19.5 0.0 collective-permute-done.5.other_ref.refs_0_
  19.6 0.1 collective-permute-start.6
  19.6 3.8 %collective-permute-done.2.refs_1_ = bf16[264,128]{1,0:T(8,128)(2,1)S(1)} collective-permute-done((bf16[264,128]{1,0:T(8,128)(2,1)S(1)}, bf16[264,128]{1,0:T(8,128)(2,1)S(1)}, u32[]{:S(2)}, u32[]{:S(2)}) %collective-permute-start.2) | collective-permute-done | bytes 67616 | tf_op jit(solution)/shard_map/ppermute | solution.py:293
  23.4 0.1 shard_map.77
  23.5 1.6 %collective-permute-start.3 = (bf16[264,128]{1,0:T(8,128)(2,1)S(1)}, bf16[264,128]{1,0:T(8,128)(2,1)S(1)}, u32[]{:S(2)}, u32[]{:S(2)}) collective-permute-start(bf16[264,128]{1,0:T(8,128)(2,1)S(1)} %get-tuple-element.37), channel_id=1, source_target_pairs={{0,4},{4,0},{8,12},{12,8},{16,20},{20,16},{24,28},{28,24},{1,5},{5... | collective-permute-start | bytes 202760 | tf_op jit(solution)/shard_map/ppermute | solution.py:293
  25.0 0.0 copy-done
  25.0 2.0 %shard_map.74 = (f32[8,128,256]{2,1,0:T(8,128)S(1)}, f32[8,128,256]{2,1,0:T(8,128)S(1)}) custom-call(bf16[256,1024]{1,0:T(8,128)(2,1)S(1)} %copy-done, bf16[256,1024]{1,0:T(8,128)(2,1)S(1)} %get-tuple-element.30.k_ref, bf16[8,128,256]{2,1,0:T(8,128)(2,1)S(1)} %get-tuple-element.31.kt_ref), custom_call_target="tpu_custom_call" | custom-call | flops 67108864 | bytes 1048576 | tf_op jit(solution)/shard_map/pallas_call | solution.py:342
  27.0 0.0 collective-permute-done.6.refs_1_
  27.0 0.1 shard_map.84
  27.1 0.0 copy-start.3
  27.1 1.4 %collective-permute-start.7 = (bf16[4,128,128]{2,1,0:T(8,128)(2,1)S(1)}, bf16[4,128,128]{2,1,0:T(8,128)(2,1)S(1)}, u32[]{:S(2)}, u32[]{:S(2)}) collective-permute-start(bf16[4,128,128]{2,1,0:T(8,128)(2,1)S(1)} %get-tuple-element.50), channel_id=1, source_target_pairs={{0,4},{4,0},{8,12},{12,8},{16,20},{20,16},{24,28},{28,24},{1,5},{5... | collective-permute-start | bytes 393224 | tf_op jit(solution)/shard_map/ppermute | solution.py:293
  28.6 0.0 collective-permute-done.3.far_ref
  28.6 0.0 copy-done.3
  28.6 4.9 %shard_map.78 = (bf16[8,128,128]{2,1,0:T(8,128)(2,1)S(1)}, f32[8,128,128]{2,1,0:T(8,128)S(1)}, f32[8,256]{1,0:T(8,128)S(1)}, f32[8,128,256]{2,1,0:T(8,128)S(1)},...) custom-call(bf16[256,1024]{1,0:T(8,128)(2,1)S(1)} %get-tuple-element.30.k_ref, ...), custom_call_target="tpu_custom_call" | custom-call | flops 671088640 | bytes 1048576 | tf_op jit(solution)/shard_map/pallas_call | solution.py:380
  33.5 2.5 %shard_map.79.x_ref = bf16[256,1024]{1,0:T(8,128)(2,1)S(1)} custom-call(bf16[256,1024]{1,0:T(8,128)(2,1)S(1)} %get-tuple-element.30.k_ref, bf16[8,128,256]{2,1,0:T(8,128)(2,1)S(1)} %get-tuple-element.31.kt_ref, bf16[8,128,128]{2,1,0:T(8,128)(2,1)S(1)} %get-tuple-element.38.mat_ref, f32[8,128,128]{2,1,0:T(8,128)S(1)} %get-tuple-element.39.ridges, ...), custom_call_target="tpu_custom_call" | custom-call | flops 671088640 | bytes 1048576 | tf_op jit(solution)/shard_map/pallas_call | solution.py:392
  36.0 0.9 %shard_map.81.local_ref = f32[256,1024]{1,0:T(8,128)S(1)} custom-call(bf16[256,1024]{1,0:T(8,128)(2,1)S(1)} %shard_map.79.x_ref, bf16[256,1024]{1,0:T(8,128)(2,1)S(1)} %get-tuple-element.30.k_ref, bf16[256,1024]{1,0:T(8,128)(2,1)S(1)} %get-tuple-element.46.val_ref), custom_call_target="tpu_custom_call" | custom-call | flops 67108864 | bytes 1048576 | tf_op jit(solution)/shard_map/pallas_call | solution.py:401
  37.0 0.0 collective-permute-done.7.far_ref
  37.0 0.0 copy-start.1
  37.0 0.0 copy-start.2
  37.0 0.4 shard_map.85
  37.4 1.6 %collective-permute-start.10 = (bf16[64,1024]{1,0:T(8,128)(2,1)S(1)}, bf16[64,1024]{1,0:T(8,128)(2,1)S(1)}, u32[]{:S(2)}, u32[]{:S(2)}) collective-permute-start(bf16[64,1024]{1,0:T(8,128)(2,1)S(1)} %get-tuple-element.54), channel_id=1, source_target_pairs={{0,2},{1,3},{2,0},{3,1},{4,6},{5,7},{6,4},{7,5},{8,10},{9,11},{10,... | collective-permute-start | bytes 393224 | tf_op jit(solution)/shard_map/ppermute | solution.py:293
  38.9 0.0 collective-permute-start.8
  39.0 0.5 %collective-permute-start.9 = (bf16[64,1024]{1,0:T(8,128)(2,1)S(1)}, bf16[64,1024]{1,0:T(8,128)(2,1)S(1)}, u32[]{:S(2)}, u32[]{:S(2)}) collective-permute-start(bf16[64,1024]{1,0:T(8,128)(2,1)S(1)} %get-tuple-element.53), channel_id=1, source_target_pairs={{0,2},{1,3},{2,0},{3,1},{4,6},{5,7},{6,4},{7,5},{8,10},{9,11},{10,... | collective-permute-start | bytes 393224 | tf_op jit(solution)/shard_map/ppermute | solution.py:293
  39.5 3.3 %collective-permute-done.10 = bf16[64,1024]{1,0:T(8,128)(2,1)S(1)} collective-permute-done((bf16[64,1024]{1,0:T(8,128)(2,1)S(1)}, bf16[64,1024]{1,0:T(8,128)(2,1)S(1)}, u32[]{:S(2)}, u32[]{:S(2)}) %collective-permute-start.10) | collective-permute-done | bytes 131104 | tf_op jit(solution)/shard_map/ppermute | solution.py:293
  42.8 0.0 collective-permute-start.11
  42.8 0.0 copy-done.1
  42.8 0.0 copy-done.2
  42.8 0.1 shard_map.86.refs_4_
  43.0 0.0 collective-permute-done.8.refs_1_
  43.0 2.2 %collective-permute-done.9.refs_2_ = bf16[64,1024]{1,0:T(8,128)(2,1)S(1)} collective-permute-done((bf16[64,1024]{1,0:T(8,128)(2,1)S(1)}, bf16[64,1024]{1,0:T(8,128)(2,1)S(1)}, u32[]{:S(2)}, u32[]{:S(2)}) %collective-permute-start.9) | collective-permute-done | bytes 131104 | tf_op jit(solution)/shard_map/ppermute | solution.py:293
  45.2 0.0 collective-permute-done.11.refs_3_
  45.2 1.1 %shard_map.87 = bf16[64,4096]{1,0:T(8,128)(2,1)} custom-call(bf16[64,1024]{1,0:T(8,128)(2,1)S(1)} %get-tuple-element.51.refs_0_, bf16[64,1024]{1,0:T(8,128)(2,1)S(1)} %collective-permute-done.8.refs_1_, bf16[64,1024]{1,0:T(8,128)(2,1)S(1)} %collective-permute-done.9.refs_2_, bf16[64,1024]{1,0:T(8,128)(2,1)S(1)} %collective-permute-done.11.refs_3_, ...), custom_call_target="tpu_custom_call" | custom-call | flops 67108864 | bytes 1048576 | tf_op jit(solution)/shard_map/pallas_call | solution.py:420
  (4 shorter events, 0.1 us)
Async XLA Ops:
  2.7 7.3 %collective-permute-start.4 = (bf16[4,128,128]{2,1,0:T(8,128)(2,1)S(1)}, bf16[4,128,128]{2,1,0:T(8,128)(2,1)S(1)}, u32[]{:S(2)}, u32[]{:S(2)}) collective-permute-start(bf16[4,128,128]{2,1,0:T(8,128)(2,1)S(1)} %get-tuple-element.48), channel_id=1, source_target_pairs={{0,4},{4,0},{8,12},{12,8},{16,20},{20,16},{24,28},{28,24},{1,5},{5... | collective-permute-start | bytes 393224 | tf_op jit(solution)/shard_map/ppermute | solution.py:293
  5.7 6.2 %collective-permute-start = (bf16[264,128]{1,0:T(8,128)(2,1)S(1)}, bf16[264,128]{1,0:T(8,128)(2,1)S(1)}, u32[]{:S(2)}, u32[]{:S(2)}) collective-permute-start(bf16[264,128]{1,0:T(8,128)(2,1)S(1)} %get-tuple-element.35), channel_id=1, source_target_pairs={{0,4},{4,0},{8,12},{12,8},{16,20},{20,16},{24,28},{28,24},{1,5},{5... | collective-permute-start | bytes 202760 | tf_op jit(solution)/shard_map/ppermute | solution.py:293
  10.0 9.5 %collective-permute-start.5 = (bf16[4,128,128]{2,1,0:T(8,128)(2,1)S(1)}, bf16[4,128,128]{2,1,0:T(8,128)(2,1)S(1)}, u32[]{:S(2)}, u32[]{:S(2)}) collective-permute-start(bf16[4,128,128]{2,1,0:T(8,128)(2,1)S(1)} %shard_map.82.mine_ref), channel_id=1, source_target_pairs={{0,8},{4,12},{8,0},{12,4},{16,24},{20,28},{24,16},{28,20},{1,9},{5... | collective-permute-start | bytes 393224 | tf_op jit(solution)/shard_map/ppermute | solution.py:293
  11.9 13.1 %copy-start = (bf16[256,1024]{1,0:T(8,128)(2,1)S(1)}, bf16[256,1024]{1,0:T(8,128)(2,1)}, u32[]{:S(2)}) copy-start(bf16[256,1024]{1,0:T(8,128)(2,1)} %q_ref.1) | copy-start | bytes 1572868
  11.9 4.4 %collective-permute-start.1 = (bf16[264,128]{1,0:T(8,128)(2,1)S(1)}, bf16[264,128]{1,0:T(8,128)(2,1)S(1)}, u32[]{:S(2)}, u32[]{:S(2)}) collective-permute-start(bf16[264,128]{1,0:T(8,128)(2,1)S(1)} %shard_map.75.mine_ref), channel_id=1, source_target_pairs={{0,8},{4,12},{8,0},{12,4},{16,24},{20,28},{24,16},{28,20},{1,9},{5... | collective-permute-start | bytes 202760 | tf_op jit(solution)/shard_map/ppermute | solution.py:293
  16.3 7.1 %collective-permute-start.2 = (bf16[264,128]{1,0:T(8,128)(2,1)S(1)}, bf16[264,128]{1,0:T(8,128)(2,1)S(1)}, u32[]{:S(2)}, u32[]{:S(2)}) collective-permute-start(bf16[264,128]{1,0:T(8,128)(2,1)S(1)} %shard_map.76), channel_id=1, source_target_pairs={{0,16},{4,20},{8,24},{12,28},{16,0},{20,4},{24,8},{28,12},{1,17},{... | collective-permute-start | bytes 202760 | tf_op jit(solution)/shard_map/ppermute | solution.py:293
  19.6 7.4 %collective-permute-start.6 = (bf16[4,128,128]{2,1,0:T(8,128)(2,1)S(1)}, bf16[4,128,128]{2,1,0:T(8,128)(2,1)S(1)}, u32[]{:S(2)}, u32[]{:S(2)}) collective-permute-start(bf16[4,128,128]{2,1,0:T(8,128)(2,1)S(1)} %shard_map.83), channel_id=1, source_target_pairs={{0,16},{4,20},{8,24},{12,28},{16,0},{20,4},{24,8},{28,12},{1,17},{... | collective-permute-start | bytes 393224 | tf_op jit(solution)/shard_map/ppermute | solution.py:293
  23.5 5.1 %collective-permute-start.3 = (bf16[264,128]{1,0:T(8,128)(2,1)S(1)}, bf16[264,128]{1,0:T(8,128)(2,1)S(1)}, u32[]{:S(2)}, u32[]{:S(2)}) collective-permute-start(bf16[264,128]{1,0:T(8,128)(2,1)S(1)} %get-tuple-element.37), channel_id=1, source_target_pairs={{0,4},{4,0},{8,12},{12,8},{16,20},{20,16},{24,28},{28,24},{1,5},{5... | collective-permute-start | bytes 202760 | tf_op jit(solution)/shard_map/ppermute | solution.py:293
  27.1 1.5 %copy-start.3 = (f32[8,128]{1,0:T(8,128)S(1)}, f32[8,128]{1,0:T(8,128)}, u32[]{:S(2)}) copy-start(f32[8,128]{1,0:T(8,128)} %ridge_ref.1) | copy-start | bytes 12292
  27.1 9.8 %collective-permute-start.7 = (bf16[4,128,128]{2,1,0:T(8,128)(2,1)S(1)}, bf16[4,128,128]{2,1,0:T(8,128)(2,1)S(1)}, u32[]{:S(2)}, u32[]{:S(2)}) collective-permute-start(bf16[4,128,128]{2,1,0:T(8,128)(2,1)S(1)} %get-tuple-element.50), channel_id=1, source_target_pairs={{0,4},{4,0},{8,12},{12,8},{16,20},{20,16},{24,28},{28,24},{1,5},{5... | collective-permute-start | bytes 393224 | tf_op jit(solution)/shard_map/ppermute | solution.py:293
  37.0 5.8 %copy-start.1 = (bf16[64,4096]{1,0:T(8,128)(2,1)S(1)}, bf16[64,4096]{1,0:T(8,128)(2,1)}, u32[]{:S(2)}) copy-start(bf16[64,4096]{1,0:T(8,128)(2,1)} %logit_ref.1) | copy-start | bytes 1572868
  37.0 5.8 %copy-start.2 = (f32[4096]{0:T(1024)S(1)}, f32[4096]{0:T(1024)}, u32[]{:S(2)}) copy-start(f32[4096]{0:T(1024)} %param.12) | copy-start | bytes 49156
  37.4 5.4 %collective-permute-start.10 = (bf16[64,1024]{1,0:T(8,128)(2,1)S(1)}, bf16[64,1024]{1,0:T(8,128)(2,1)S(1)}, u32[]{:S(2)}, u32[]{:S(2)}) collective-permute-start(bf16[64,1024]{1,0:T(8,128)(2,1)S(1)} %get-tuple-element.54), channel_id=1, source_target_pairs={{0,2},{1,3},{2,0},{3,1},{4,6},{5,7},{6,4},{7,5},{8,10},{9,11},{10,... | collective-permute-start | bytes 393224 | tf_op jit(solution)/shard_map/ppermute | solution.py:293
  38.9 4.0 %collective-permute-start.8 = (bf16[64,1024]{1,0:T(8,128)(2,1)S(1)}, bf16[64,1024]{1,0:T(8,128)(2,1)S(1)}, u32[]{:S(2)}, u32[]{:S(2)}) collective-permute-start(bf16[64,1024]{1,0:T(8,128)(2,1)S(1)} %get-tuple-element.52), channel_id=1, source_target_pairs={{0,1},{1,0},{2,3},{3,2},{4,5},{5,4},{6,7},{7,6},{8,9},{9,8},{10,11... | collective-permute-start | bytes 393224 | tf_op jit(solution)/shard_map/ppermute | solution.py:293
  39.0 6.3 %collective-permute-start.9 = (bf16[64,1024]{1,0:T(8,128)(2,1)S(1)}, bf16[64,1024]{1,0:T(8,128)(2,1)S(1)}, u32[]{:S(2)}, u32[]{:S(2)}) collective-permute-start(bf16[64,1024]{1,0:T(8,128)(2,1)S(1)} %get-tuple-element.53), channel_id=1, source_target_pairs={{0,2},{1,3},{2,0},{3,1},{4,6},{5,7},{6,4},{7,5},{8,10},{9,11},{10,... | collective-permute-start | bytes 393224 | tf_op jit(solution)/shard_map/ppermute | solution.py:293
  42.8 2.4 %collective-permute-start.11 = (bf16[64,1024]{1,0:T(8,128)(2,1)S(1)}, bf16[64,1024]{1,0:T(8,128)(2,1)S(1)}, u32[]{:S(2)}, u32[]{:S(2)}) collective-permute-start(bf16[64,1024]{1,0:T(8,128)(2,1)S(1)} %collective-permute-done.10), channel_id=1, source_target_pairs={{0,1},{1,0},{2,3},{3,2},{4,5},{5,4},{6,7},{7,6},{8,9},{9,8},{10,11... | collective-permute-start | bytes 393224 | tf_op jit(solution)/shard_map/ppermute | solution.py:293
